TPU v7x, 32 devices: a whole 2x2x4 slice. The times are simulated.
32 devices in a mesh: seq: 8 (over z, x), rep: 4 (over y, core).
Axes of the slice: x: 2, y: 2, z: 4, core: 2. Of those that a mesh axis runs over, the one named last changes fastest.
Arguments:
- layer_in: bfloat16 [2, 16384, 768], P(None, ('seq', 'rep')), may hold values from -6 to 6
- qkv_weight: bfloat16 [768, 2304], replicated, may hold values from -0.21875 to 0.21875
- out_weight: bfloat16 [768, 768], replicated, may hold values from -0.21875 to 0.21875
- up_weight: bfloat16 [768, 3072], replicated, may hold values from -0.21875 to 0.21875
- down_weight: bfloat16 [3072, 768], replicated, may hold values from -0.109375 to 0.109375
- input_gain: float32 [768], replicated, may hold values from 0.5 to 1.5
- input_bias: float32 [768], replicated, may hold values from -3 to 3
- mixer_gain: float32 [768], replicated, may hold values from 0.5 to 1.5
- mixer_bias: float32 [768], replicated, may hold values from -3 to 3
- block_gain: float32 [768], replicated, may hold values from 0.5 to 1.5
- block_bias: float32 [768], replicated, may hold values from -3 to 3
- hidden_gain: float32 [3072], replicated, may hold values from 0.5 to 1.5
- hidden_bias: float32 [3072], replicated, may hold values from -3 to 3
- output_grad: bfloat16 [2, 16384, 768], P(None, ('seq', 'rep')), may hold values from -6 to 6
- seq_lengths: int32 [2, 4], replicated, may hold values from 1024 to 13312, as said below
Outputs:
- layer_out: bfloat16 [2, 16384, 768], P(None, ('seq', 'rep'))
- input_grad: bfloat16 [2, 16384, 768], P(None, ('seq', 'rep'))
- grad_qkv: float32 [768, 2304], P('seq')
- grad_proj: float32 [768, 768], P('seq')
- grad_up: float32 [768, 3072], P('seq')
- grad_down: float32 [3072, 768], P('seq')
- grad_norms: float32 [768, 6], P('seq')
- grad_hidden_norm: float32 [3072, 2], P('seq')
Inputs may be any that keep to these rules, and one draw needn't show every extreme that they name: `seq_lengths`: each row holds 4 positive multiples of 1024 that add up to 16384; the first row holds 3 sequences of 1024 and one of the largest length.
All inputs are finite; a program needn't handle non-finite values.
Results may differ from a plain program's by a relative error of at most 0.024.
Values may be sent and summed in bfloat16 or wider, within the bound.
A program may use at most 512 MiB of HBM per device.

v0:
```python
from functools import reduce
import math

import jax
import jax.numpy as jnp
from jax import lax
from jax.sharding import PartitionSpec as P

HEADS = 12
PATTERNS = 3


norm_eps = 1e-05
neg_large = -1e30
exact_mode = lax.Precision.HIGHEST


def as_sent(shard):

    def short(part):
        return part.astype(jnp.bfloat16) if part.dtype == jnp.float32 else part

    return jax.tree.map(short, shard)


def partner(block, axis, apart):
    count = lax.axis_size(axis)
    route = []
    for low in range(count):
        high = low | 1 << apart
        if high != low and high < count:
            route += [(low, high), (high, low)]
    return lax.ppermute(block, axis, route)


def layer_norm(values, norm_gain, norm_bias):
    centred = values - jnp.mean(values, axis=-1, keepdims=True)
    spread = jnp.mean(centred * centred, axis=-1, keepdims=True)
    return centred * lax.rsqrt(spread + norm_eps) * norm_gain + norm_bias


def hidden_norm(upward, norm_gain, norm_bias):
    return layer_norm(jax.nn.gelu(upward, approximate=False), norm_gain, norm_bias)


def contract_rows(left_side, right_side):
    return lax.dot_general(
        left_side, right_side, (((0,), (0,)), ((), ())), preferred_element_type=jnp.float32
    )


def contract_cols(left_side, right_side):
    return lax.dot_general(
        left_side, right_side, (((1,), (1,)), ((), ())), preferred_element_type=jnp.float32
    )


def class_table(dilation, slot_count, heads_dev, rep_index):
    category_list = jnp.arange(dilation, dtype=jnp.int32)[:, None, None]
    slot_ids = jnp.arange(slot_count, dtype=jnp.int32)[None, :, None]
    head_ids = jnp.arange(heads_dev, dtype=jnp.int32)[None, None, :]
    first_head = (category_list - heads_dev * rep_index) % dilation + dilation * slot_ids
    return (head_ids == first_head).astype(jnp.float32)


def doc_index(positions, bounds):
    return jnp.sum((positions[..., None] >= bounds).astype(jnp.int32), axis=-1)


def partner_swap_path(transfer_contents, team_size_total, team_position, transfer_holder):
    if team_size_total == 1:
        return transfer_contents
    xor_order = jnp.bitwise_xor(jnp.arange(team_size_total, dtype=jnp.int32), team_position)
    buffer = tuple(
        (jnp.take(member_portion, xor_order, axis=0) for member_portion in transfer_contents)
    )
    for exchange_bit_level in range(team_size_total.bit_length() - 1):
        stride = 2**exchange_bit_level
        reshaped_block = tuple(
            (
                member_portion.reshape(
                    (team_size_total // (2 * stride), 2, stride) + member_portion.shape[1:]
                )
                for member_portion in buffer
            )
        )
        incoming_tile = transfer_holder(
            tuple((member_portion[:, 1] for member_portion in reshaped_block)), exchange_bit_level
        )
        buffer = tuple(
            (
                jnp.stack([kept_half[:, 0], came_half], axis=1).reshape(full_part.shape)
                for kept_half, came_half, full_part in zip(reshaped_block, incoming_tile, buffer)
            )
        )
    return tuple((jnp.take(member_portion, xor_order, axis=0) for member_portion in buffer))


def owner_forward(owned, key_pos, key_doc, scale):
    slot_count, span, triple, head_dim = owned.shape
    block_rows = min(512, span)
    block_count = span // block_rows
    out_parts = []
    lse_parts = []
    for block_index in range(block_count):
        row_start = block_index * block_rows
        key_end = row_start + block_rows
        query_blk = owned[:, row_start:key_end, 0]
        key_rows = owned[:, :key_end, 1]
        value_rows = owned[:, :key_end, 2]
        pos_blk = key_pos[row_start:key_end]
        doc_blk = key_doc[row_start:key_end]
        scores = (
            jnp.einsum("sqd,skd->sqk", query_blk, key_rows, preferred_element_type=jnp.float32)
            * scale
        )
        allowed = (key_pos[None, :key_end] <= pos_blk[:, None]) & (
            key_doc[None, :key_end] == doc_blk[:, None]
        )
        scores = jnp.where(allowed[None], scores, neg_large)
        top_score = jnp.max(scores, axis=2, keepdims=True)
        log_total = top_score + jnp.log(jnp.sum(jnp.exp(scores - top_score), axis=2, keepdims=True))
        weights = jnp.exp(scores - log_total).astype(jnp.bfloat16)
        out_parts.append(
            jnp.einsum("sqk,skd->sqd", weights, value_rows, preferred_element_type=jnp.float32)
        )
        lse_parts.append(log_total[:, :, 0])
    return (jnp.concatenate(out_parts, axis=1), jnp.concatenate(lse_parts, axis=1))


def owner_backward(owned, key_pos, key_doc, scale, outputs, log_sums, grad_in, stat_in):
    slot_count, span, triple, head_dim = owned.shape
    block_rows = min(512, span)
    block_count = span // block_rows
    share = jnp.exp(log_sums - stat_in[:, :, 0])
    grad_low = (share[:, :, None] * grad_in).astype(jnp.bfloat16)
    lse_shift = share * (jnp.sum(grad_in * outputs, axis=2) - stat_in[:, :, 1])
    key_grad = jnp.zeros((slot_count, span, head_dim), jnp.float32)
    value_grad = jnp.zeros((slot_count, span, head_dim), jnp.float32)
    query_parts = []
    for block_index in range(block_count):
        row_start = block_index * block_rows
        key_end = row_start + block_rows
        query_blk = owned[:, row_start:key_end, 0]
        key_rows = owned[:, :key_end, 1]
        value_rows = owned[:, :key_end, 2]
        grad_blk = grad_low[:, row_start:key_end]
        lse_blk = log_sums[:, row_start:key_end]
        shift_blk = lse_shift[:, row_start:key_end]
        pos_blk = key_pos[row_start:key_end]
        doc_blk = key_doc[row_start:key_end]
        scores = (
            jnp.einsum("sqd,skd->sqk", query_blk, key_rows, preferred_element_type=jnp.float32)
            * scale
        )
        allowed = (key_pos[None, :key_end] <= pos_blk[:, None]) & (
            key_doc[None, :key_end] == doc_blk[:, None]
        )
        scores = jnp.where(allowed[None], scores, neg_large)
        probs = jnp.exp(scores - lse_blk[:, :, None])
        grad_probs = jnp.einsum(
            "sqd,skd->sqk", grad_blk, value_rows, preferred_element_type=jnp.float32
        )
        row_inner = jnp.sum(probs * grad_probs, axis=2, keepdims=True)
        grad_scores = (probs * (grad_probs - row_inner + shift_blk[:, :, None])).astype(
            jnp.bfloat16
        )
        query_parts.append(
            jnp.einsum("sqk,skd->sqd", grad_scores, key_rows, preferred_element_type=jnp.float32)
            * scale
        )
        key_grad = key_grad.at[:, :key_end].add(
            jnp.einsum("sqk,sqd->skd", grad_scores, query_blk, preferred_element_type=jnp.float32)
            * scale
        )
        value_grad = value_grad.at[:, :key_end].add(
            jnp.einsum(
                "sqk,sqd->skd",
                probs.astype(jnp.bfloat16),
                grad_blk,
                preferred_element_type=jnp.float32,
            )
        )
    query_grad = jnp.concatenate(query_parts, axis=1)
    return jnp.stack([query_grad, key_grad, value_grad], axis=2)


def on_device(
    layer_in,
    qkv_weight,
    out_weight,
    up_weight,
    down_weight,
    input_gain,
    input_bias,
    mixer_gain,
    mixer_bias,
    block_gain,
    block_bias,
    hidden_gain,
    hidden_bias,
    output_grad,
    seq_lengths,
):
    micro_count, tok_dev, model_width = layer_in.shape
    rep_count = lax.axis_size("rep")
    rep_index = lax.axis_index("rep")
    seq_index = lax.axis_index("seq")
    heads_dev = HEADS // rep_count
    head_dim = model_width // HEADS
    span = tok_dev * rep_count
    scale = 1.0 / math.sqrt(head_dim)
    level_count = PATTERNS

    def pieces_swap(transfer_contents, exchange_bit_level):
        return jax.tree.map(
            lambda part, own: part.astype(own.dtype),
            partner(as_sent(transfer_contents), "seq", exchange_bit_level),
            transfer_contents,
        )

    def results_swap(transfer_contents, exchange_bit_level):
        return jax.tree.map(
            lambda part, own: part.astype(own.dtype),
            partner(as_sent(transfer_contents), "seq", exchange_bit_level),
            transfer_contents,
        )

    def grads_swap(transfer_contents, exchange_bit_level):
        return jax.tree.map(
            lambda part, own: part.astype(own.dtype),
            partner(as_sent(transfer_contents), "seq", exchange_bit_level),
            transfer_contents,
        )

    def partials_swap(transfer_contents, exchange_bit_level):
        return jax.tree.map(
            lambda part, own: part.astype(own.dtype),
            partner(as_sent(transfer_contents), "seq", exchange_bit_level),
            transfer_contents,
        )

    movers = (pieces_swap, results_swap, grads_swap, partials_swap)

    def route_all(payloads, mover_slot):
        return [
            partner_swap_path(
                transfer_contents, 2**pattern, seq_index % 2**pattern, movers[mover_slot]
            )
            for pattern, transfer_contents in enumerate(payloads)
        ]

    grad_qkv = jnp.zeros(qkv_weight.shape, jnp.float32)
    grad_proj = jnp.zeros(out_weight.shape, jnp.float32)
    grad_up = jnp.zeros(up_weight.shape, jnp.float32)
    grad_down = jnp.zeros(down_weight.shape, jnp.float32)
    model_norms = [jnp.zeros((model_width,), jnp.float32) for column_index in range(6)]
    inner_norms = [jnp.zeros(hidden_gain.shape, jnp.float32) for column_index in range(2)]
    outputs_all = []
    input_grads = []
    for micro_index in range(micro_count):
        bounds = jnp.cumsum(seq_lengths[micro_index])
        residual = layer_in[micro_index].astype(jnp.float32)
        normed_in, input_back = jax.vjp(layer_norm, residual, input_gain, input_bias)
        normed_low = normed_in.astype(jnp.bfloat16)
        qkv_low = jnp.dot(normed_low, qkv_weight, preferred_element_type=jnp.float32).astype(
            jnp.bfloat16
        )
        head_side = lax.all_to_all(
            qkv_low.reshape(tok_dev, 3, rep_count, heads_dev * head_dim),
            "rep",
            split_axis=2,
            concat_axis=0,
            tiled=True,
        )
        head_side = head_side.reshape(span, 3, heads_dev, head_dim)
        tables = []
        piece_list = []
        for pattern in range(level_count):
            dilation = 2**pattern
            slot_count = (heads_dev + dilation - 1) // dilation
            per_class = span // dilation
            table = class_table(dilation, slot_count, heads_dev, rep_index)
            tables.append(table)
            reshaped_block = head_side.reshape(per_class, dilation, 3, heads_dev, head_dim)
            pieces = jnp.einsum(
                "cue,acwed->cuawd",
                table.astype(jnp.bfloat16),
                reshaped_block,
                preferred_element_type=jnp.float32,
            ).astype(jnp.bfloat16)
            piece_list.append((pieces,))
        arrived_list = route_all(piece_list, 0)
        records = []
        back_list = []
        for pattern in range(level_count):
            dilation = 2**pattern
            table = tables[pattern]
            slot_count = table.shape[1]
            per_class = span // dilation
            team_position = seq_index % dilation
            owned = (
                arrived_list[pattern][0]
                .transpose(1, 0, 2, 3, 4)
                .reshape(slot_count, span, 3, head_dim)
            )
            local_row = jnp.arange(span, dtype=jnp.int32)
            key_pos = (
                (seq_index - team_position) * span
                + local_row // per_class * span
                + local_row % per_class * dilation
                + team_position
            )
            key_doc = doc_index(key_pos, bounds)
            out_own, lse_own = owner_forward(owned, key_pos, key_doc, scale)
            back_out = out_own.reshape(slot_count, dilation, per_class, head_dim).transpose(
                1, 0, 2, 3
            )
            back_lse = lse_own.reshape(slot_count, dilation, per_class).transpose(1, 0, 2)
            back_list.append((back_out, back_lse))
            records.append((table, owned, key_pos, key_doc, out_own, lse_own))
        got_list = route_all(back_list, 1)
        pattern_outs = []
        pattern_lses = []
        for pattern in range(level_count):
            dilation = 2**pattern
            table = tables[pattern]
            per_class = span // dilation
            got_out, got_lse = got_list[pattern]
            pattern_outs.append(
                jnp.einsum("cue,cuad->aced", table, got_out, precision=exact_mode).reshape(
                    span, heads_dev, head_dim
                )
            )
            pattern_lse = jnp.einsum("cue,cua->ace", table, got_lse, precision=exact_mode).reshape(
                span, heads_dev
            )
            chosen = (
                jnp.broadcast_to(
                    jnp.sum(table, axis=1)[None], (per_class, dilation, heads_dev)
                ).reshape(span, heads_dev)
                > 0.5
            )
            pattern_lses.append(jnp.where(chosen, pattern_lse, neg_large))
        top_lse = reduce(jnp.maximum, pattern_lses)
        mix_total = top_lse + jnp.log(
            sum((jnp.exp(item_lse - top_lse) for item_lse in pattern_lses))
        )
        mixed = sum(
            (
                jnp.exp(item_lse - mix_total)[:, :, None] * item_out
                for item_lse, item_out in zip(pattern_lses, pattern_outs)
            )
        )
        attended = lax.all_to_all(
            mixed.astype(jnp.bfloat16).reshape(span, 1, heads_dev * head_dim),
            "rep",
            split_axis=0,
            concat_axis=1,
            tiled=True,
        )
        attended = attended.reshape(tok_dev, model_width).astype(jnp.float32)
        mixer_normed, mixer_back = jax.vjp(layer_norm, attended, mixer_gain, mixer_bias)
        mixer_low = mixer_normed.astype(jnp.bfloat16)
        after_mixer = residual + jnp.dot(mixer_low, out_weight, preferred_element_type=jnp.float32)
        block_normed, block_back = jax.vjp(layer_norm, after_mixer, block_gain, block_bias)
        block_low = block_normed.astype(jnp.bfloat16)
        upward = jnp.dot(block_low, up_weight, preferred_element_type=jnp.float32)
        hidden, hidden_back = jax.vjp(hidden_norm, upward, hidden_gain, hidden_bias)
        hidden_low = hidden.astype(jnp.bfloat16)
        result = after_mixer + jnp.dot(hidden_low, down_weight, preferred_element_type=jnp.float32)
        outputs_all.append(result.astype(jnp.bfloat16))
        cot_low = output_grad[micro_index]
        grad_down = grad_down + contract_rows(hidden_low, cot_low)
        hidden_grad = contract_cols(cot_low, down_weight)
        upward_grad, gain_hidden, bias_hidden = hidden_back(hidden_grad)
        upward_low = upward_grad.astype(jnp.bfloat16)
        grad_up = grad_up + contract_rows(block_low, upward_low)
        block_grad = contract_cols(upward_low, up_weight)
        middle_grad, gain_block, bias_block = block_back(block_grad)
        branch_grad = cot_low.astype(jnp.float32) + middle_grad
        branch_low = branch_grad.astype(jnp.bfloat16)
        grad_proj = grad_proj + contract_rows(mixer_low, branch_low)
        mixer_grad = contract_cols(branch_low, out_weight)
        attended_grad, gain_mixer, bias_mixer = mixer_back(mixer_grad)
        head_grad = lax.all_to_all(
            attended_grad.astype(jnp.bfloat16).reshape(tok_dev, rep_count, heads_dev * head_dim),
            "rep",
            split_axis=1,
            concat_axis=0,
            tiled=True,
        )
        head_grad = head_grad.reshape(span, heads_dev, head_dim).astype(jnp.float32)
        inner = jnp.sum(head_grad * mixed, axis=2)
        stats = jnp.stack([mix_total, inner], axis=2)
        grad_list = []
        for pattern in range(level_count):
            dilation = 2**pattern
            table = tables[pattern]
            per_class = span // dilation
            grad_pieces = jnp.einsum(
                "cue,aced->cuad",
                table,
                head_grad.reshape(per_class, dilation, heads_dev, head_dim),
                precision=exact_mode,
            )
            stat_pieces = jnp.einsum(
                "cue,acef->cuaf",
                table,
                stats.reshape(per_class, dilation, heads_dev, 2),
                precision=exact_mode,
            )
            grad_list.append((grad_pieces, stat_pieces))
        got_grads = route_all(grad_list, 2)
        partial_list = []
        for pattern in range(level_count):
            table, owned, key_pos, key_doc, out_own, lse_own = records[pattern]
            dilation = 2**pattern
            slot_count = table.shape[1]
            per_class = span // dilation
            got_grad, got_stat = got_grads[pattern]
            grad_in = got_grad.transpose(1, 0, 2, 3).reshape(slot_count, span, head_dim)
            stat_in = got_stat.transpose(1, 0, 2, 3).reshape(slot_count, span, 2)
            own_grads = owner_backward(
                owned, key_pos, key_doc, scale, out_own, lse_own, grad_in, stat_in
            )
            partial_list.append(
                (
                    own_grads.reshape(slot_count, dilation, per_class, 3, head_dim).transpose(
                        1, 0, 2, 3, 4
                    ),
                )
            )
        got_partials = route_all(partial_list, 3)
        qkv_grad = jnp.zeros((span, 3, heads_dev, head_dim), jnp.float32)
        for pattern in range(level_count):
            qkv_grad = qkv_grad + jnp.einsum(
                "cue,cuawd->acwed", tables[pattern], got_partials[pattern][0], precision=exact_mode
            ).reshape(span, 3, heads_dev, head_dim)
        token_grad = lax.all_to_all(
            qkv_grad.astype(jnp.bfloat16).reshape(span, 3, 1, heads_dev * head_dim),
            "rep",
            split_axis=0,
            concat_axis=2,
            tiled=True,
        )
        token_grad = token_grad.reshape(tok_dev, 3 * model_width)
        grad_qkv = grad_qkv + contract_rows(normed_low, token_grad)
        normed_grad = contract_cols(token_grad, qkv_weight)
        input_part, gain_input, bias_input = input_back(normed_grad)
        input_grads.append((branch_grad + input_part).astype(jnp.bfloat16))
        model_terms = (gain_input, bias_input, gain_mixer, bias_mixer, gain_block, bias_block)
        model_norms = [running + term_now for running, term_now in zip(model_norms, model_terms)]
        inner_norms = [inner_norms[0] + gain_hidden, inner_norms[1] + bias_hidden]
    norm_rows = jnp.stack(model_norms, axis=1)
    hidden_rows = jnp.stack(inner_norms, axis=1)
    shards = (
        lax.psum_scatter(grad_qkv, "seq", scatter_dimension=0, tiled=True),
        lax.psum_scatter(grad_proj, "seq", scatter_dimension=0, tiled=True),
        lax.psum_scatter(grad_up, "seq", scatter_dimension=0, tiled=True),
        lax.psum_scatter(grad_down, "seq", scatter_dimension=0, tiled=True),
        lax.psum_scatter(norm_rows, "seq", scatter_dimension=0, tiled=True),
        lax.psum_scatter(hidden_rows, "seq", scatter_dimension=0, tiled=True),
    )
    totals = (
        lax.psum(shards[0].astype(jnp.bfloat16), "rep").astype(jnp.float32),
        lax.psum(shards[1].astype(jnp.bfloat16), "rep").astype(jnp.float32),
        lax.psum(shards[2].astype(jnp.bfloat16), "rep").astype(jnp.float32),
        lax.psum(shards[3].astype(jnp.bfloat16), "rep").astype(jnp.float32),
        lax.psum(shards[4].astype(jnp.bfloat16), "rep").astype(jnp.float32),
        lax.psum(shards[5].astype(jnp.bfloat16), "rep").astype(jnp.float32),
    )
    return (
        jnp.stack(outputs_all),
        jnp.stack(input_grads),
        totals[0],
        totals[1],
        totals[2],
        totals[3],
        totals[4],
        totals[5],
    )


def solution(mesh):
    placed = (
        P(None, ("seq", "rep"), None),
        P(),
        P(),
        P(),
        P(),
        P(),
        P(),
        P(),
        P(),
        P(),
        P(),
        P(),
        P(),
        P(None, ("seq", "rep"), None),
        P(),
    )
    return jax.shard_map(
        on_device,
        mesh=mesh,
        in_specs=placed,
        out_specs=(
            P(None, ("seq", "rep"), None),
            P(None, ("seq", "rep"), None),
            P("seq", None),
            P("seq", None),
            P("seq", None),
            P("seq", None),
            P("seq", None),
            P("seq", None),
        ),
        check_vma=False,
    )
```

profile of v0, /device:TPU:0, one launch (start us, length us, event | category | flops | bytes accessed | tf_op | source)
XLA Modules:
  0.0 3065.3 jit_solution(10553005436198177088)
XLA Ops:
  219.3 40.3 %multiply_reduce_fusion.1 = (bf16[4,512,3,64]{3,0,1,2:T(4,128)(2,1)}, bf16[4,512,3,64]{3,0,1,2:T(4,128)(2,1)}) fusion(f32[4,3]{1,0:T(4,128)S(1)} %copy-done.425, bf16[512,4,3,3,64]{4,3,1,0,2:T(4,128)(2,1)} %reshape_reshape.51, bf16[512,4,3,3,64]{4,3,1,0,2:T(4,128)(2,1)} %reshape_reshape.56), kind=kLoop, calls=%fused_computation.65 | loop fusion | flops 6291456 | bytes 6291504
  951.1 20.5 fusion.1301
  971.6 18.3 fusion.1299
  1015.3 18.5 add_convert_fusion
  1356.8 17.0 fusion.619
  1390.2 16.9 fusion.613
  1407.1 20.9 fusion.654
  1428.1 22.0 fusion.373
  1450.0 21.0 fusion.657
  1471.0 21.8 fusion.367
  1492.8 26.5 fusion.666
  1519.4 25.8 fusion.384
  1557.7 26.3 fusion.669
  1584.0 25.7 fusion.393
  1892.3 17.9 fusion.706
  1910.2 19.5 fusion.429
  2116.1 18.2 fusion.709
  2134.3 19.5 fusion.426
  2424.1 37.0 %all-to-all-done.5 = bf16[2048,3,1,192]{3,1,2,0:T(4,128)(2,1)} async-done(((bf16[2048,3,1,192]{3,1,2,0:T(4,128)(2,1)}), bf16[2048,3,1,192]{3,1,2,0:T(4,128)(2,1)}, u32[]{:S(2)}, u32[]{:S(2)}) %all-to-all-start.5) | async-done | bytes 2359328 | tf_op jit(solution)/shard_map/all_to_all | solution.py:440
  2537.2 69.6 %reduce-scatter.11.cloned.1.call-done = f32[96,2304]{1,0:T(8,128)} async-done(((f32[768,2304]{1,0:T(8,128)}), f32[96,2304]{1,0:T(8,128)}) %reduce-scatter.11.cloned.1.call-update) | async-done | bytes 884752 | tf_op jit(solution)/shard_map/reduce_scatter | solution.py:458
  2608.8 164.0 %reduce-scatter.15.cloned.1.call-done = f32[96,3072]{1,0:T(8,128)} async-done(((f32[768,3072]{1,0:T(8,128)}), f32[96,3072]{1,0:T(8,128)}) %reduce-scatter.15.cloned.1.call-update) | async-done | bytes 1179664 | tf_op jit(solution)/shard_map/reduce_scatter | solution.py:460
  2774.9 163.9 %reduce-scatter.17.cloned.1.call-done = f32[384,768]{1,0:T(8,128)} async-done(((f32[3072,768]{1,0:T(8,128)}), f32[384,768]{1,0:T(8,128)}) %reduce-scatter.17.cloned.1.call-update) | async-done | bytes 1179664 | tf_op jit(solution)/shard_map/reduce_scatter | solution.py:461
  2947.5 54.9 %reduce-scatter.19.cloned.1.call-done = f32[96,6]{1,0:T(8,128)} async-done(((f32[768,6]{1,0:T(8,128)}), f32[96,6]{1,0:T(8,128)}) %reduce-scatter.19.cloned.1.call-update) | async-done | bytes 2320
  3010.2 41.1 %all-reduce.16.cloned.1.call-done = (bf16[96,2304]{1,0:T(8,128)(2,1)}, bf16[96,768]{1,0:T(8,128)(2,1)}, bf16[96,3072]{1,0:T(8,128)(2,1)}, bf16[384,768]{1,0:T(8,128)(2,1)}) async-done(((bf16[96,2304]{1,0:T(8,128)(2,1)}, bf16[96,768]{1,0:T(8,128)(2,1)}, bf16[96,3072]{1,0:T(8,128)(2,1)}, bf16[384,768]{1,0:T(8,128)(2,1)}), (bf16[96,2304]{1,0:T(8,128)(2,1)}, bf16[96,768]{1,0:T(8,128)(2,1)}, ...) | async-done | bytes 1769488 | tf_op jit(solution)/shard_map/psum | solution.py:466
  (1980 shorter events, 2117.5 us)
Async XLA Ops:
  275.4 146.5 %collective-permute-start.2 = (bf16[2,1,1,512,3,64]{3,5,4,0,2,1:T(8,128)(2,1)}, bf16[2,1,1,512,3,64]{3,5,4,0,2,1:T(8,128)(2,1)}, u32[]{:S(2)}, u32[]{:S(2)}) collective-permute-start(bf16[2,1,1,512,3,64]{3,5,4,0,2,1:T(8,128)(2,1)} %get-tuple-element.821), channel_id=1, source_target_pairs={{0,4},{4,0},{8,12},{12,8},{16,20},{20,16},{24,28},{28,24},{1,5},{5... | collective-permute-start | bytes 1179656 | tf_op jit(solution)/shard_map/ppermute | solution.py:33
  278.3 147.8 %collective-permute-start.11 = (bf16[2,1,1,512,3,64]{3,5,4,0,2,1:T(8,128)(2,1)}, bf16[2,1,1,512,3,64]{3,5,4,0,2,1:T(8,128)(2,1)}, u32[]{:S(2)}, u32[]{:S(2)}) collective-permute-start(bf16[2,1,1,512,3,64]{3,5,4,0,2,1:T(8,128)(2,1)} %get-tuple-element.825), channel_id=1, source_target_pairs={{0,4},{4,0},{8,12},{12,8},{16,20},{20,16},{24,28},{28,24},{1,5},{5... | collective-permute-start | bytes 1179656 | tf_op jit(solution)/shard_map/ppermute | solution.py:33
  317.4 110.8 %collective-permute-start = (bf16[1,1,2,1024,3,64]{3,2,5,4,1,0:T(2,128)(2,1)}, bf16[1,1,2,1024,3,64]{3,2,5,4,1,0:T(2,128)(2,1)}, u32[]{:S(2)}, u32[]{:S(2)}) collective-permute-start(bf16[1,1,2,1024,3,64]{3,2,5,4,1,0:T(2,128)(2,1)} %slice_bitcast_fusion.10), channel_id=1, source_target_pairs={{0,4},{4,0},{8,12},{12,8},{16,20},{20,16},{24,28},{28,24},{1,5},{5... | collective-permute-start | bytes 2359304 | tf_op jit(solution)/shard_map/ppermute | solution.py:33
  319.4 119.6 %collective-permute-start.9 = (bf16[1,1,2,1024,3,64]{3,2,5,4,1,0:T(2,128)(2,1)}, bf16[1,1,2,1024,3,64]{3,2,5,4,1,0:T(2,128)(2,1)}, u32[]{:S(2)}, u32[]{:S(2)}) collective-permute-start(bf16[1,1,2,1024,3,64]{3,2,5,4,1,0:T(2,128)(2,1)} %slice_bitcast_fusion.7), channel_id=1, source_target_pairs={{0,4},{4,0},{8,12},{12,8},{16,20},{20,16},{24,28},{28,24},{1,5},{5... | collective-permute-start | bytes 2359304 | tf_op jit(solution)/shard_map/ppermute | solution.py:33
  424.1 64.0 %collective-permute-start.3 = (bf16[1,2,1,512,3,64]{3,5,4,1,2,0:T(8,128)(2,1)}, bf16[1,2,1,512,3,64]{3,5,4,1,2,0:T(8,128)(2,1)}, u32[]{:S(2)}, u32[]{:S(2)}) collective-permute-start(bf16[1,2,1,512,3,64]{3,5,4,1,2,0:T(8,128)(2,1)} %get-tuple-element.819), channel_id=1, source_target_pairs={{0,8},{8,0},{4,12},{12,4},{16,24},{24,16},{20,28},{28,20},{1,9},{9... | collective-permute-start | bytes 1179656 | tf_op jit(solution)/shard_map/ppermute | solution.py:33
  428.1 97.8 %collective-permute-start.12 = (bf16[1,2,1,512,3,64]{3,5,4,1,2,0:T(8,128)(2,1)}, bf16[1,2,1,512,3,64]{3,5,4,1,2,0:T(8,128)(2,1)}, u32[]{:S(2)}, u32[]{:S(2)}) collective-permute-start(bf16[1,2,1,512,3,64]{3,5,4,1,2,0:T(8,128)(2,1)} %get-tuple-element.823), channel_id=1, source_target_pairs={{0,8},{8,0},{4,12},{12,4},{16,24},{24,16},{20,28},{28,20},{1,9},{9... | collective-permute-start | bytes 1179656 | tf_op jit(solution)/shard_map/ppermute | solution.py:33
  578.6 92.4 %collective-permute-start.7 = (bf16[2,1,1,512,64]{3,4,2,1,0:T(8,128)(2,1)}, bf16[2,1,1,512,64]{3,4,2,1,0:T(8,128)(2,1)}, u32[]{:S(2)}, u32[]{:S(2)}) collective-permute-start(bf16[2,1,1,512,64]{3,4,2,1,0:T(8,128)(2,1)} %fusion.934), channel_id=1, source_target_pairs={{0,4},{4,0},{8,12},{12,8},{16,20},{20,16},{24,28},{28,24},{1,5},{5... | collective-permute-start | bytes 393224 | tf_op jit(solution)/shard_map/ppermute | solution.py:33
  578.7 87.6 %collective-permute-start.16 = (bf16[2,1,1,512,64]{3,4,2,1,0:T(8,128)(2,1)}, bf16[2,1,1,512,64]{3,4,2,1,0:T(8,128)(2,1)}, u32[]{:S(2)}, u32[]{:S(2)}) collective-permute-start(bf16[2,1,1,512,64]{3,4,2,1,0:T(8,128)(2,1)} %fusion.936), channel_id=1, source_target_pairs={{0,4},{4,0},{8,12},{12,8},{16,20},{20,16},{24,28},{28,24},{1,5},{5... | collective-permute-start | bytes 393224 | tf_op jit(solution)/shard_map/ppermute | solution.py:33
  806.6 87.7 %all-to-all-start.3 = ((bf16[4,2,49152]{2,1,0:T(2,128)(2,1)}), bf16[4,2,49152]{2,1,0:T(2,128)(2,1)}, u32[]{:S(2)}, u32[]{:S(2)}) async-start(bf16[4,2,49152]{2,1,0:T(2,128)(2,1)} %reshape.7184), calls=%async_computation.3 | async-start | bytes 1572864 | tf_op jit(solution)/shard_map/all_to_all | solution.py:355
  1064.4 1454.9 %reduce-scatter.21.cloned.1.call-start = ((), (), s32[]{:S(2)}) async-start(), calls=%async_computation.19 | async-start | bytes 1769472
  1080.5 1455.1 %reduce-scatter.13.cloned.1.call-start = ((), (), s32[]{:S(2)}) async-start(), calls=%async_computation.15 | async-start | bytes 2654208 | tf_op jit(solution)/shard_map/reduce_scatter | solution.py:459
  1257.5 388.5 %collective-permute-start.30 = (bf16[2,1,1,512,2]{3,4,0,2,1:T(2,128)(2,1)}, bf16[2,1,1,512,2]{3,4,0,2,1:T(2,128)(2,1)}, u32[]{:S(2)}, u32[]{:S(2)}) collective-permute-start(bf16[2,1,1,512,2]{3,4,0,2,1:T(2,128)(2,1)} %fusion.1050), channel_id=1, source_target_pairs={{0,4},{4,0},{8,12},{12,8},{16,20},{20,16},{24,28},{28,24},{1,5},{5... | collective-permute-start | bytes 12296 | tf_op jit(solution)/shard_map/ppermute | solution.py:33
  1646.0 75.3 %collective-permute-start.19 = (bf16[1,1,2,1024,64]{3,2,4,1,0:T(2,128)(2,1)}, bf16[1,1,2,1024,64]{3,2,4,1,0:T(2,128)(2,1)}, u32[]{:S(2)}, u32[]{:S(2)}) collective-permute-start(bf16[1,1,2,1024,64]{3,2,4,1,0:T(2,128)(2,1)} %fusion.870), channel_id=1, source_target_pairs={{0,4},{4,0},{8,12},{12,8},{16,20},{20,16},{24,28},{28,24},{1,5},{5... | collective-permute-start | bytes 786440 | tf_op jit(solution)/shard_map/ppermute | solution.py:33
  2060.0 119.9 %collective-permute-start.34 = (bf16[2,1,1,512,3,64]{3,5,4,2,1,0:T(8,128)(2,1)}, bf16[2,1,1,512,3,64]{3,5,4,2,1,0:T(8,128)(2,1)}, u32[]{:S(2)}, u32[]{:S(2)}) collective-permute-start(bf16[2,1,1,512,3,64]{3,5,4,2,1,0:T(8,128)(2,1)} %fusion.838), channel_id=1, source_target_pairs={{0,4},{4,0},{8,12},{12,8},{16,20},{20,16},{24,28},{28,24},{1,5},{5... | collective-permute-start | bytes 1179656 | tf_op jit(solution)/shard_map/ppermute | solution.py:33
  2060.5 115.2 %collective-permute-start.25 = (bf16[2,1,1,512,3,64]{3,5,4,2,1,0:T(8,128)(2,1)}, bf16[2,1,1,512,3,64]{3,5,4,2,1,0:T(8,128)(2,1)}, u32[]{:S(2)}, u32[]{:S(2)}) collective-permute-start(bf16[2,1,1,512,3,64]{3,5,4,2,1,0:T(8,128)(2,1)} %fusion.836), channel_id=1, source_target_pairs={{0,4},{4,0},{8,12},{12,8},{16,20},{20,16},{24,28},{28,24},{1,5},{5... | collective-permute-start | bytes 1179656 | tf_op jit(solution)/shard_map/ppermute | solution.py:33
  2115.6 68.0 %collective-permute-start.29 = (bf16[1,1,2,1024,3,64]{3,5,4,2,1,0:T(8,128)(2,1)}, bf16[1,1,2,1024,3,64]{3,5,4,2,1,0:T(8,128)(2,1)}, u32[]{:S(2)}, u32[]{:S(2)}) collective-permute-start(bf16[1,1,2,1024,3,64]{3,5,4,2,1,0:T(8,128)(2,1)} %fusion.751), channel_id=1, source_target_pairs={{0,4},{4,0},{8,12},{12,8},{16,20},{20,16},{24,28},{28,24},{1,5},{5... | collective-permute-start | bytes 2359304 | tf_op jit(solution)/shard_map/ppermute | solution.py:33
  2182.8 65.5 %collective-permute-start.35 = (bf16[1,2,1,512,3,64]{3,5,4,1,2,0:T(8,128)(2,1)}, bf16[1,2,1,512,3,64]{3,5,4,1,2,0:T(8,128)(2,1)}, u32[]{:S(2)}, u32[]{:S(2)}) collective-permute-start(bf16[1,2,1,512,3,64]{3,5,4,1,2,0:T(8,128)(2,1)} %fusion.839), channel_id=1, source_target_pairs={{0,8},{8,0},{4,12},{12,4},{16,24},{24,16},{20,28},{28,20},{1,9},{9... | collective-permute-start | bytes 1179656 | tf_op jit(solution)/shard_map/ppermute | solution.py:33
  2197.2 143.6 %collective-permute-start.20 = (bf16[1,1,2,1024,3,64]{3,5,4,2,1,0:T(8,128)(2,1)}, bf16[1,1,2,1024,3,64]{3,5,4,2,1,0:T(8,128)(2,1)}, u32[]{:S(2)}, u32[]{:S(2)}) collective-permute-start(bf16[1,1,2,1024,3,64]{3,5,4,2,1,0:T(8,128)(2,1)} %fusion.750), channel_id=1, source_target_pairs={{0,4},{4,0},{8,12},{12,8},{16,20},{20,16},{24,28},{28,24},{1,5},{5... | collective-permute-start | bytes 2359304 | tf_op jit(solution)/shard_map/ppermute | solution.py:33
  2315.0 93.0 %all-to-all-start.7 = ((bf16[2048,3,1,192]{3,1,2,0:T(4,128)(2,1)}), bf16[2048,3,1,192]{3,1,2,0:T(4,128)(2,1)}, u32[]{:S(2)}, u32[]{:S(2)}) async-start(bf16[2048,3,1,192]{3,1,2,0:T(4,128)(2,1)} %copy.2763), calls=%async_computation.7 | async-start | bytes 8388608 | tf_op jit(solution)/shard_map/all_to_all | solution.py:440
  2412.9 193.9 %reduce-scatter.11.cloned.1.call-start = ((), (), s32[]{:S(2)}) async-start(), calls=%async_computation.14 | async-start | bytes 7962624 | tf_op jit(solution)/shard_map/reduce_scatter | solution.py:458
  2478.7 294.0 %reduce-scatter.15.cloned.1.call-start = ((), (), s32[]{:S(2)}) async-start(), calls=%async_computation.16 | async-start | bytes 10616832 | tf_op jit(solution)/shard_map/reduce_scatter | solution.py:460
  2490.7 448.1 %reduce-scatter.17.cloned.1.call-start = ((), (), s32[]{:S(2)}) async-start(), calls=%async_computation.17 | async-start | bytes 10616832 | tf_op jit(solution)/shard_map/reduce_scatter | solution.py:461
  2501.2 501.3 %reduce-scatter.19.cloned.1.call-start = ((), (), s32[]{:S(2)}) async-start(), calls=%async_computation.18 | async-start | bytes 442368
  2534.3 517.0 %all-reduce.16.cloned.1.call-start = ((), (), s32[]{:S(2)}) async-start(), calls=%async_computation.20 | async-start | bytes 3538944 | tf_op jit(solution)/shard_map/psum | solution.py:466
  (534 other events, 4823.5 us)
Sparse Core Ops, SparseCore 0:
  1069.1 66.3 reduce-scatter.20
  1139.4 68.0 reduce-scatter.12
  2478.9 127.9 reduce-scatter.10
  2610.3 162.4 reduce-scatter.14
  2776.2 162.5 reduce-scatter.16
  2941.9 60.4 reduce-scatter.18
  3005.6 45.6 all-reduce.15
where the time goes:
time: 3090 us; the launch traced here: 3070 us
  matrix products  1010 us (33%)
  local copies, waits for them, and re-layouts  959 us (31%)
  waiting for transfers between devices  538 us (17%)
  other arithmetic  460 us (15%)
  starting transfers between devices  74.6 us (2%)
    dot_general x24, matrix products, owner_backward(): jnp.einsum('sqk,sqd->skd', grad_scores, query_blk, preferred_element_type...  257 us
    dot_general x24, matrix products, owner_backward(): jnp.einsum('sqk,skd->sqd', grad_scores, key_rows, preferred_element_type=...  250 us
    reduce_scatter x1, waiting for transfers between devices, on_device(): lax.psum_scatter(grad_up, 'seq', scatter_dimension=0, tiled=True)  164 us
    reduce_scatter x1, waiting for transfers between devices, on_device(): lax.psum_scatter(grad_down, 'seq', scatter_dimension=0, tiled=True)  164 us
    gather x48, local copies, waits for them, and re-layouts, partner_swap_path(): jnp.take(member_portion, xor_order, axis=0)  140 us
    dot_general x24, matrix products, owner_backward(): jnp.einsum('sqd,skd->sqk', grad_blk, value_rows, preferred_element_type=j...  90.7 us
    reshape x8, local copies, waits for them, and re-layouts, on_device(): qkv_grad = qkv_grad + jnp.einsum('cue,cuawd->acwed', tables[pattern], got...  83.8 us
    unnamed x1040, local copies, waits for them, and re-layouts  75.6 us
  transfers between devices with their start and end apart: 51, of which 12 were waited for; matrix products, arithmetic and copies ran while one was open for 64% of the time, Pallas kernels for 0%

commit v1 on v0

v1 whole, which is shorter than its diff:
```python
import functools
import math

import jax
import jax.numpy as jnp
from jax import lax
from jax.experimental import pallas as pl
from jax.experimental.pallas import tpu as pltpu
from jax.sharding import PartitionSpec as P

HEADS = 12
HD = 64
HPAD = 80
CLASS_SLOT = (0, 2, 1, 3)
LOG2E = 1.4426950408889634
NEG = -1e30
EPS = 1e-05
VMEM = 56 << 20

f32 = jnp.float32
bf16 = jnp.bfloat16


def dot_nn(a, b):
    return lax.dot_general(a, b, (((1,), (0,)), ((), ())), preferred_element_type=f32)


def dot_nt(a, b):
    return lax.dot_general(a, b, (((1,), (1,)), ((), ())), preferred_element_type=f32)


def dot_tn(a, b):
    return lax.dot_general(a, b, (((0,), (0,)), ((), ())), preferred_element_type=f32)


def class_slot(cls):
    return jnp.where(cls == 1, 2, jnp.where(cls == 2, 1, cls))


def rel_pos(shape, dim, offset, pattern):
    i = lax.broadcasted_iota(jnp.int32, shape, dim) + offset
    if pattern == 0:
        return (i % 128) * 4 + class_slot((i // 128) % 4)
    if pattern == 1:
        return (i // 256) * 512 + (i % 128) * 4 + ((i // 128) % 2) * 2
    return i


def doc_rows(len_ref, micro, start, dilation, count):
    pos = lax.broadcasted_iota(jnp.int32, (1, count), 1) * dilation + start
    edge = len_ref[micro, 0]
    doc = (pos >= edge).astype(jnp.int32)
    for n in range(1, len_ref.shape[1] - 1):
        edge = edge + len_ref[micro, n]
        doc = doc + (pos >= edge).astype(jnp.int32)
    return doc


def segment_start(pattern, span):
    team = 2**pattern
    return (lax.axis_index("seq") // team) * (team * span)


def split3(x):
    hi = x.astype(bf16).astype(f32)
    mid = (x - hi).astype(bf16).astype(f32)
    return hi, mid, x - hi - mid


def stat_rows(rows, count):
    r = lax.broadcasted_iota(jnp.int32, (HPAD - HD, count), 0)
    out = jnp.zeros((HPAD - HD, count), f32)
    for n, row in enumerate(rows):
        out = jnp.where(r == n, row, out)
    return out.astype(bf16)


def attn_fwd_body(x_ref, len_ref, o_ref, ks, qs, *, pattern, micro, span):
    groups, _, _, lanes = x_ref.shape
    count = groups * lanes
    doc = doc_rows(len_ref, micro, segment_start(pattern, span), 2**pattern, count)

    def block(c, start, size):
        return x_ref[start // lanes, c, :, start % lanes : start % lanes + size]

    kb = min(512, lanes)
    for s in range(0, count, kb):
        sl = slice(s, s + kb)
        r = lax.broadcasted_iota(jnp.int32, (HD, kb), 0)
        same = doc[:, sl] == r
        aux_k = jnp.where(same, 1.0, 0.0).astype(bf16)
        aux_q = jnp.where(same | (r >= 4), 0.0, NEG).astype(bf16)
        q = (block(0, s, kb).astype(f32) * 0.125).astype(bf16)
        qs[:, sl] = jnp.concatenate([q, aux_q], 0)
        ks[sl, :] = jnp.concatenate([block(1, s, kb), aux_k], 0).T

    qb = 256
    grain = 512 if pattern == 0 else 256

    def tiles(i):
        low = (i * qb) // grain * grain
        out = [(s, min(512, low - s), False) for s in range(0, low, 512)]
        return out + [(low, grain, True)]

    def scores(i):
        out = []
        for s, size, diagonal in tiles(i):
            t = dot_nn(ks[s : s + size, :], qs[:, i * qb : (i + 1) * qb])
            if diagonal:
                keep = rel_pos((size, qb), 0, s % 512, pattern) <= rel_pos(
                    (size, qb), 1, (i * qb) % 512, pattern
                )
                t = jnp.where(keep, t, NEG)
            out.append(t)
        return out

    following = scores(0)
    for i in range(count // qb):
        current = following
        if (i + 1) * qb < count:
            following = scores(i + 1)
        top = functools.reduce(jnp.maximum, [jnp.max(t, 0, keepdims=True) for t in current])
        top2 = top * LOG2E
        acc, total = None, None
        for t, (s, size, _) in zip(current, tiles(i)):
            p = jnp.exp2(t * LOG2E - top2)
            part = jnp.sum(p, 0, keepdims=True)
            out = dot_nn(block(2, s, size), p.astype(bf16))
            acc = out if acc is None else acc + out
            total = part if total is None else total + part
        lse = top + jnp.log(total)
        g, at = (i * qb) // lanes, (i * qb) % lanes
        o_ref[g, :HD, at : at + qb] = (acc / total).astype(bf16)
        o_ref[g, HD:, at : at + qb] = stat_rows(split3(lse), qb)


def attn_bwd_body(
    x_ref, g_ref, len_ref, o_ref, ks, vs, qs, qr, gs, gr, dq, *, pattern, micro, span
):
    groups, _, _, lanes = x_ref.shape
    count = groups * lanes
    doc = doc_rows(len_ref, micro, segment_start(pattern, span), 2**pattern, count)
    bs = min(512, lanes)

    def block(c, start, size):
        return x_ref[start // lanes, c, :, start % lanes : start % lanes + size]

    zeros = jnp.zeros((HD, bs), bf16)
    r = lax.broadcasted_iota(jnp.int32, (HD, bs), 0)
    fill = jnp.zeros((HD - 32, bs), bf16)
    for s in range(0, count, bs):
        sl = slice(s, s + bs)
        same = doc[:, sl] == r
        aux_k = jnp.where(same | ((r >= 16) & (r < 19)), 1.0, 0.0).astype(bf16)
        aux_q = jnp.where(same | (r >= 4), 0.0, NEG).astype(bf16)
        aux_v = jnp.where((r >= 19) & (r < 21), 1.0, 0.0).astype(bf16)
        q = (block(0, s, bs).astype(f32) * 0.125).astype(bf16)
        k = block(1, s, bs)
        v = block(2, s, bs)
        at = s % lanes
        g = g_ref[s // lanes, :HD, at : at + bs]
        stats = g_ref[s // lanes, HD:, at : at + bs]
        qs[:, sl] = jnp.concatenate([q, aux_q[:16], stats, fill], 0)
        gs[:, sl] = jnp.concatenate([g, zeros[:16], stats, fill], 0)
        qr[sl, :] = jnp.concatenate([q, zeros], 0).T
        gr[sl, :] = jnp.concatenate([g, zeros], 0).T
        ks[sl, :] = jnp.concatenate([k, aux_k], 0).T
        vs[sl, :] = jnp.concatenate([v, aux_v], 0).T

    keep = rel_pos((bs, bs), 0, 0, pattern) <= rel_pos((bs, bs), 1, 0, pattern)
    for j in range(count // bs):
        jl = slice(j * bs, (j + 1) * bs)
        dva, dka = None, None
        for i in range(j, count // bs):
            il = slice(i * bs, (i + 1) * bs)
            p = jnp.exp2(dot_nn(ks[jl, :], qs[:, il]) * LOG2E)
            if i == j:
                p = jnp.where(keep, p, 0.0)
            dp = dot_nn(vs[jl, :], gs[:, il])
            ds = (p * dp).astype(bf16)
            dvi = dot_nn(p.astype(bf16), gr[il, :])
            dki = dot_nn(ds, qr[il, :])
            dva = dvi if dva is None else dva + dvi
            dka = dki if dka is None else dka + dki
            dqi = dot_nn(block(1, j * bs, bs), ds) * 0.125
            if j == 0:
                dq[:, il] = dqi
            else:
                dq[:, il] += dqi
        g, at = (j * bs) // lanes, (j * bs) % lanes
        o_ref[g, 1, :, at : at + bs] = dka.T[:HD].astype(bf16)
        o_ref[g, 2, :, at : at + bs] = dva.T[:HD].astype(bf16)
        o_ref[g, 0, :, at : at + bs] = dq[:, jl].astype(bf16)


def specs_of(pattern, span, reps):
    if pattern == 0:
        return (
            3,
            pl.BlockSpec((reps, 3, HD, span // reps), lambda n: (0, 0, n, 0)),
            pl.BlockSpec((reps, None, HPAD, span // reps), lambda n: (0, n, 0, 0)),
            (reps, 3, HPAD, span // reps),
            (reps, 3, 3 * HD, span // reps),
        )
    if pattern == 1:
        return (
            2,
            pl.BlockSpec((2, None, 3, HD, span // 2), lambda n: (0, n, 0, 0, 0)),
            pl.BlockSpec((2, None, HPAD, span // 2), lambda n: (0, n, 0, 0)),
            (2, 2, HPAD, span // 2),
            (2, 2, 3, HD, span // 2),
        )
    return (
        1,
        pl.BlockSpec((4, 3, HD, span // 4), lambda n: (0, 0, 0, 0)),
        pl.BlockSpec((4, HPAD, span // 4), lambda n: (0, 0, 0)),
        (4, HPAD, span // 4),
        (4, 3, HD, span // 4),
    )


def smem_spec():
    return pl.BlockSpec(memory_space=pltpu.SMEM)


def attn_fwd(x, lengths, pattern, micro, span, reps):
    n, x_spec, o_spec, o_shape, _ = specs_of(pattern, span, reps)
    return pl.pallas_call(
        functools.partial(attn_fwd_body, pattern=pattern, micro=micro, span=span),
        grid=(n,),
        in_specs=[x_spec, smem_spec()],
        out_specs=o_spec,
        out_shape=jax.ShapeDtypeStruct(o_shape, bf16),
        scratch_shapes=[pltpu.VMEM((span, 128), bf16), pltpu.VMEM((128, span), bf16)],
        compiler_params=pltpu.CompilerParams(vmem_limit_bytes=VMEM),
        cost_estimate=pl.CostEstimate(
            flops=n * 5_000_000_000, bytes_accessed=n * 1_200_000, transcendentals=n * 2_600_000
        ),
        name=f"attn_fwd_{pattern}_{micro}",
    )(x, lengths)


def attn_bwd(x, g, lengths, pattern, micro, span, reps):
    n, x_spec, g_spec, _, d_shape = specs_of(pattern, span, reps)
    wide = pltpu.VMEM((128, span), bf16)
    tall = pltpu.VMEM((span, 128), bf16)
    return pl.pallas_call(
        functools.partial(attn_bwd_body, pattern=pattern, micro=micro, span=span),
        grid=(n,),
        in_specs=[x_spec, g_spec, smem_spec()],
        out_specs=x_spec,
        out_shape=jax.ShapeDtypeStruct(d_shape, bf16),
        scratch_shapes=[tall, tall, wide, tall, wide, tall, pltpu.VMEM((HD, span), f32)],
        compiler_params=pltpu.CompilerParams(vmem_limit_bytes=VMEM),
        cost_estimate=pl.CostEstimate(
            flops=n * 8_000_000_000, bytes_accessed=n * 2_000_000, transcendentals=n * 2_600_000
        ),
        name=f"attn_bwd_{pattern}_{micro}",
    )(x, g, lengths)


OWNER1 = {(0, 0): 0, (0, 1): 2, (1, 0): 1}
PLACE1 = {0: (0, 0), 1: (1, 0), 2: (0, 1)}


def half_of(j):
    return (3 * lax.axis_index("rep") + j) % 2


def quarter_of(j):
    return class_slot((3 * lax.axis_index("rep") + j) % 4)


def lane_slice(start, size):
    return pl.ds(pl.multiple_of(start, size), size)


def pack_qkv_body(r_ref, p1_ref, p2_ref):
    reps = r_ref.shape[0]
    for e in range(2):
        for s in range(2):
            j = OWNER1.get((e, s), 1)
            for b in range(reps):
                p1_ref[e, s, :, :, b * 256 : (b + 1) * 256] = r_ref[
                    b, :, j * HD : (j + 1) * HD, lane_slice(half_of(j) * 256, 256)
                ]
    for g in range(4):
        j = min(g, 2)
        for b in range(reps):
            p2_ref[g, :, :, b * 128 : (b + 1) * 128] = r_ref[
                b, :, j * HD : (j + 1) * HD, lane_slice(quarter_of(j) * 128, 128)
            ]


def vmem_spec():
    return pl.BlockSpec(memory_space=pltpu.VMEM)


def small_call(body, outs, args, name, nbytes, scratch=(), smem=()):
    return pl.pallas_call(
        body,
        in_specs=[smem_spec() if n in smem else vmem_spec() for n in range(len(args))],
        out_specs=[vmem_spec() for _ in outs],
        out_shape=[jax.ShapeDtypeStruct(s, d) for s, d in outs],
        scratch_shapes=list(scratch),
        compiler_params=pltpu.CompilerParams(vmem_limit_bytes=VMEM),
        cost_estimate=pl.CostEstimate(flops=1_000_000, bytes_accessed=nbytes, transcendentals=0),
        name=name,
    )(*args)


def pack_qkv(r, span, reps, micro):
    return small_call(
        pack_qkv_body,
        [((2, 2, 3, HD, span // 2), bf16), ((4, 3, HD, span // 4), bf16)],
        (r,),
        f"pack_qkv_{micro}",
        5_000_000,
    )


def mix_body(o0_ref, o1_ref, o2_ref, att_ref, mix_ref):
    reps = o0_ref.shape[0]

    def stat(tile):
        t = tile[HD:, :].astype(f32)
        return t[0:1] + t[1:2] + t[2:3]

    mix_ref[...] = jnp.zeros_like(mix_ref)
    for j in range(3):
        half, quarter = half_of(j), quarter_of(j)
        e, s = PLACE1[j]
        for b in range(reps):
            for a in range(4):
                la = slice(a * 128, (a + 1) * 128)
                t0 = o0_ref[b, j, :, la]
                lb = b * 256 + (a % 2) * 128
                t1 = o1_ref[e, s, :, lb : lb + 128]
                t2 = o2_ref[j, :, b * 128 : (b + 1) * 128]
                l0 = stat(t0)
                l1 = jnp.where(half == a // 2, stat(t1), NEG)
                l2 = jnp.where(quarter == a, stat(t2), NEG)
                top = jnp.maximum(jnp.maximum(l0, l1), l2)
                e0, e1, e2 = jnp.exp(l0 - top), jnp.exp(l1 - top), jnp.exp(l2 - top)
                total = e0 + e1 + e2
                inv = 1.0 / total
                mixed = (
                    t0[:HD].astype(f32) * (e0 * inv)
                    + t1[:HD].astype(f32) * (e1 * inv)
                    + t2[:HD].astype(f32) * (e2 * inv)
                )
                att_ref[b, j * HD : (j + 1) * HD, la] = mixed.astype(bf16)
                col = b * 512 + a * 128
                mix_ref[j : j + 1, col : col + 128] = top + jnp.log(total)


def mix(o0, o1, o2, span, reps, micro):
    return small_call(
        mix_body,
        [((reps, 3 * HD, span // reps), bf16), ((8, span), f32)],
        (o0, o1, o2),
        f"mix_{micro}",
        4_000_000,
    )


def pack_grad_body(g_ref, att_ref, mix_ref, g0_ref, p1_ref, p2_ref):
    reps, _, tok = g_ref.shape
    for j in range(3):
        rows = slice(j * HD, (j + 1) * HD)
        for b in range(reps):
            g = g_ref[b, rows, :]
            inner = jnp.sum(g.astype(f32) * att_ref[b, rows, :].astype(f32), 0, keepdims=True)
            total = mix_ref[j : j + 1, b * tok : (b + 1) * tok]
            h, m, l = split3(-total)
            ih, im, _ = split3(-inner)
            g0_ref[b, j, :HD, :] = g
            g0_ref[b, j, HD:, :] = stat_rows((h, m, l, ih, im), tok)
    for e in range(2):
        for s in range(2):
            j = OWNER1.get((e, s), 1)
            for b in range(reps):
                p1_ref[e, s, :, b * 256 : (b + 1) * 256] = g0_ref[
                    b, j, :, lane_slice(half_of(j) * 256, 256)
                ]
    for g in range(4):
        j = min(g, 2)
        for b in range(reps):
            p2_ref[g, :, b * 128 : (b + 1) * 128] = g0_ref[
                b, j, :, lane_slice(quarter_of(j) * 128, 128)
            ]


def pack_grad(g, att, mixed, span, reps, micro):
    return small_call(
        pack_grad_body,
        [
            ((reps, 3, HPAD, span // reps), bf16),
            ((2, 2, HPAD, span // 2), bf16),
            ((4, HPAD, span // 4), bf16),
        ],
        (g, att, mixed),
        f"pack_grad_{micro}",
        5_000_000,
    )


def sum_grad_body(d0_ref, d1_ref, d2_ref, out_ref):
    reps = d0_ref.shape[0]
    for j in range(3):
        rows = slice(j * HD, (j + 1) * HD)
        half, quarter = half_of(j), quarter_of(j)
        e, s = PLACE1[j]
        for b in range(reps):
            for a in range(4):
                la = slice(a * 128, (a + 1) * 128)
                lb = b * 256 + (a % 2) * 128
                t0 = d0_ref[b, :, rows, la].astype(f32)
                t1 = d1_ref[e, s, :, :, lb : lb + 128].astype(f32)
                t2 = d2_ref[j, :, :, b * 128 : (b + 1) * 128].astype(f32)
                t = t0 + jnp.where(half == a // 2, t1, 0.0) + jnp.where(quarter == a, t2, 0.0)
                out_ref[b, :, rows, la] = t.astype(bf16)


def sum_grad(d0, d1, d2, span, reps, micro):
    return small_call(
        sum_grad_body,
        [((reps, 3, 3 * HD, span // reps), bf16)],
        (d0, d1, d2),
        f"sum_grad_{micro}",
        7_000_000,
    )[0]


def onehot_rows(tok):
    i = lax.broadcasted_iota(jnp.int32, (tok, tok), 0)
    t = lax.broadcasted_iota(jnp.int32, (tok, tok), 1)
    return ((i % 128) * 4 + class_slot(i // 128) == t).astype(bf16)


def onehot_cols(tok):
    t = lax.broadcasted_iota(jnp.int32, (tok, tok), 0)
    i = lax.broadcasted_iota(jnp.int32, (tok, tok), 1)
    return ((i % 128) * 4 + class_slot(i // 128) == t).astype(bf16)


def normalize(x):
    c = x - jnp.mean(x, axis=-1, keepdims=True)
    rstd = lax.rsqrt(jnp.mean(c * c, axis=-1, keepdims=True) + EPS)
    return c * rstd, rstd


def norm_back(grad, gain, xhat, rstd):
    dn = grad * gain
    low = jnp.mean(dn, axis=-1, keepdims=True)
    along = jnp.mean(dn * xhat, axis=-1, keepdims=True)
    dx = rstd * (dn - low - xhat * along)
    return dx, jnp.sum(grad * xhat, 0, keepdims=True), jnp.sum(grad, 0, keepdims=True)


def qkv_body(x_ref, w_ref, gain_ref, bias_ref, out_ref, xp_ref, nt_ref, n_scr):
    tok, width = x_ref.shape

    @pl.when(pl.program_id(0) == 0)
    def _():
        xp = dot_nn(onehot_rows(tok), x_ref[...])
        xp_ref[...] = xp.astype(bf16)
        xhat, _ = normalize(xp)
        n = (xhat * gain_ref[...] + bias_ref[...]).astype(bf16)
        n_scr[...] = n
        nt_ref[...] = n.T

    t = dot_nn(n_scr[...], w_ref[...]).astype(bf16).T
    reps, _, cols, _ = out_ref.shape
    for r in range(reps):
        out_ref[r, 0] = t[r * cols : (r + 1) * cols]


def qkv_call(layer_in, weight, gain, bias, m, reps):
    _, tok, width = layer_in.shape
    cols = width // reps
    return pl.pallas_call(
        qkv_body,
        grid=(3,),
        in_specs=[
            pl.BlockSpec((None, tok, width), lambda c: (m, 0, 0)),
            pl.BlockSpec((width, width), lambda c: (0, c)),
            pl.BlockSpec((1, width), lambda c: (0, 0)),
            pl.BlockSpec((1, width), lambda c: (0, 0)),
        ],
        out_specs=[
            pl.BlockSpec((reps, 1, cols, tok), lambda c: (0, c, 0, 0)),
            pl.BlockSpec((tok, width), lambda c: (0, 0)),
            pl.BlockSpec((width, tok), lambda c: (0, 0)),
        ],
        out_shape=[
            jax.ShapeDtypeStruct((reps, 3, cols, tok), bf16),
            jax.ShapeDtypeStruct((tok, width), bf16),
            jax.ShapeDtypeStruct((width, tok), bf16),
        ],
        scratch_shapes=[pltpu.VMEM((tok, width), bf16)],
        compiler_params=pltpu.CompilerParams(vmem_limit_bytes=VMEM),
        cost_estimate=pl.CostEstimate(
            flops=6 * tok * width * width, bytes_accessed=9_000_000, transcendentals=0
        ),
        name=f"qkv_{m}",
    )(layer_in, weight, gain, bias)


CHUNK = 512
SQRT_HALF = 0.7071067811865476
INV_SQRT_2PI = 0.3989422804014327


def ffn_body(
    att_ref,
    xp_ref,
    cot_ref,
    wo_hbm,
    wu_hbm,
    wd_hbm,
    mg_ref,
    mb_ref,
    bg_ref,
    bb_ref,
    hg_ref,
    hb_ref,
    out_ref,
    branch_ref,
    da_ref,
    mix_ref,
    low_ref,
    hid_ref,
    dup_ref,
    brl_ref,
    cotp_ref,
    ng_ref,
    nh_ref,
    wo,
    wu,
    wd,
    g_scr,
    dg_scr,
    dn_scr,
    am_scr,
    acc_scr,
    sems,
):
    tok, width = xp_ref.shape
    hidden = hid_ref.shape[1]
    chunks = hidden // CHUNK
    reps, cols, _ = att_ref.shape
    copies = [
        pltpu.make_async_copy(a, b, sems.at[n])
        for n, (a, b) in enumerate(((wo_hbm, wo), (wu_hbm, wu), (wd_hbm, wd)))
    ]
    for c in copies:
        c.start()
    cotp = dot_nn(onehot_rows(tok), cot_ref[...])
    cotp_ref[...] = cotp.astype(bf16)
    att = att_ref[...].reshape(width, tok).T.astype(f32)
    ahat, _ = normalize(att)
    mix_ref[...] = (ahat * mg_ref[...] + mb_ref[...]).astype(bf16)
    copies[0].wait()
    am = xp_ref[...].astype(f32) + dot_nn(mix_ref[...], wo[...])
    am_scr[...] = am
    bhat, _ = normalize(am)
    low_ref[...] = (bhat * bg_ref[...] + bb_ref[...]).astype(bf16)
    copies[1].wait()

    def lanes(n):
        return pl.ds(pl.multiple_of(n * CHUNK, CHUNK), CHUNK)

    def upward(n, total):
        u = dot_nn(low_ref[...], wu[:, lanes(n)])
        cdf = 0.5 + 0.5 * lax.erf(u * SQRT_HALF)
        g = u * cdf
        g_scr[:, lanes(n)] = g
        dg_scr[:, lanes(n)] = cdf + u * (jnp.exp(u * u * -0.5) * INV_SQRT_2PI)
        return total + jnp.sum(g, 1, keepdims=True)

    mean = lax.fori_loop(0, chunks, upward, jnp.zeros((tok, 1), f32)) / hidden

    def spread(n, total):
        c = g_scr[:, lanes(n)] - mean
        return total + jnp.sum(c * c, 1, keepdims=True)

    var = lax.fori_loop(0, chunks, spread, jnp.zeros((tok, 1), f32)) / hidden
    rstd = lax.rsqrt(var + EPS)
    copies[2].wait()
    acc_scr[...] = jnp.zeros_like(acc_scr)

    def downward(n, sums):
        first, second = sums
        ghat = (g_scr[:, lanes(n)] - mean) * rstd
        g_scr[:, lanes(n)] = ghat
        gain = hg_ref[:, lanes(n)]
        h = (ghat * gain + hb_ref[:, lanes(n)]).astype(bf16)
        hid_ref[:, lanes(n)] = h
        acc_scr[...] += dot_nn(h, wd[lanes(n), :])
        back = dot_nt(cotp_ref[...], wd[lanes(n), :])
        nh_ref[0:1, lanes(n)] = jnp.sum(back * ghat, 0, keepdims=True)
        nh_ref[1:2, lanes(n)] = jnp.sum(back, 0, keepdims=True)
        dn = back * gain
        dn_scr[:, lanes(n)] = dn
        return (
            first + jnp.sum(dn, 1, keepdims=True),
            second + jnp.sum(dn * ghat, 1, keepdims=True),
        )

    zero = jnp.zeros((tok, 1), f32)
    first, second = lax.fori_loop(0, chunks, downward, (zero, zero))
    first, second = first / hidden, second / hidden
    out_ref[...] = dot_nn(onehot_cols(tok), (am_scr[...] + acc_scr[...]).astype(bf16)).astype(bf16)
    acc_scr[...] = jnp.zeros_like(acc_scr)

    def backward(n, carry):
        d = rstd * (dn_scr[:, lanes(n)] - first - g_scr[:, lanes(n)] * second)
        dup = (d * dg_scr[:, lanes(n)]).astype(bf16)
        dup_ref[:, lanes(n)] = dup
        acc_scr[...] += dot_nt(dup, wu[:, lanes(n)])
        return carry

    lax.fori_loop(0, chunks, backward, 0)
    bhat, brstd = normalize(am_scr[...])
    middle, gain_b, bias_b = norm_back(acc_scr[...], bg_ref[...], bhat, brstd)
    branch = cotp_ref[...].astype(f32) + middle
    branch_ref[...] = branch
    brl_ref[...] = branch.astype(bf16)
    att = att_ref[...].reshape(width, tok).T.astype(f32)
    ahat, arstd = normalize(att)
    da, gain_m, bias_m = norm_back(dot_nt(brl_ref[...], wo[...]), mg_ref[...], ahat, arstd)
    da_ref[...] = da.astype(bf16).T.reshape(reps, cols, tok)
    ng_ref[0:1] = gain_m
    ng_ref[1:2] = bias_m
    ng_ref[2:3] = gain_b
    ng_ref[3:4] = bias_b


def ffn_call(att, xp, output_grad, weights, gains, m):
    reps, cols, tok = att.shape
    width = xp.shape[1]
    hidden = weights[1].shape[1]
    vec = vmem_spec()
    shapes = [
        ((tok, width), bf16),
        ((tok, width), f32),
        ((reps, cols, tok), bf16),
        ((tok, width), bf16),
        ((tok, width), bf16),
        ((tok, hidden), bf16),
        ((tok, hidden), bf16),
        ((tok, width), bf16),
        ((tok, width), bf16),
        ((4, width), f32),
        ((2, hidden), f32),
    ]
    return pl.pallas_call(
        ffn_body,
        grid=(1,),
        in_specs=[
            pl.BlockSpec((reps, cols, tok), lambda n: (0, 0, 0)),
            pl.BlockSpec((tok, width), lambda n: (0, 0)),
            pl.BlockSpec((None, tok, width), lambda n: (m, 0, 0)),
        ]
        + [pl.BlockSpec(memory_space=pl.ANY)] * 3
        + [pl.BlockSpec(g.shape, lambda n: (0, 0)) for g in gains],
        out_specs=[pl.BlockSpec(s, lambda n, k=len(s): (0,) * k) for s, _ in shapes],
        out_shape=[jax.ShapeDtypeStruct(s, d) for s, d in shapes],
        scratch_shapes=[pltpu.VMEM(w.shape, bf16) for w in weights]
        + [pltpu.VMEM((tok, hidden), f32)] * 3
        + [pltpu.VMEM((tok, width), f32)] * 2
        + [pltpu.SemaphoreType.DMA((3,))],
        compiler_params=pltpu.CompilerParams(vmem_limit_bytes=VMEM),
        cost_estimate=pl.CostEstimate(
            flops=4 * tok * width * (2 * hidden + width),
            bytes_accessed=25_000_000,
            transcendentals=2 * tok * hidden,
        ),
        name=f"ffn_{m}",
    )(att, xp, output_grad, *weights, *gains)


def weight_grad_body(*refs):
    micros = (len(refs) - 6) // 6
    groups = [refs[6 * k : 6 * k + 6] for k in range(micros)]
    down_ref, up_ref, proj_ref, lt, _, _ = refs[6 * micros :]

    @pl.when(pl.program_id(0) == 0)
    def _():
        total = None
        for k, (low, dup, hid, cot, mix, brl) in enumerate(groups):
            lt[k] = low[...].T
            part = dot_tn(mix[...], brl[...])
            total = part if total is None else total + part
        proj_ref[...] = total.astype(bf16)

    up = down = None
    for k, (low, dup, hid, cot, mix, brl) in enumerate(groups):
        u = dot_nn(lt[k], dup[...])
        d = dot_tn(hid[...], cot[...])
        up = u if up is None else up + u
        down = d if down is None else down + d
    up_ref[...] = up.astype(bf16)
    down_ref[...] = down.astype(bf16)


def weight_grads(groups, tok, width, hidden):
    full = pl.BlockSpec((tok, width), lambda n: (0, 0))
    part = pl.BlockSpec((tok, CHUNK), lambda n: (0, n))
    micros = len(groups)
    return pl.pallas_call(
        weight_grad_body,
        grid=(hidden // CHUNK,),
        in_specs=[full, part, part, full, full, full] * micros,
        out_specs=[
            pl.BlockSpec((CHUNK, width), lambda n: (n, 0)),
            pl.BlockSpec((width, CHUNK), lambda n: (0, n)),
            pl.BlockSpec((width, width), lambda n: (0, 0)),
        ],
        out_shape=[
            jax.ShapeDtypeStruct((hidden, width), bf16),
            jax.ShapeDtypeStruct((width, hidden), bf16),
            jax.ShapeDtypeStruct((width, width), bf16),
        ],
        scratch_shapes=[pltpu.VMEM((micros, width, tok), bf16)]
        + [pltpu.VMEM((8, 128), f32)] * 2,
        compiler_params=pltpu.CompilerParams(vmem_limit_bytes=VMEM),
        cost_estimate=pl.CostEstimate(
            flops=2 * micros * tok * width * (2 * hidden + width),
            bytes_accessed=30_000_000,
            transcendentals=0,
        ),
        name="weight_grads",
    )(*[a for g in groups for a in g])


def join_heads(tg_ref, c):
    reps = tg_ref.shape[0]
    return jnp.concatenate([tg_ref[r, c] for r in range(reps)], 0)


def qkv_grad_body(*refs):
    micros = (len(refs) - 1) // 2
    out_ref = refs[-1]
    total = None
    for k in range(micros):
        nt, tg = refs[2 * k], refs[2 * k + 1]
        part = dot_nt(nt[...], join_heads(tg, 0))
        total = part if total is None else total + part
    out_ref[...] = total.astype(bf16)


def qkv_grad_call(pairs, tok, width, reps):
    cols = width // reps
    return pl.pallas_call(
        qkv_grad_body,
        grid=(3,),
        in_specs=[
            pl.BlockSpec((width, tok), lambda c: (0, 0)),
            pl.BlockSpec((reps, 1, cols, tok), lambda c: (0, c, 0, 0)),
        ]
        * len(pairs),
        out_specs=pl.BlockSpec((width, width), lambda c: (0, c)),
        out_shape=jax.ShapeDtypeStruct((width, 3 * width), bf16),
        compiler_params=pltpu.CompilerParams(vmem_limit_bytes=VMEM),
        cost_estimate=pl.CostEstimate(
            flops=6 * len(pairs) * tok * width * width, bytes_accessed=10_000_000, transcendentals=0
        ),
        name="qkv_grad",
    )(*[a for p in pairs for a in p])


def input_grad_body(tg_ref, w_ref, xp_ref, branch_ref, gain_ref, out_ref, ng_ref, acc):
    tok, width = xp_ref.shape
    c = pl.program_id(0)
    part = dot_nn(w_ref[...], join_heads(tg_ref, 0))

    @pl.when(c == 0)
    def _():
        acc[...] = part

    @pl.when(c > 0)
    def _():
        acc[...] += part

    @pl.when(c == 2)
    def _():
        xhat, rstd = normalize(xp_ref[...].astype(f32))
        dx, gain_i, bias_i = norm_back(acc[...].T, gain_ref[...], xhat, rstd)
        ng_ref[0:1] = gain_i
        ng_ref[1:2] = bias_i
        total = (branch_ref[...] + dx).astype(bf16)
        out_ref[...] = dot_nn(onehot_cols(tok), total).astype(bf16)


def input_grad_call(tg, weight, xp, branch, gain, m):
    reps, _, cols, tok = tg.shape
    width = reps * cols
    return pl.pallas_call(
        input_grad_body,
        grid=(3,),
        in_specs=[
            pl.BlockSpec((reps, 1, cols, tok), lambda c: (0, c, 0, 0)),
            pl.BlockSpec((width, width), lambda c: (0, c)),
            pl.BlockSpec((tok, width), lambda c: (0, 0)),
            pl.BlockSpec((tok, width), lambda c: (0, 0)),
            pl.BlockSpec((1, width), lambda c: (0, 0)),
        ],
        out_specs=[
            pl.BlockSpec((tok, width), lambda c: (0, 0)),
            pl.BlockSpec((2, width), lambda c: (0, 0)),
        ],
        out_shape=[
            jax.ShapeDtypeStruct((tok, width), bf16),
            jax.ShapeDtypeStruct((2, width), f32),
        ],
        scratch_shapes=[pltpu.VMEM((width, tok), f32)],
        compiler_params=pltpu.CompilerParams(vmem_limit_bytes=VMEM),
        cost_estimate=pl.CostEstimate(
            flops=6 * tok * width * width, bytes_accessed=10_000_000, transcendentals=0
        ),
        name=f"input_grad_{m}",
    )(tg, weight, xp, branch, gain)


def swap(block, axis, bit):
    count = lax.axis_size(axis)
    return lax.ppermute(block, axis, [(n, n ^ (1 << bit)) for n in range(count)])


def bits_of(count):
    return count.bit_length() - 1


def reduce_rows(x, order):
    seqs, reps = lax.axis_size("seq"), lax.axis_size("rep")
    rows, cols = x.shape
    sb, rb = bits_of(seqs), bits_of(reps)
    y = x.reshape((2,) * (sb + rb) + (rows // (seqs * reps), cols))
    names = [("seq", b) for b in reversed(range(sb))] + [("rep", b) for b in reversed(range(rb))]
    for step in order(sb, rb):
        at = names.index(step)
        axis, bit = step
        mine = (lax.axis_index(axis) >> bit) & 1
        send = lax.dynamic_index_in_dim(y, 1 - mine, at, keepdims=False)
        keep = lax.dynamic_index_in_dim(y, mine, at, keepdims=False)
        got = swap(send.astype(x.dtype), axis, bit)
        y = (keep.astype(f32) + got.astype(f32)).astype(x.dtype)
        names.pop(at)
    for bit in range(rb):
        other = swap(y, "rep", bit)
        mine = (lax.axis_index("rep") >> bit) & 1
        y = jnp.where(mine == 0, jnp.stack([y, other]), jnp.stack([other, y]))
        y = y.reshape((-1,) + y.shape[2:])
    return y.astype(f32)


def order_yxz(sb, rb):
    return [("rep", b) for b in range(rb)] + [("seq", b) for b in range(sb)]


def order_xzy(sb, rb):
    return [("rep", 0)] + [("seq", b) for b in range(sb)] + [("rep", b) for b in range(1, rb)]


def on_device(
    layer_in,
    qkv_weight,
    out_weight,
    up_weight,
    down_weight,
    input_gain,
    input_bias,
    mixer_gain,
    mixer_bias,
    block_gain,
    block_bias,
    hidden_gain,
    hidden_bias,
    output_grad,
    seq_lengths,
):
    micro_count, tok, width = layer_in.shape
    reps = lax.axis_size("rep")
    seqs = lax.axis_size("seq")
    span = tok * reps
    heads_dev = HEADS // reps
    cols = heads_dev * HD
    pairs = [[2 * n, 2 * n + 1] for n in range(seqs // 2)]
    fours = [[4 * n + k for k in range(4)] for n in range(seqs // 4)]

    def to_reps(x):
        return lax.all_to_all(x, "rep", 0, 0, tiled=True)

    def to_pair(x):
        return lax.all_to_all(x, "seq", 0, 0, tiled=True, axis_index_groups=pairs)

    def to_four(x):
        return lax.all_to_all(x, "seq", 0, 0, tiled=True, axis_index_groups=fours)

    def row(v):
        return v.reshape(1, -1)

    micros = range(micro_count)
    residual, normed, got_qkv = [], [], []
    for m in micros:
        sent, xp, nt = qkv_call(layer_in, qkv_weight, row(input_gain), row(input_bias), m, reps)
        residual.append(xp)
        normed.append(nt)
        got_qkv.append(to_reps(sent))

    pieces, attended, own_att, totals = [], [], [], []
    for m in micros:
        p1, p2 = pack_qkv(got_qkv[m], span, reps, m)
        p1, p2 = to_pair(p1), to_four(p2)
        pieces.append((got_qkv[m], p1, p2))
        o0 = attn_fwd(got_qkv[m], seq_lengths, 0, m, span, reps)
        o1 = to_pair(attn_fwd(p1, seq_lengths, 1, m, span, reps))
        o2 = to_four(attn_fwd(p2, seq_lengths, 2, m, span, reps))
        att, total = mix(o0, o1, o2, span, reps, m)
        own_att.append(att)
        totals.append(total)
        attended.append(to_reps(att))

    outputs, branch_grads, head_grads, groups, norm_terms, hidden_terms = [], [], [], [], [], []
    weights = (out_weight, up_weight, down_weight)
    gains = tuple(
        row(v) for v in (mixer_gain, mixer_bias, block_gain, block_bias, hidden_gain, hidden_bias)
    )
    for m in micros:
        out, branch, da, mixl, low, hid, dup, brl, cotp, ng, nh = ffn_call(
            attended[m], residual[m], output_grad, weights, gains, m
        )
        outputs.append(out)
        branch_grads.append(branch)
        head_grads.append(to_reps(da))
        groups.append((low, dup, hid, cotp, mixl, brl))
        norm_terms.append(ng)
        hidden_terms.append(nh)
    grad_down, grad_up, grad_proj = weight_grads(groups, tok, width, up_weight.shape[1])

    down_total = reduce_rows(grad_down, order_yxz)
    up_total = reduce_rows(grad_up, order_xzy)
    proj_total = reduce_rows(grad_proj, order_xzy)

    input_grads, input_terms, token_grads = [], [], []
    for m in micros:
        g0, g1, g2 = pack_grad(head_grads[m], own_att[m], totals[m], span, reps, m)
        g1, g2 = to_pair(g1), to_four(g2)
        x0, x1, x2 = pieces[m]
        d0 = attn_bwd(x0, g0, seq_lengths, 0, m, span, reps)
        d1 = to_pair(attn_bwd(x1, g1, seq_lengths, 1, m, span, reps))
        d2 = to_four(attn_bwd(x2, g2, seq_lengths, 2, m, span, reps))
        token_grads.append(to_reps(sum_grad(d0, d1, d2, span, reps, m)))
    grad_qkv = qkv_grad_call(list(zip(normed, token_grads)), tok, width, reps)
    for m in micros:
        grad, terms = input_grad_call(
            token_grads[m], qkv_weight, residual[m], branch_grads[m], row(input_gain), m
        )
        input_grads.append(grad)
        input_terms.append(terms)

    qkv_total = reduce_rows(grad_qkv, order_yxz)
    model = jnp.concatenate([sum(input_terms), sum(norm_terms)], 0)
    norm_total = reduce_rows(model.T, order_yxz)
    hidden_total = reduce_rows(sum(hidden_terms).T, order_yxz)
    return (
        jnp.stack(outputs),
        jnp.stack(input_grads),
        qkv_total,
        proj_total,
        up_total,
        down_total,
        norm_total,
        hidden_total,
    )


def solution(mesh):
    tokens = P(None, ("seq", "rep"), None)
    rows = P("seq", None)
    return jax.shard_map(
        on_device,
        mesh=mesh,
        in_specs=(tokens,) + (P(),) * 12 + (tokens, P()),
        out_specs=(tokens, tokens) + (rows,) * 6,
        check_vma=False,
    )
```

time: 3090 us -> 728 us (0.24)
  matrix products: 1010 us -> 0 us
  local copies, waits for them, and re-layouts: 959 us -> 29.2 us
  other arithmetic: 460 us -> 26.2 us
  waiting for transfers between devices: 538 us -> 203 us
  Pallas kernels: 0 us -> 302 us
  starting transfers between devices: 74.6 us -> 136 us
    dot_general x192 -> x0, matrix products: 1010 us -> none  [the longest x24 257 us: owner_backward(): jnp.einsum('sqk,sqd->skd', grad_scores, query_blk, preferred_element_type...]
    reduce_scatter x4 -> x0, waiting for transfers between devices: 397 us -> none  [the longest x1 164 us: on_device(): lax.psum_scatter(grad_up, 'seq', scatter_dimension=0, tiled=True)]
    pallas_call x0 -> x28, Pallas kernels: none -> 302 us  [the longest x6 97.4 us: attn_bwd(): pl.pallas_call(functools.partial(attn_bwd_body, pattern=pattern, micro=mi...]
    reshape x42 -> x8, local copies, waits for them, and re-layouts: 204 us -> 6.56 us  [the longest x6 4.87 us: row(): return v.reshape(1, -1)]
    another operation x62 -> x3, local copies, waits for them, and re-layouts: 186 us -> 0.01 us  [reduce_rows(): y = jnp.where(mine == 0, jnp.stack([y, other]), jnp.stack([other, y]))]
    gather x48 -> x0, local copies, waits for them, and re-layouts: 140 us -> none  [partner_swap_path(): jnp.take(member_portion, xor_order, axis=0)]
    reduce_sum x46 -> x0, other arithmetic: 104 us -> none  [the longest x24 42.3 us: owner_forward(): jnp.sum(jnp.exp(scores - top_score), axis=2, keepdims=True)]
    transpose x22 -> x0, local copies, waits for them, and re-layouts: 95.6 us -> none  [the longest x4 37.2 us: on_device(): jnp.einsum('cue,cuawd->acwed', tables[pattern], got_partials[pattern][0],...]
  transfers between devices with their start and end apart: 51 -> 64, of which waited for: 12 -> 28; matrix products, arithmetic and copies ran while one was open for 64% -> 6% of each run, Pallas kernels for 0% -> 37%
where the time goes in v1:
time: 728 us; the launch traced here: 722 us
  Pallas kernels  302 us (41%)
  waiting for transfers between devices  203 us (28%)
  starting transfers between devices  136 us (19%)
  local copies, waits for them, and re-layouts  29.2 us (4%)
  other arithmetic  26.2 us (4%)
  blocking collectives  24.8 us (3%)
    pallas_call x6, Pallas kernels, attn_bwd(): pl.pallas_call(functools.partial(attn_bwd_body, pattern=pattern, micro=mi...  97.4 us
    ppermute x42, waiting for transfers between devices, swap(): return lax.ppermute(block, axis, [(n, n ^ 1 << bit) for n in range(count)])  89 us
    pallas_call x2, Pallas kernels, ffn_call(): pl.pallas_call(ffn_body, grid=(1,), in_specs=[pl.BlockSpec((reps, cols, t...  60.8 us
    all_to_all x8, waiting for transfers between devices, to_reps(): return lax.all_to_all(x, 'rep', 0, 0, tiled=True)  60.4 us
    pallas_call x6, Pallas kernels, attn_fwd(): pl.pallas_call(functools.partial(attn_fwd_body, pattern=pattern, micro=mi...  58.7 us
    all_to_all x7, waiting for transfers between devices, to_pair(): return lax.all_to_all(x, 'seq', 0, 0, tiled=True, axis_index_groups=pairs)  51 us
    all_to_all x8, starting transfers between devices, to_reps(): return lax.all_to_all(x, 'rep', 0, 0, tiled=True)  42.8 us
    ppermute x42, starting transfers between devices, swap(): return lax.ppermute(block, axis, [(n, n ^ 1 << bit) for n in range(count)])  42 us
  transfers between devices with their start and end apart: 64, of which 28 were waited for; matrix products, arithmetic and copies ran while one was open for 6% of the time, Pallas kernels for 37%

profile of v1, /device:TPU:0, one launch (start us, length us, event | category | flops | bytes accessed | tf_op | source)
XLA Modules:
  0.0 722.4 jit_solution(11856947173274233713)
XLA Ops:
  22.0 21.3 %all-to-all-done.6.x_ref.r_ref = bf16[4,3,192,512]{3,2,1,0:T(8,128)(2,1)S(1)} async-done(((bf16[4,3,192,512]{3,2,1,0:T(8,128)(2,1)}), bf16[4,3,192,512]{3,2,1,0:T(8,128)(2,1)S(1)}, u32[]{:S(2)}, u32[]{:S(2)}) %all-to-all-start.6) | async-done | bytes 2359328 | tf_op jit(solution)/shard_map/all_to_all | solution.py:894
  52.5 25.2 %all-to-all-done.x_ref.r_ref = bf16[4,3,192,512]{3,2,1,0:T(8,128)(2,1)} async-done(((bf16[4,3,192,512]{3,2,1,0:T(8,128)(2,1)}), bf16[4,3,192,512]{3,2,1,0:T(8,128)(2,1)}, u32[]{:S(2)}, u32[]{:S(2)}) %all-to-all-start) | async-done | bytes 2359328 | tf_op jit(solution)/shard_map/all_to_all | solution.py:894
  84.8 16.5 %all-to-all-done.7.x_ref = bf16[2,2,3,64,1024]{4,3,2,1,0:T(8,128)(2,1)S(1)} async-done(((bf16[2,2,3,64,1024]{4,3,2,1,0:T(8,128)(2,1)}), bf16[2,2,3,64,1024]{4,3,2,1,0:T(8,128)(2,1)S(1)}, u32[]{:S(2)}, u32[]{:S(2)}) %all-to-all-start.7) | async-done | bytes 1572896 | tf_op jit(solution)/shard_map/all_to_all | solution.py:897
  104.9 9.5 %attn_fwd_1_1.1 = bf16[2,2,80,1024]{3,2,1,0:T(8,128)(2,1)} custom-call(bf16[2,2,3,64,1024]{4,3,2,1,0:T(8,128)(2,1)} %copy-done.13, s32[2,4]{1,0:T(2,128)} %len_ref.23), custom_call_target="tpu_custom_call" | custom-call | flops 10000000000 | bytes 2400000 | tf_op jit(solution)/shard_map/attn_fwd_1_1/pallas_call | solution.py:228
  114.5 9.1 %all-to-all-done.1.x_ref = bf16[2,2,3,64,1024]{4,3,2,1,0:T(8,128)(2,1)S(1)} async-done(((bf16[2,2,3,64,1024]{4,3,2,1,0:T(8,128)(2,1)}), bf16[2,2,3,64,1024]{4,3,2,1,0:T(8,128)(2,1)S(1)}, u32[]{:S(2)}, u32[]{:S(2)}) %all-to-all-start.1) | async-done | bytes 1572896 | tf_op jit(solution)/shard_map/all_to_all | solution.py:897
  127.2 9.6 %attn_fwd_1_0.1 = bf16[2,2,80,1024]{3,2,1,0:T(8,128)(2,1)} custom-call(bf16[2,2,3,64,1024]{4,3,2,1,0:T(8,128)(2,1)} %copy-done.14, s32[2,4]{1,0:T(2,128)} %len_ref.23), custom_call_target="tpu_custom_call" | custom-call | flops 10000000000 | bytes 2400000 | tf_op jit(solution)/shard_map/attn_fwd_1_0/pallas_call | solution.py:228
  136.7 12.4 %all_to_all.120.o1_ref = bf16[2,2,80,1024]{3,2,1,0:T(8,128)(2,1)} all-to-all(bf16[2,2,80,1024]{3,2,1,0:T(8,128)(2,1)} %attn_fwd_1_0.1), channel_id=1, replica_groups={{0,4},{8,12},{16,20},{24,28},{1,5},{9,13},{17,21},{25,29},{2,6},{10,14}..., dimensions={0} | all-to-all | bytes 1310720 | tf_op jit(solution)/shard_map/all_to_all | solution.py:897
  149.2 12.3 %all_to_all.121.x_ref = bf16[4,3,64,512]{3,2,1,0:T(8,128)(2,1)} all-to-all(bf16[4,3,64,512]{3,2,1,0:T(8,128)(2,1)S(1)} %copy-done.24), channel_id=1, replica_groups={{0,4,8,12},{16,20,24,28},{1,5,9,13},{17,21,25,29},{2,6,10,14},{18,22,26..., dimensions={0} | all-to-all | bytes 1572864 | tf_op jit(solution)/shard_map/all_to_all | solution.py:900
  188.5 14.3 %attn_fwd_0_0.1.o0_ref = bf16[4,3,80,512]{3,2,1,0:T(8,128)(2,1)} custom-call(bf16[4,3,192,512]{3,2,1,0:T(8,128)(2,1)} %all-to-all-done.x_ref.r_ref, s32[2,4]{1,0:T(2,128)} %len_ref.23), custom_call_target="tpu_custom_call" | custom-call | flops 15000000512 | bytes 3600000 | tf_op jit(solution)/shard_map/attn_fwd_0_0/pallas_call | solution.py:228
  205.9 14.9 %all-to-all-start.5 = ((bf16[4,192,512]{2,1,0:T(8,128)(2,1)}), bf16[4,192,512]{2,1,0:T(8,128)(2,1)S(1)}, u32[]{:S(2)}, u32[]{:S(2)}) async-start(bf16[4,192,512]{2,1,0:T(8,128)(2,1)} %get-tuple-element.60.att_ref), calls=%async_computation.5 | async-start | bytes 1572864 | tf_op jit(solution)/shard_map/all_to_all | solution.py:894
  220.8 14.3 %attn_fwd_0_1.1.o0_ref = bf16[4,3,80,512]{3,2,1,0:T(8,128)(2,1)} custom-call(bf16[4,3,192,512]{3,2,1,0:T(8,128)(2,1)} %copy-done.2, s32[2,4]{1,0:T(2,128)} %len_ref.23), custom_call_target="tpu_custom_call" | custom-call | flops 15000000512 | bytes 3600000 | tf_op jit(solution)/shard_map/attn_fwd_0_1/pallas_call | solution.py:228
  241.7 30.2 %ffn_0.1 = (bf16[512,768]{1,0:T(8,128)(2,1)}, f32[512,768]{1,0:T(8,128)}, bf16[4,192,512]{2,1,0:T(8,128)(2,1)}, bf16[512,768]{1,0:T(8,128)(2,1)}, bf16[512,768]{...) custom-call(bf16[4,192,512]{2,1,0:T(8,128)(2,1)} %copy-done.23, ...), custom_call_target="tpu_custom_call" | custom-call | flops 10871635968 | bytes 25000000 | tf_op jit(solution)/shard_map/ffn_0/pallas_call | solution.py:658
  272.8 30.6 %ffn_1.1 = (bf16[512,768]{1,0:T(8,128)(2,1)}, f32[512,768]{1,0:T(8,128)}, bf16[4,192,512]{2,1,0:T(8,128)(2,1)}, bf16[512,768]{1,0:T(8,128)(2,1)}, bf16[512,768]{...) custom-call(bf16[4,192,512]{2,1,0:T(8,128)(2,1)} %copy-done.22, ...), custom_call_target="tpu_custom_call" | custom-call | flops 10871635968 | bytes 25000000 | tf_op jit(solution)/shard_map/ffn_1/pallas_call | solution.py:658
  316.6 17.1 %weight_grads.1 = (bf16[3072,768]{1,0:T(8,128)(2,1)}, bf16[768,3072]{1,0:T(8,128)(2,1)}, bf16[768,768]{1,0:T(8,128)(2,1)}) custom-call(bf16[512,768]{1,0:T(8,128)(2,1)} %get-tuple-element.85.refs_0_, bf16[512,3072]{1,0:T(8,128)(2,1)} %get-tuple-element.86.refs_1_, bf16[512,3072]{1,0:T(8,128)(2,1)} %get-tuple-element.87.refs_2_, ...), custom_call_target="tpu_custom_call" | custom-call | flops 10871635968 | bytes 30000000 | tf_op jit(solution)/shard_map/weight_grads/pallas_call | solution.py:712
  394.3 16.3 %attn_bwd_1_0.1 = bf16[2,2,3,64,1024]{4,3,2,1,0:T(8,128)(2,1)} custom-call(bf16[2,2,3,64,1024]{4,3,2,1,0:T(8,128)(2,1)} %copy-done.14, bf16[2,2,80,1024]{3,2,1,0:T(8,128)(2,1)} %copy-done.25, s32[2,4]{1,0:T(2,128)} %len_ref.23), custom_call_target="tpu_custom_call" | custom-call | flops 16000000000 | bytes 4000000 | tf_op jit(solution)/shard_map/attn_bwd_1_0/pallas_call | solution.py:247
  414.3 16.4 %attn_bwd_1_1.1 = bf16[2,2,3,64,1024]{4,3,2,1,0:T(8,128)(2,1)} custom-call(bf16[2,2,3,64,1024]{4,3,2,1,0:T(8,128)(2,1)} %copy-done.13, bf16[2,2,80,1024]{3,2,1,0:T(8,128)(2,1)} %copy-done.26, s32[2,4]{1,0:T(2,128)} %len_ref.23), custom_call_target="tpu_custom_call" | custom-call | flops 16000000000 | bytes 4000000 | tf_op jit(solution)/shard_map/attn_bwd_1_1/pallas_call | solution.py:247
  438.5 9.0 %attn_bwd_2_0.1 = bf16[4,3,64,512]{3,2,1,0:T(8,128)(2,1)} custom-call(bf16[4,3,64,512]{3,2,1,0:T(8,128)(2,1)} %all_to_all.121.x_ref, bf16[4,80,512]{2,1,0:T(8,128)(2,1)} %copy-done.27, s32[2,4]{1,0:T(2,128)} %len_ref.23), custom_call_target="tpu_custom_call" | custom-call | flops 8000000000 | bytes 2000000 | tf_op jit(solution)/shard_map/attn_bwd_2_0/pallas_call | solution.py:247
  473.2 23.4 %attn_bwd_0_0.1.d0_ref = bf16[4,3,192,512]{3,2,1,0:T(8,128)(2,1)} custom-call(bf16[4,3,192,512]{3,2,1,0:T(8,128)(2,1)} %all-to-all-done.x_ref.r_ref, bf16[4,3,80,512]{3,2,1,0:T(8,128)(2,1)} %get-tuple-element.71.g_ref, s32[2,4]{1,0:T(2,128)} %len_ref.23), custom_call_target="tpu_custom_call" | custom-call | flops 24000000000 | bytes 6000000 | tf_op jit(solution)/shard_map/attn_bwd_0_0/pallas_call | solution.py:247
  508.4 23.4 %attn_bwd_0_1.1.d0_ref = bf16[4,3,192,512]{3,2,1,0:T(8,128)(2,1)} custom-call(bf16[4,3,192,512]{3,2,1,0:T(8,128)(2,1)} %copy-done.2, bf16[4,3,80,512]{3,2,1,0:T(8,128)(2,1)} %get-tuple-element.78.g_ref, s32[2,4]{1,0:T(2,128)} %len_ref.23), custom_call_target="tpu_custom_call" | custom-call | flops 24000000000 | bytes 6000000 | tf_op jit(solution)/shard_map/attn_bwd_0_1/pallas_call | solution.py:247
  585.1 12.4 %collective-permute-done.22 = bf16[2,2,2,96,768]{4,3,2,1,0:T(8,128)(2,1)} collective-permute-done((bf16[2,2,2,96,768]{4,3,2,1,0:T(8,128)(2,1)S(1)}, bf16[2,2,2,96,768]{4,3,2,1,0:T(8,128)(2,1)}, u32[]{:S(2)}, u32[]{:S(2)}) %collective-permute-start.22) | collective-permute-done | bytes 1179680 | tf_op jit(solution)/shard_map/ppermute | solution.py:829
  607.3 9.1 %collective-permute-done.30 = f32[2,2,24,6]{2,1,3,0:T(2,128)S(1)} collective-permute-done((f32[2,2,24,6]{2,1,3,0:T(2,128)S(1)}, f32[2,2,24,6]{2,1,3,0:T(2,128)S(1)}, u32[]{:S(2)}, u32[]{:S(2)}) %collective-permute-start.30) | collective-permute-done | bytes 2336 | tf_op jit(solution)/shard_map/ppermute | solution.py:829
  646.3 9.1 %collective-permute-done.24 = bf16[2,96,768]{2,1,0:T(8,128)(2,1)S(1)} collective-permute-done((bf16[2,96,768]{2,1,0:T(8,128)(2,1)S(1)}, bf16[2,96,768]{2,1,0:T(8,128)(2,1)S(1)}, u32[]{:S(2)}, u32[]{:S(2)}) %collective-permute-start.24) | collective-permute-done | bytes 294944 | tf_op jit(solution)/shard_map/ppermute | solution.py:829
  655.6 10.5 %collective-permute-done.17 = bf16[2,24,3072]{2,1,0:T(8,128)(2,1)S(1)} collective-permute-done((bf16[2,24,3072]{2,1,0:T(8,128)(2,1)S(1)}, bf16[2,24,3072]{2,1,0:T(8,128)(2,1)S(1)}, u32[]{:S(2)}, u32[]{:S(2)}) %collective-permute-start.17) | collective-permute-done | bytes 294944 | tf_op jit(solution)/shard_map/ppermute | solution.py:829
  673.1 15.9 %collective-permute-done.1 = bf16[2,2,2,24,2304]{4,3,2,1,0:T(8,128)(2,1)S(1)} collective-permute-done((bf16[2,2,2,24,2304]{4,3,2,1,0:T(8,128)(2,1)S(1)}, bf16[2,2,2,24,2304]{4,3,2,1,0:T(8,128)(2,1)S(1)}, u32[]{:S(2)}, u32[]{:S(2)}) %collective-permute-start.1) | collective-permute-done | bytes 884768 | tf_op jit(solution)/shard_map/ppermute | solution.py:829
  (314 shorter events, 337.9 us)
Async XLA Ops:
  10.5 32.7 %all-to-all-start.6 = ((bf16[4,3,192,512]{3,2,1,0:T(8,128)(2,1)}), bf16[4,3,192,512]{3,2,1,0:T(8,128)(2,1)S(1)}, u32[]{:S(2)}, u32[]{:S(2)}) async-start(bf16[4,3,192,512]{3,2,1,0:T(8,128)(2,1)} %get-tuple-element.63), calls=%async_computation.6 | async-start | bytes 4718592 | tf_op jit(solution)/shard_map/all_to_all | solution.py:894
  44.7 33.1 %all-to-all-start = ((bf16[4,3,192,512]{3,2,1,0:T(8,128)(2,1)}), bf16[4,3,192,512]{3,2,1,0:T(8,128)(2,1)}, u32[]{:S(2)}, u32[]{:S(2)}) async-start(bf16[4,3,192,512]{3,2,1,0:T(8,128)(2,1)} %get-tuple-element.57), calls=%async_computation | async-start | bytes 4718592 | tf_op jit(solution)/shard_map/all_to_all | solution.py:894
  77.7 23.5 %all-to-all-start.7 = ((bf16[2,2,3,64,1024]{4,3,2,1,0:T(8,128)(2,1)}), bf16[2,2,3,64,1024]{4,3,2,1,0:T(8,128)(2,1)S(1)}, u32[]{:S(2)}, u32[]{:S(2)}) async-start(bf16[2,2,3,64,1024]{4,3,2,1,0:T(8,128)(2,1)} %get-tuple-element.64), calls=%async_computation.7 | async-start | bytes 3145728 | tf_op jit(solution)/shard_map/all_to_all | solution.py:897
  101.3 22.4 %all-to-all-start.1 = ((bf16[2,2,3,64,1024]{4,3,2,1,0:T(8,128)(2,1)}), bf16[2,2,3,64,1024]{4,3,2,1,0:T(8,128)(2,1)S(1)}, u32[]{:S(2)}, u32[]{:S(2)}) async-start(bf16[2,2,3,64,1024]{4,3,2,1,0:T(8,128)(2,1)} %get-tuple-element.58), calls=%async_computation.1 | async-start | bytes 3145728 | tf_op jit(solution)/shard_map/all_to_all | solution.py:897
  205.9 32.3 %all-to-all-start.5 = ((bf16[4,192,512]{2,1,0:T(8,128)(2,1)}), bf16[4,192,512]{2,1,0:T(8,128)(2,1)S(1)}, u32[]{:S(2)}, u32[]{:S(2)}) async-start(bf16[4,192,512]{2,1,0:T(8,128)(2,1)} %get-tuple-element.60.att_ref), calls=%async_computation.5 | async-start | bytes 1572864 | tf_op jit(solution)/shard_map/all_to_all | solution.py:894
  238.2 33.7 %all-to-all-start.11 = ((bf16[4,192,512]{2,1,0:T(8,128)(2,1)}), bf16[4,192,512]{2,1,0:T(8,128)(2,1)S(1)}, u32[]{:S(2)}, u32[]{:S(2)}) async-start(bf16[4,192,512]{2,1,0:T(8,128)(2,1)} %get-tuple-element.66.att_ref), calls=%async_computation.11 | async-start | bytes 1572864 | tf_op jit(solution)/shard_map/all_to_all | solution.py:894
  311.5 26.1 %all-to-all-start.12 = ((bf16[4,192,512]{2,1,0:T(8,128)(2,1)}), bf16[4,192,512]{2,1,0:T(8,128)(2,1)S(1)}, u32[]{:S(2)}, u32[]{:S(2)}) async-start(bf16[4,192,512]{2,1,0:T(8,128)(2,1)} %get-tuple-element.69), calls=%async_computation.12 | async-start | bytes 1572864 | tf_op jit(solution)/shard_map/all_to_all | solution.py:894
  337.6 21.9 %collective-permute-start.7 = (bf16[2,2,2,2,24,768]{5,4,3,2,1,0:T(8,128)(2,1)}, bf16[2,2,2,2,24,768]{5,4,3,2,1,0:T(8,128)(2,1)}, u32[]{:S(2)}, u32[]{:S(2)}) collective-permute-start(bf16[2,2,2,2,24,768]{5,4,3,2,1,0:T(8,128)(2,1)} %dynamic-slice_bitcast_fusion.8), channel_id=1, source_target_pairs={{0,1},{1,0},{2,3},{3,2},{4,5},{5,4},{6,7},{7,6},{8,9},{9,8},{10,11... | collective-permute-start | bytes 1769480 | tf_op jit(solution)/shard_map/ppermute | solution.py:829
  387.3 156.3 %collective-permute-start.21 = (bf16[2,2,2,2,96,768]{5,4,3,2,1,0:T(8,128)(2,1)}, bf16[2,2,2,2,96,768]{5,4,3,2,1,0:T(8,128)(2,1)}, u32[]{:S(2)}, u32[]{:S(2)}) collective-permute-start(bf16[2,2,2,2,96,768]{5,4,3,2,1,0:T(8,128)(2,1)} %dynamic-slice_bitcast_fusion), channel_id=1, source_target_pairs={{0,1},{1,0},{2,3},{3,2},{4,5},{5,4},{6,7},{7,6},{8,9},{9,8},{10,11... | collective-permute-start | bytes 7077896 | tf_op jit(solution)/shard_map/ppermute | solution.py:829
  387.3 161.5 %collective-permute-start.14 = (bf16[2,2,2,2,24,3072]{5,4,3,2,1,0:T(8,128)(2,1)}, bf16[2,2,2,2,24,3072]{5,4,3,2,1,0:T(8,128)(2,1)}, u32[]{:S(2)}, u32[]{:S(2)}) collective-permute-start(bf16[2,2,2,2,24,3072]{5,4,3,2,1,0:T(8,128)(2,1)} %dynamic-slice_bitcast_fusion.1), channel_id=1, source_target_pairs={{0,1},{1,0},{2,3},{3,2},{4,5},{5,4},{6,7},{7,6},{8,9},{9,8},{10,11... | collective-permute-start | bytes 7077896 | tf_op jit(solution)/shard_map/ppermute | solution.py:829
  388.7 42.0 %collective-permute-start.9 = (bf16[2,2,24,768]{3,2,1,0:T(8,128)(2,1)S(1)}, bf16[2,2,24,768]{3,2,1,0:T(8,128)(2,1)S(1)}, u32[]{:S(2)}, u32[]{:S(2)}) collective-permute-start(bf16[2,2,24,768]{3,2,1,0:T(8,128)(2,1)S(1)} %dynamic-slice_bitcast_fusion.16), channel_id=1, source_target_pairs={{0,8},{4,12},{8,0},{12,4},{16,24},{20,28},{24,16},{28,20},{1,9},{5... | collective-permute-start | bytes 442376 | tf_op jit(solution)/shard_map/ppermute | solution.py:829
  410.6 23.1 %all-to-all-start.14 = ((bf16[2,2,3,64,1024]{4,3,2,1,0:T(8,128)(2,1)}), bf16[2,2,3,64,1024]{4,3,2,1,0:T(8,128)(2,1)S(1)}, u32[]{:S(2)}, u32[]{:S(2)}) async-start(bf16[2,2,3,64,1024]{4,3,2,1,0:T(8,128)(2,1)} %attn_bwd_1_0.1), calls=%async_computation.14 | async-start | bytes 3145728 | tf_op jit(solution)/shard_map/all_to_all | solution.py:897
  433.7 22.2 %all-to-all-start.20 = ((bf16[2,2,3,64,1024]{4,3,2,1,0:T(8,128)(2,1)}), bf16[2,2,3,64,1024]{4,3,2,1,0:T(8,128)(2,1)S(1)}, u32[]{:S(2)}, u32[]{:S(2)}) async-start(bf16[2,2,3,64,1024]{4,3,2,1,0:T(8,128)(2,1)} %attn_bwd_1_1.1), calls=%async_computation.20 | async-start | bytes 3145728 | tf_op jit(solution)/shard_map/all_to_all | solution.py:897
  437.4 22.2 %collective-permute-start.10 = (bf16[2,24,768]{2,1,0:T(8,128)(2,1)S(1)}, bf16[2,24,768]{2,1,0:T(8,128)(2,1)S(1)}, u32[]{:S(2)}, u32[]{:S(2)}) collective-permute-start(bf16[2,24,768]{2,1,0:T(8,128)(2,1)S(1)} %dynamic-slice_bitcast_fusion.18), channel_id=1, source_target_pairs={{0,16},{4,20},{8,24},{12,28},{16,0},{20,4},{24,8},{28,12},{1,17},{... | collective-permute-start | bytes 221192 | tf_op jit(solution)/shard_map/ppermute | solution.py:829
  468.9 27.6 %collective-permute-start.12 = (bf16[24,768]{1,0:T(8,128)(2,1)S(1)}, bf16[24,768]{1,0:T(8,128)(2,1)S(1)}, u32[]{:S(2)}, u32[]{:S(2)}) collective-permute-start(bf16[24,768]{1,0:T(8,128)(2,1)S(1)} %fusion.19), channel_id=1, source_target_pairs={{0,1},{1,0},{2,3},{3,2},{4,5},{5,4},{6,7},{7,6},{8,9},{9,8},{10,11... | collective-permute-start | bytes 110600 | tf_op jit(solution)/shard_map/ppermute | solution.py:829
  469.0 34.5 %all-to-all-start.22 = ((bf16[4,3,64,512]{3,2,1,0:T(8,128)(2,1)}), bf16[4,3,64,512]{3,2,1,0:T(8,128)(2,1)S(1)}, u32[]{:S(2)}, u32[]{:S(2)}) async-start(bf16[4,3,64,512]{3,2,1,0:T(8,128)(2,1)} %attn_bwd_2_1.1), calls=%async_computation.22 | async-start | bytes 1572864 | tf_op jit(solution)/shard_map/all_to_all | solution.py:900
  496.5 35.2 %collective-permute-start.13 = (bf16[48,768]{1,0:T(8,128)(2,1)S(1)}, bf16[48,768]{1,0:T(8,128)(2,1)S(1)}, u32[]{:S(2)}, u32[]{:S(2)}) collective-permute-start(bf16[48,768]{1,0:T(8,128)(2,1)S(1)} %bitcast.254), channel_id=1, source_target_pairs={{0,2},{1,3},{2,0},{3,1},{4,6},{5,7},{6,4},{7,5},{8,10},{9,11},{10,... | collective-permute-start | bytes 221192 | tf_op jit(solution)/shard_map/ppermute | solution.py:829
  504.3 33.2 %all-to-all-start.17 = ((bf16[4,3,192,512]{3,2,1,0:T(8,128)(2,1)}), bf16[4,3,192,512]{3,2,1,0:T(8,128)(2,1)S(1)}, u32[]{:S(2)}, u32[]{:S(2)}) async-start(bf16[4,3,192,512]{3,2,1,0:T(8,128)(2,1)} %sum_grad_0.1), calls=%async_computation.17 | async-start | bytes 4718592 | tf_op jit(solution)/shard_map/all_to_all | solution.py:894
  539.0 33.7 %all-to-all-start.23 = ((bf16[4,3,192,512]{3,2,1,0:T(8,128)(2,1)}), bf16[4,3,192,512]{3,2,1,0:T(8,128)(2,1)}, u32[]{:S(2)}, u32[]{:S(2)}) async-start(bf16[4,3,192,512]{3,2,1,0:T(8,128)(2,1)} %sum_grad_1.1), calls=%async_computation.23 | async-start | bytes 4718592 | tf_op jit(solution)/shard_map/all_to_all | solution.py:894
  546.8 50.7 %collective-permute-start.22 = (bf16[2,2,2,96,768]{4,3,2,1,0:T(8,128)(2,1)S(1)}, bf16[2,2,2,96,768]{4,3,2,1,0:T(8,128)(2,1)}, u32[]{:S(2)}, u32[]{:S(2)}) collective-permute-start(bf16[2,2,2,96,768]{4,3,2,1,0:T(8,128)(2,1)S(1)} %dynamic-slice_bitcast_fusion.3), channel_id=1, source_target_pairs={{0,2},{1,3},{2,0},{3,1},{4,6},{5,7},{6,4},{7,5},{8,10},{9,11},{10,... | collective-permute-start | bytes 3538952 | tf_op jit(solution)/shard_map/ppermute | solution.py:829
  553.4 52.2 %collective-permute-start.15 = (bf16[2,2,2,24,3072]{4,3,2,1,0:T(8,128)(2,1)}, bf16[2,2,2,24,3072]{4,3,2,1,0:T(8,128)(2,1)}, u32[]{:S(2)}, u32[]{:S(2)}) collective-permute-start(bf16[2,2,2,24,3072]{4,3,2,1,0:T(8,128)(2,1)} %dynamic-slice_bitcast_fusion.4), channel_id=1, source_target_pairs={{0,4},{4,0},{8,12},{12,8},{16,20},{20,16},{24,28},{28,24},{1,5},{5... | collective-permute-start | bytes 3538952 | tf_op jit(solution)/shard_map/ppermute | solution.py:829
  600.8 39.4 %collective-permute-start.23 = (bf16[2,2,96,768]{3,2,1,0:T(8,128)(2,1)}, bf16[2,2,96,768]{3,2,1,0:T(8,128)(2,1)}, u32[]{:S(2)}, u32[]{:S(2)}) collective-permute-start(bf16[2,2,96,768]{3,2,1,0:T(8,128)(2,1)} %dynamic-slice_bitcast_fusion.6), channel_id=1, source_target_pairs={{0,4},{4,0},{8,12},{12,8},{16,20},{20,16},{24,28},{28,24},{1,5},{5... | collective-permute-start | bytes 1769480 | tf_op jit(solution)/shard_map/ppermute | solution.py:829
  619.1 25.2 %collective-permute-start.16 = (bf16[2,2,24,3072]{3,2,1,0:T(8,128)(2,1)}, bf16[2,2,24,3072]{3,2,1,0:T(8,128)(2,1)}, u32[]{:S(2)}, u32[]{:S(2)}) collective-permute-start(bf16[2,2,24,3072]{3,2,1,0:T(8,128)(2,1)} %dynamic-slice_bitcast_fusion.7), channel_id=1, source_target_pairs={{0,8},{4,12},{8,0},{12,4},{16,24},{20,28},{24,16},{28,20},{1,9},{5... | collective-permute-start | bytes 1769480 | tf_op jit(solution)/shard_map/ppermute | solution.py:829
  634.4 32.6 %collective-permute-start = (bf16[2,2,2,2,24,2304]{5,4,3,2,1,0:T(8,128)(2,1)}, bf16[2,2,2,2,24,2304]{5,4,3,2,1,0:T(8,128)(2,1)}, u32[]{:S(2)}, u32[]{:S(2)}) collective-permute-start(bf16[2,2,2,2,24,2304]{5,4,3,2,1,0:T(8,128)(2,1)} %dynamic-slice_bitcast_fusion.2), channel_id=1, source_target_pairs={{0,1},{1,0},{2,3},{3,2},{4,5},{5,4},{6,7},{7,6},{8,9},{9,8},{10,11... | collective-permute-start | bytes 5308424 | tf_op jit(solution)/shard_map/ppermute | solution.py:829
  (77 other events, 878.3 us)

commit v2 on v1

--- a/solution.py
+++ b/solution.py
@@ -824,6 +824,452 @@
     )(tg, weight, xp, branch, gain)
 
 
+def rep_peer(k):
+    count = lax.axis_size("rep")
+    return (lax.axis_index("rep") + k) % count
+
+
+def team_place():
+    return lax.axis_index("seq") % 4
+
+
+def team_member(k):
+    s = lax.axis_index("seq")
+    return s // 4 * 4 + (s + k) % 4
+
+
+def pair_partner():
+    s = lax.axis_index("seq")
+    return s + 1 - 2 * (s % 2)
+
+
+def remote(src, dst, send_sem, recv_sem, axis, peer):
+    return pltpu.make_async_remote_copy(
+        src_ref=src,
+        dst_ref=dst,
+        send_sem=send_sem,
+        recv_sem=recv_sem,
+        device_id={axis: peer},
+        device_id_type=pl.DeviceIdType.MESH,
+    )
+
+
+def meet_peers():
+    barrier = pltpu.get_barrier_semaphore()
+    for k in range(1, 4):
+        for axis, peer in (("rep", rep_peer(k)), ("seq", team_member(k))):
+            pl.semaphore_signal(
+                barrier, inc=1, device_id={axis: peer}, device_id_type=pl.DeviceIdType.MESH
+            )
+    pl.semaphore_wait(barrier, 6)
+
+
+def head_rows(j):
+    return pl.ds(pl.multiple_of(j * HD, HD), HD)
+
+
+def attend(block, doc, put, ks, qs, pattern, count, lanes):
+    kb = min(512, lanes)
+    for s in range(0, count, kb):
+        sl = slice(s, s + kb)
+        r = lax.broadcasted_iota(jnp.int32, (HD, kb), 0)
+        same = doc[:, sl] == r
+        aux_k = jnp.where(same, 1.0, 0.0).astype(bf16)
+        aux_q = jnp.where(same | (r >= 4), 0.0, NEG).astype(bf16)
+        q = (block(0, s, kb).astype(f32) * 0.125).astype(bf16)
+        qs[:, sl] = jnp.concatenate([q, aux_q], 0)
+        ks[sl, :] = jnp.concatenate([block(1, s, kb), aux_k], 0).T
+
+    qb = 256
+    grain = 512 if pattern == 0 else 256
+
+    def tiles(i):
+        low = (i * qb) // grain * grain
+        out = [(s, min(512, low - s), False) for s in range(0, low, 512)]
+        return out + [(low, grain, True)]
+
+    def scores(i):
+        out = []
+        for s, size, diagonal in tiles(i):
+            t = dot_nn(ks[s : s + size, :], qs[:, i * qb : (i + 1) * qb])
+            if diagonal:
+                keep = rel_pos((size, qb), 0, s % 512, pattern) <= rel_pos(
+                    (size, qb), 1, (i * qb) % 512, pattern
+                )
+                t = jnp.where(keep, t, NEG)
+            out.append(t)
+        return out
+
+    following = scores(0)
+    for i in range(count // qb):
+        current = following
+        if (i + 1) * qb < count:
+            following = scores(i + 1)
+        top = functools.reduce(jnp.maximum, [jnp.max(t, 0, keepdims=True) for t in current])
+        top2 = top * LOG2E
+        acc, total = None, None
+        for t, (s, size, _) in zip(current, tiles(i)):
+            p = jnp.exp2(t * LOG2E - top2)
+            part = jnp.sum(p, 0, keepdims=True)
+            out = dot_nn(block(2, s, size), p.astype(bf16))
+            acc = out if acc is None else acc + out
+            total = part if total is None else total + part
+        lse = top + jnp.log(total)
+        put(i * qb, qb, (acc / total).astype(bf16), stat_rows(split3(lse), qb))
+
+
+def forward_body(
+    x_ref,
+    w_ref,
+    gain_ref,
+    bias_ref,
+    len_ref,
+    xp_ref,
+    nt_ref,
+    r_out,
+    p1_out,
+    p2_out,
+    att_ref,
+    got_ref,
+    mix_ref,
+    sent,
+    r,
+    stage1,
+    stage2,
+    p1,
+    p2,
+    o0,
+    o1,
+    o2,
+    b1,
+    b2,
+    ks,
+    qs,
+    qkv_sems,
+    p1_sems,
+    p2_sems,
+    b1_sems,
+    b2_sems,
+    att_sems,
+    out_sems,
+):
+    micros, tok, width = x_ref.shape
+    reps = r.shape[1]
+    span = tok * reps
+    cols = width // reps
+    me = lax.axis_index("rep")
+    place = team_place()
+    side = place % 2
+    meet_peers()
+
+    def qkv_copy(m, j, k, source):
+        return remote(
+            sent.at[m, rep_peer(k), :, head_rows(j)],
+            r.at[m, source, :, head_rows(j)],
+            qkv_sems.at[0, m, j, k - 1],
+            qkv_sems.at[1, m, j, k - 1],
+            "rep",
+            rep_peer(k),
+        )
+
+    def p1_copy(m, s, source):
+        return remote(
+            stage1.at[m, s],
+            p1.at[m, source, s],
+            p1_sems.at[0, m, s],
+            p1_sems.at[1, m, s],
+            "seq",
+            pair_partner(),
+        )
+
+    def p2_copy(m, k, source):
+        return remote(
+            stage2.at[m, (place + k) % 4],
+            p2.at[m, source],
+            p2_sems.at[0, m, k - 1],
+            p2_sems.at[1, m, k - 1],
+            "seq",
+            team_member(k),
+        )
+
+    def b1_copy(m, s, source):
+        return remote(
+            o1.at[m, s, 1 - side],
+            b1.at[m, source, s],
+            b1_sems.at[0, m, s],
+            b1_sems.at[1, m, s],
+            "seq",
+            pair_partner(),
+        )
+
+    def b2_copy(m, k, source):
+        return remote(
+            o2.at[m, (place + k) % 4],
+            b2.at[m, source],
+            b2_sems.at[0, m, k - 1],
+            b2_sems.at[1, m, k - 1],
+            "seq",
+            team_member(k),
+        )
+
+    def att_copy(k, source):
+        return remote(
+            att_ref.at[0, rep_peer(k)],
+            got_ref.at[source],
+            att_sems.at[0, k - 1],
+            att_sems.at[1, k - 1],
+            "rep",
+            rep_peer(k),
+        )
+
+    def out_copies(m):
+        return (
+            pltpu.make_async_copy(r.at[m], r_out.at[m], out_sems.at[m, 0]),
+            pltpu.make_async_copy(p1.at[m], p1_out.at[m], out_sems.at[m, 1]),
+            pltpu.make_async_copy(p2.at[m], p2_out.at[m], out_sems.at[m, 2]),
+        )
+
+    def project(m, carry):
+        xp = dot_nn(onehot_rows(tok), x_ref[m])
+        xp_ref[m] = xp.astype(bf16)
+        xhat, _ = normalize(xp)
+        n = (xhat * gain_ref[...] + bias_ref[...]).astype(bf16)
+        nt_ref[m] = n.T
+        for c in range(3):
+            t = dot_nn(n, w_ref[:, c * width : (c + 1) * width]).astype(bf16).T
+            for d in range(reps):
+                sent[m, d, c] = t[d * cols : (d + 1) * cols]
+        for j in range(3):
+            for k in range(1, 4):
+                qkv_copy(m, j, k, me).start()
+        r[m, me] = sent[m, me]
+        return carry
+
+    lax.fori_loop(0, micros, project, 0)
+
+    def half(j):
+        return pl.ds(pl.multiple_of(((3 * me + j) % 2) * 256, 256), 256)
+
+    def quarter_at(j):
+        c = (3 * me + j) % 4
+        return c % 2 * 2 + c // 2
+
+    def quarter(j):
+        return pl.ds(pl.multiple_of(quarter_at(j) * 128, 128), 128)
+
+    def send_first(m):
+        for b in range(reps):
+            bl = slice(b * 256, (b + 1) * 256)
+            stage1[m, 0, :, :, bl] = r[m, b, :, head_rows(1 - side), half(1 - side)]
+            p1[m, side, 0, :, :, bl] = r[m, b, :, head_rows(side), half(side)]
+        p1_copy(m, 0, side).start()
+
+    def send_second(m):
+        for b in range(reps):
+            bl = slice(b * 256, (b + 1) * 256)
+            piece = r[m, b, :, head_rows(2), half(2)]
+            stage1[m, 1, :, :, bl] = piece
+            p1[m, side, 1, :, :, bl] = piece
+        p1_copy(m, 1, side).start()
+        for g in range(4):
+            j = min(g, 2)
+            for b in range(reps):
+                stage2[m, g, :, :, b * 128 : (b + 1) * 128] = r[m, b, :, head_rows(j), quarter(j)]
+        p2[m, place] = stage2[m, place]
+        for k in range(1, 4):
+            p2_copy(m, k, place).start()
+
+    def mix_all(m):
+        for s in range(2):
+            b1_copy(m, s, 1 - side).wait_recv()
+        for k in range(1, 4):
+            b2_copy(m, k, (place + 4 - k) % 4).wait_recv()
+
+        def stat(tile):
+            t = tile[HD:, :].astype(f32)
+            return t[0:1] + t[1:2] + t[2:3]
+
+        mix_ref[m] = jnp.zeros(mix_ref.shape[1:], f32)
+        for j in range(3):
+            e, s = PLACE1[j]
+            for b in range(reps):
+                for a in range(4):
+                    la = slice(a * 128, (a + 1) * 128)
+                    lb = b * 256 + (a % 2) * 128
+                    t0 = o0[m, j, b, :, la]
+                    t1 = b1[m, e, s, :, lb : lb + 128]
+                    t2 = b2[m, j, :, b * 128 : (b + 1) * 128]
+                    l0 = stat(t0)
+                    l1 = jnp.where((3 * me + j) % 2 == a // 2, stat(t1), NEG)
+                    l2 = jnp.where(quarter_at(j) == a, stat(t2), NEG)
+                    top = jnp.maximum(jnp.maximum(l0, l1), l2)
+                    e0, e1, e2 = jnp.exp(l0 - top), jnp.exp(l1 - top), jnp.exp(l2 - top)
+                    total = e0 + e1 + e2
+                    inv = 1.0 / total
+                    mixed = (
+                        t0[:HD].astype(f32) * (e0 * inv)
+                        + t1[:HD].astype(f32) * (e1 * inv)
+                        + t2[:HD].astype(f32) * (e2 * inv)
+                    )
+                    att_ref[m, b, j * HD : (j + 1) * HD, la] = mixed.astype(bf16)
+                    col = b * tok + a * 128
+                    mix_ref[m, j : j + 1, col : col + 128] = top + jnp.log(total)
+
+    docs_of = lambda m, pattern: doc_rows(
+        len_ref, m, segment_start(pattern, span), 2**pattern, span
+    )
+
+    def micro(m, carry):
+        def local(j, inner):
+            for k in range(1, 4):
+                qkv_copy(m, j, k, (me + reps - k) % reps).wait_recv()
+
+            @pl.when(j == 1)
+            def _():
+                send_first(m)
+
+            @pl.when(j == 2)
+            def _():
+                send_second(m)
+
+            def block(c, start, size):
+                at = start % tok
+                return r[m, start // tok, c, head_rows(j), at : at + size]
+
+            def put(start, size, out, stats):
+                at = start % tok
+                o0[m, j, start // tok, :HD, at : at + size] = out
+                o0[m, j, start // tok, HD:, at : at + size] = stats
+
+            attend(block, docs_of(m, 0), put, ks, qs, 0, span, tok)
+            return inner
+
+        lax.fori_loop(0, 3, local, 0)
+
+        @pl.when(m == 1)
+        def _():
+            mix_all(0)
+            for k in range(1, 4):
+                att_copy(k, me).start()
+            got_ref[me] = att_ref[0, me]
+
+        def paired(s, inner):
+            p1_copy(m, s, 1 - side).wait_recv()
+            wide = span // 2
+
+            def block(c, start, size):
+                at = start % wide
+                return p1[m, start // wide, s, c, :, at : at + size]
+
+            def put(start, size, out, stats):
+                at = start % wide
+                o1[m, s, start // wide, :HD, at : at + size] = out
+                o1[m, s, start // wide, HD:, at : at + size] = stats
+
+            attend(block, docs_of(m, 1), put, ks, qs, 1, span, wide)
+            b1[m, side, s] = o1[m, s, side]
+            b1_copy(m, s, side).start()
+            return inner
+
+        lax.fori_loop(0, 2, paired, 0)
+        for k in range(1, 4):
+            p2_copy(m, k, (place + 4 - k) % 4).wait_recv()
+
+        def block(c, start, size):
+            at = start % tok
+            return p2[m, start // tok, c, :, at : at + size]
+
+        def put(start, size, out, stats):
+            at = start % tok
+            o2[m, start // tok, :HD, at : at + size] = out
+            o2[m, start // tok, HD:, at : at + size] = stats
+
+        attend(block, docs_of(m, 2), put, ks, qs, 2, span, tok)
+        b2[m, place] = o2[m, place]
+        for k in range(1, 4):
+            b2_copy(m, k, place).start()
+        for c in out_copies(m):
+            c.start()
+        return carry
+
+    lax.fori_loop(0, micros, micro, 0)
+    mix_all(1)
+    for k in range(1, 4):
+        att_copy(k, (me + reps - k) % reps).wait_recv()
+        att_copy(k, me).wait_send()
+
+    def finish(m, carry):
+        for c in out_copies(m):
+            c.wait()
+        for k in range(1, 4):
+            for j in range(3):
+                qkv_copy(m, j, k, me).wait_send()
+            p2_copy(m, k, place).wait_send()
+            b2_copy(m, k, place).wait_send()
+        for s in range(2):
+            p1_copy(m, s, side).wait_send()
+            b1_copy(m, s, side).wait_send()
+        return carry
+
+    lax.fori_loop(0, micros, finish, 0)
+
+
+def forward_call(layer_in, weight, gain, bias, lengths, reps):
+    micros, tok, width = layer_in.shape
+    span, cols = tok * reps, width // reps
+    any_spec = pl.BlockSpec(memory_space=pl.ANY)
+    outs = [
+        ((micros, tok, width), bf16, vmem_spec()),
+        ((micros, width, tok), bf16, vmem_spec()),
+        ((micros, reps, 3, cols, tok), bf16, any_spec),
+        ((micros, 2, 2, 3, HD, span // 2), bf16, any_spec),
+        ((micros, 4, 3, HD, span // 4), bf16, any_spec),
+        ((micros, reps, cols, tok), bf16, vmem_spec()),
+        ((reps, cols, tok), bf16, vmem_spec()),
+        ((micros, 8, span), f32, vmem_spec()),
+    ]
+
+    def vm(*shape):
+        return pltpu.VMEM(shape, bf16)
+
+    dma = pltpu.SemaphoreType.DMA
+    return pl.pallas_call(
+        forward_body,
+        in_specs=[vmem_spec()] * 4 + [smem_spec()],
+        out_specs=[o[2] for o in outs],
+        out_shape=[jax.ShapeDtypeStruct(o[0], o[1]) for o in outs],
+        scratch_shapes=[
+            vm(micros, reps, 3, cols, tok),
+            vm(micros, reps, 3, cols, tok),
+            vm(micros, 2, 3, HD, span // 2),
+            vm(micros, 4, 3, HD, span // 4),
+            vm(micros, 2, 2, 3, HD, span // 2),
+            vm(micros, 4, 3, HD, span // 4),
+            vm(micros, 3, reps, HPAD, tok),
+            vm(micros, 2, 2, HPAD, span // 2),
+            vm(micros, 4, HPAD, span // 4),
+            vm(micros, 2, 2, HPAD, span // 2),
+            vm(micros, 4, HPAD, span // 4),
+            vm(span, 128),
+            vm(128, span),
+            dma((2, micros, 3, 3)),
+            dma((2, micros, 2)),
+            dma((2, micros, 3)),
+            dma((2, micros, 2)),
+            dma((2, micros, 3)),
+            dma((2, 3)),
+            dma((micros, 3)),
+        ],
+        compiler_params=pltpu.CompilerParams(
+            vmem_limit_bytes=VMEM, collective_id=1, has_side_effects=True
+        ),
+        cost_estimate=pl.CostEstimate(
+            flops=60_000_000_000, bytes_accessed=30_000_000, transcendentals=30_000_000
+        ),
+        name="forward",
+    )(layer_in, weight, gain, bias, lengths)
+
+
 def swap(block, axis, bit):
     count = lax.axis_size(axis)
     return lax.ppermute(block, axis, [(n, n ^ (1 << bit)) for n in range(count)])
@@ -903,25 +1349,13 @@
         return v.reshape(1, -1)
 
     micros = range(micro_count)
-    residual, normed, got_qkv = [], [], []
-    for m in micros:
-        sent, xp, nt = qkv_call(layer_in, qkv_weight, row(input_gain), row(input_bias), m, reps)
-        residual.append(xp)
-        normed.append(nt)
-        got_qkv.append(to_reps(sent))
-
-    pieces, attended, own_att, totals = [], [], [], []
-    for m in micros:
-        p1, p2 = pack_qkv(got_qkv[m], span, reps, m)
-        p1, p2 = to_pair(p1), to_four(p2)
-        pieces.append((got_qkv[m], p1, p2))
-        o0 = attn_fwd(got_qkv[m], seq_lengths, 0, m, span, reps)
-        o1 = to_pair(attn_fwd(p1, seq_lengths, 1, m, span, reps))
-        o2 = to_four(attn_fwd(p2, seq_lengths, 2, m, span, reps))
-        att, total = mix(o0, o1, o2, span, reps, m)
-        own_att.append(att)
-        totals.append(total)
-        attended.append(to_reps(att))
+    xp, nt, got_qkv, got_pair, got_four, own_att, got_att, totals = forward_call(
+        layer_in, qkv_weight, row(input_gain), row(input_bias), seq_lengths, reps
+    )
+    residual = [xp[m] for m in micros]
+    normed = [nt[m] for m in micros]
+    pieces = [(got_qkv[m], got_pair[m], got_four[m]) for m in micros]
+    attended = [got_att, to_reps(own_att[1])]
 
     outputs, branch_grads, head_grads, groups, norm_terms, hidden_terms = [], [], [], [], [], []
     weights = (out_weight, up_weight, down_weight)

time: 728 us -> 611 us (0.84)
  waiting for transfers between devices: 203 us -> 123 us
  starting transfers between devices: 136 us -> 97.2 us
  blocking collectives: 24.8 us -> 0 us
  Pallas kernels: 302 us -> 317 us
  local copies, waits for them, and re-layouts: 29.2 us -> 41 us
    all_to_all x8 -> x5, waiting for transfers between devices: 60.4 us -> 14.3 us  [to_reps(): return lax.all_to_all(x, 'rep', 0, 0, tiled=True)]
    pallas_call x8 -> x1, Pallas kernels: 73.2 us -> 102 us  [forward_call(): pl.pallas_call(forward_body, in_specs=[vmem_spec()] * 4 + [smem_spec()],...]
    all_to_all x2 -> x0, blocking collectives: 24.8 us -> none  [the longest x1 12.4 us: to_pair(): return lax.all_to_all(x, 'seq', 0, 0, tiled=True, axis_index_groups=pairs)]
    all_to_all x7 -> x4, waiting for transfers between devices: 51 us -> 26.9 us  [to_pair(): return lax.all_to_all(x, 'seq', 0, 0, tiled=True, axis_index_groups=pairs)]
    all_to_all x8 -> x5, starting transfers between devices: 42.8 us -> 19.7 us  [to_reps(): return lax.all_to_all(x, 'rep', 0, 0, tiled=True)]
    squeeze x0 -> x7, local copies, waits for them, and re-layouts: none -> 15.8 us  [the longest x3 9.86 us: on_device(): pieces = [(got_qkv[m], got_pair[m], got_four[m]) for m in micros]]
    pallas_call x8 -> x4, Pallas kernels: 28.7 us -> 15.8 us  [small_call(): pl.pallas_call(body, in_specs=[smem_spec() if n in smem else vmem_spec()...]
    all_to_all x7 -> x4, starting transfers between devices: 25.9 us -> 14.8 us  [to_four(): return lax.all_to_all(x, 'seq', 0, 0, tiled=True, axis_index_groups=fours)]
  transfers between devices with their start and end apart: 64 -> 55, of which waited for: 28 -> 22; matrix products, arithmetic and copies ran while one was open for 6% -> 9% of each run, Pallas kernels for 37% -> 35%
where the time goes in v2:
time: 611 us; the launch traced here: 606 us
  Pallas kernels  317 us (52%)
  waiting for transfers between devices  123 us (20%)
  starting transfers between devices  97.2 us (16%)
  local copies, waits for them, and re-layouts  41 us (7%)
  other arithmetic  26.3 us (4%)
    pallas_call x1, Pallas kernels, forward_call(): pl.pallas_call(forward_body, in_specs=[vmem_spec()] * 4 + [smem_spec()],...  102 us
    pallas_call x6, Pallas kernels, attn_bwd(): pl.pallas_call(functools.partial(attn_bwd_body, pattern=pattern, micro=mi...  96.9 us
    ppermute x42, waiting for transfers between devices, swap(): return lax.ppermute(block, axis, [(n, n ^ 1 << bit) for n in range(count)])  81.5 us
    pallas_call x2, Pallas kernels, ffn_call(): pl.pallas_call(ffn_body, grid=(1,), in_specs=[pl.BlockSpec((reps, cols, t...  60.6 us
    ppermute x42, starting transfers between devices, swap(): return lax.ppermute(block, axis, [(n, n ^ 1 << bit) for n in range(count)])  47.8 us
    all_to_all x4, waiting for transfers between devices, to_pair(): return lax.all_to_all(x, 'seq', 0, 0, tiled=True, axis_index_groups=pairs)  26.9 us
    all_to_all x5, starting transfers between devices, to_reps(): return lax.all_to_all(x, 'rep', 0, 0, tiled=True)  19.7 us
    pallas_call x1, Pallas kernels, weight_grads(): pl.pallas_call(weight_grad_body, grid=(hidden // CHUNK,), in_specs=[full,...  17.2 us
  transfers between devices with their start and end apart: 55, of which 22 were waited for; matrix products, arithmetic and copies ran while one was open for 9% of the time, Pallas kernels for 35%

profile of v2, /device:TPU:0, one launch (start us, length us, event | category | flops | bytes accessed | tf_op | source)
XLA Modules:
  0.0 606.1 jit_solution(1659518022749909113)
XLA Ops:
  3.2 101.7 %forward.1 = (bf16[2,512,768]{2,1,0:T(8,128)(2,1)}, bf16[2,768,512]{2,1,0:T(8,128)(2,1)}, bf16[2,4,3,192,512]{4,3,2,1,0:T(8,128)(2,1)}, bf16[2,2,2,3,64,1024]{5,...) custom-call(bf16[2,512,768]{2,1,0:T(8,128)(2,1)} %x_ref.1, ...), custom_call_target="tpu_custom_call" | custom-call | flops 60000002048 | bytes 30000000 | tf_op jit(solution)/shard_map/forward/pallas_call | solution.py:1236
  119.8 30.3 %ffn_0.1 = (bf16[512,768]{1,0:T(8,128)(2,1)}, f32[512,768]{1,0:T(8,128)}, bf16[4,192,512]{2,1,0:T(8,128)(2,1)}, bf16[512,768]{1,0:T(8,128)(2,1)}, bf16[512,768]{...) custom-call(bf16[4,192,512]{2,1,0:T(8,128)(2,1)} %get-tuple-element., ...), custom_call_target="tpu_custom_call" | custom-call | flops 10871635968 | bytes 25000000 | tf_op jit(solution)/shard_map/ffn_0/pallas_call | solution.py:658
  157.1 30.3 %ffn_1.1 = (bf16[512,768]{1,0:T(8,128)(2,1)}, f32[512,768]{1,0:T(8,128)}, bf16[4,192,512]{2,1,0:T(8,128)(2,1)}, bf16[512,768]{1,0:T(8,128)(2,1)}, bf16[512,768]{...) custom-call(bf16[4,192,512]{2,1,0:T(8,128)(2,1)} %copy-done.19, ...), custom_call_target="tpu_custom_call" | custom-call | flops 10871635968 | bytes 25000000 | tf_op jit(solution)/shard_map/ffn_1/pallas_call | solution.py:658
  204.0 17.2 %weight_grads.1 = (bf16[3072,768]{1,0:T(8,128)(2,1)}, bf16[768,3072]{1,0:T(8,128)(2,1)}, bf16[768,768]{1,0:T(8,128)(2,1)}) custom-call(bf16[512,768]{1,0:T(8,128)(2,1)} %get-tuple-element.73.refs_0_, bf16[512,3072]{1,0:T(8,128)(2,1)} %get-tuple-element.74.refs_1_, bf16[512,3072]{1,0:T(8,128)(2,1)} %get-tuple-element.75.refs_2_, ...), custom_call_target="tpu_custom_call" | custom-call | flops 10871635968 | bytes 30000000 | tf_op jit(solution)/shard_map/weight_grads/pallas_call | solution.py:712
  231.2 5.3 all-to-all-done.7.g_ref
  253.3 10.0 %all-to-all-done.8.g_ref = bf16[2,2,80,1024]{3,2,1,0:T(8,128)(2,1)S(1)} async-done(((bf16[2,2,80,1024]{3,2,1,0:T(8,128)(2,1)}), bf16[2,2,80,1024]{3,2,1,0:T(8,128)(2,1)S(1)}, u32[]{:S(2)}, u32[]{:S(2)}) %all-to-all-start.8) | async-done | bytes 655392 | tf_op jit(solution)/shard_map/all_to_all | solution.py:1343
  266.8 16.2 %attn_bwd_1_0.1 = bf16[2,2,3,64,1024]{4,3,2,1,0:T(8,128)(2,1)} custom-call(bf16[2,2,3,64,1024]{4,3,2,1,0:T(8,128)(2,1)} %get-tuple-element.96.x_ref, bf16[2,2,80,1024]{3,2,1,0:T(8,128)(2,1)} %copy-done.20, s32[2,4]{1,0:T(2,128)} %len_ref.13), custom_call_target="tpu_custom_call" | custom-call | flops 16000000000 | bytes 4000000 | tf_op jit(solution)/shard_map/attn_bwd_1_0/pallas_call | solution.py:247
  291.2 9.0 %attn_bwd_2_0.1 = bf16[4,3,64,512]{3,2,1,0:T(8,128)(2,1)} custom-call(bf16[4,3,64,512]{3,2,1,0:T(8,128)(2,1)} %get-tuple-element.100.x_ref, bf16[4,80,512]{2,1,0:T(8,128)(2,1)} %all-to-all-done.4.g_ref, s32[2,4]{1,0:T(2,128)} %len_ref.13), custom_call_target="tpu_custom_call" | custom-call | flops 8000000000 | bytes 2000000 | tf_op jit(solution)/shard_map/attn_bwd_2_0/pallas_call | solution.py:247
  301.8 8.3 %all-to-all-done.3.d1_ref = bf16[2,2,3,64,1024]{4,3,2,1,0:T(8,128)(2,1)S(1)} async-done(((bf16[2,2,3,64,1024]{4,3,2,1,0:T(8,128)(2,1)}), bf16[2,2,3,64,1024]{4,3,2,1,0:T(8,128)(2,1)S(1)}, u32[]{:S(2)}, u32[]{:S(2)}) %all-to-all-start.3) | async-done | bytes 1572896 | tf_op jit(solution)/shard_map/all_to_all | solution.py:1343
  313.9 16.2 %attn_bwd_1_1.1 = bf16[2,2,3,64,1024]{4,3,2,1,0:T(8,128)(2,1)} custom-call(bf16[2,2,3,64,1024]{4,3,2,1,0:T(8,128)(2,1)} %get-tuple-element.97.x_ref, bf16[2,2,80,1024]{3,2,1,0:T(8,128)(2,1)} %copy-done.21, s32[2,4]{1,0:T(2,128)} %len_ref.13), custom_call_target="tpu_custom_call" | custom-call | flops 16000000000 | bytes 4000000 | tf_op jit(solution)/shard_map/attn_bwd_1_1/pallas_call | solution.py:247
  336.7 9.0 %attn_bwd_2_1.1 = bf16[4,3,64,512]{3,2,1,0:T(8,128)(2,1)} custom-call(bf16[4,3,64,512]{3,2,1,0:T(8,128)(2,1)} %get-tuple-element.101.x_ref, bf16[4,80,512]{2,1,0:T(8,128)(2,1)} %copy-done.22, s32[2,4]{1,0:T(2,128)} %len_ref.13), custom_call_target="tpu_custom_call" | custom-call | flops 8000000000 | bytes 2000000 | tf_op jit(solution)/shard_map/attn_bwd_2_1/pallas_call | solution.py:247
  346.1 8.5 %all-to-all-done.9.d1_ref = bf16[2,2,3,64,1024]{4,3,2,1,0:T(8,128)(2,1)S(1)} async-done(((bf16[2,2,3,64,1024]{4,3,2,1,0:T(8,128)(2,1)}), bf16[2,2,3,64,1024]{4,3,2,1,0:T(8,128)(2,1)S(1)}, u32[]{:S(2)}, u32[]{:S(2)}) %all-to-all-start.9) | async-done | bytes 1572896 | tf_op jit(solution)/shard_map/all_to_all | solution.py:1343
  358.2 23.2 %attn_bwd_0_0.1.d0_ref = bf16[4,3,192,512]{3,2,1,0:T(8,128)(2,1)} custom-call(bf16[4,3,192,512]{3,2,1,0:T(8,128)(2,1)} %get-tuple-element.94.x_ref, bf16[4,3,80,512]{3,2,1,0:T(8,128)(2,1)} %get-tuple-element.59.g_ref, s32[2,4]{1,0:T(2,128)} %len_ref.13), custom_call_target="tpu_custom_call" | custom-call | flops 24000000000 | bytes 6000000 | tf_op jit(solution)/shard_map/attn_bwd_0_0/pallas_call | solution.py:247
  393.0 23.3 %attn_bwd_0_1.1.d0_ref = bf16[4,3,192,512]{3,2,1,0:T(8,128)(2,1)} custom-call(bf16[4,3,192,512]{3,2,1,0:T(8,128)(2,1)} %get-tuple-element.95.x_ref, bf16[4,3,80,512]{3,2,1,0:T(8,128)(2,1)} %get-tuple-element.67.g_ref, s32[2,4]{1,0:T(2,128)} %len_ref.13), custom_call_target="tpu_custom_call" | custom-call | flops 24000000000 | bytes 6000000 | tf_op jit(solution)/shard_map/attn_bwd_0_1/pallas_call | solution.py:247
  440.1 8.4 %input_grad_0.1 = (bf16[512,768]{1,0:T(8,128)(2,1)}, f32[2,768]{1,0:T(2,128)}) custom-call(bf16[4,3,192,512]{3,2,1,0:T(8,128)(2,1)} %copy-done, bf16[768,2304]{1,0:T(8,128)(2,1)} %w_ref.5, bf16[512,768]{1,0:T(8,128)(2,1)} %get-tuple-element.104.xp_ref, f32[512,768]{1,0:T(8,128)} %get-tuple-element.64.branch_ref, f32[1,768]{1,0:T(1,128)} %reshape.282.gain_ref), custom_call_target="tpu_custom_call" | custom-call | flops 1811939328 | bytes 10000000 | tf_op jit(solution)/shard_map/input_grad_0/pallas_call | solution.py:800
  448.4 9.0 %all-to-all-done.12.tg_ref.refs_3_ = bf16[4,3,192,512]{3,2,1,0:T(8,128)(2,1)} async-done(((bf16[4,3,192,512]{3,2,1,0:T(8,128)(2,1)}), bf16[4,3,192,512]{3,2,1,0:T(8,128)(2,1)}, u32[]{:S(2)}, u32[]{:S(2)}) %all-to-all-start.12) | async-done | bytes 2359328 | tf_op jit(solution)/shard_map/all_to_all | solution.py:1340
  457.4 8.4 %input_grad_1.1 = (bf16[512,768]{1,0:T(8,128)(2,1)}, f32[2,768]{1,0:T(2,128)}) custom-call(bf16[4,3,192,512]{3,2,1,0:T(8,128)(2,1)} %all-to-all-done.12.tg_ref.refs_3_, bf16[768,2304]{1,0:T(8,128)(2,1)} %w_ref.5, bf16[512,768]{1,0:T(8,128)(2,1)} %get-tuple-element.105.xp_ref, f32[512,768]{1,0:T(8,128)} %get-tuple-element.70.branch_ref, ...), custom_call_target="tpu_custom_call" | custom-call | flops 1811939328 | bytes 10000000 | tf_op jit(solution)/shard_map/input_grad_1/pallas_call | solution.py:800
  469.8 12.3 %collective-permute-done.22 = bf16[2,2,2,96,768]{4,3,2,1,0:T(8,128)(2,1)} collective-permute-done((bf16[2,2,2,96,768]{4,3,2,1,0:T(8,128)(2,1)S(1)}, bf16[2,2,2,96,768]{4,3,2,1,0:T(8,128)(2,1)}, u32[]{:S(2)}, u32[]{:S(2)}) %collective-permute-start.22) | collective-permute-done | bytes 1179680 | tf_op jit(solution)/shard_map/ppermute | solution.py:1275
  491.9 9.2 %collective-permute-done.30 = f32[2,2,24,6]{2,1,3,0:T(2,128)S(1)} collective-permute-done((f32[2,2,24,6]{2,1,3,0:T(2,128)S(1)}, f32[2,2,24,6]{2,1,3,0:T(2,128)S(1)}, u32[]{:S(2)}, u32[]{:S(2)}) %collective-permute-start.30) | collective-permute-done | bytes 2336 | tf_op jit(solution)/shard_map/ppermute | solution.py:1275
  505.3 7.8 %qkv_grad.1 = bf16[768,2304]{1,0:T(8,128)(2,1)} custom-call(bf16[768,512]{1,0:T(8,128)(2,1)} %get-tuple-element.99.refs_0_, bf16[4,3,192,512]{3,2,1,0:T(8,128)(2,1)} %copy-done, bf16[768,512]{1,0:T(8,128)(2,1)} %get-tuple-element.98.refs_2_, bf16[4,3,192,512]{3,2,1,0:T(8,128)(2,1)} %all-to-all-done.12.tg_ref.refs_3_), custom_call_target="tpu_custom_call" | custom-call | flops 3623878656 | bytes 10000000 | tf_op jit(solution)/shard_map/qkv_grad/pallas_call | solution.py:756
  530.8 9.1 %collective-permute-done.24 = bf16[2,96,768]{2,1,0:T(8,128)(2,1)S(1)} collective-permute-done((bf16[2,96,768]{2,1,0:T(8,128)(2,1)S(1)}, bf16[2,96,768]{2,1,0:T(8,128)(2,1)S(1)}, u32[]{:S(2)}, u32[]{:S(2)}) %collective-permute-start.24) | collective-permute-done | bytes 294944 | tf_op jit(solution)/shard_map/ppermute | solution.py:1275
  540.2 9.7 %collective-permute-done.17 = bf16[2,24,3072]{2,1,0:T(8,128)(2,1)S(1)} collective-permute-done((bf16[2,24,3072]{2,1,0:T(8,128)(2,1)S(1)}, bf16[2,24,3072]{2,1,0:T(8,128)(2,1)S(1)}, u32[]{:S(2)}, u32[]{:S(2)}) %collective-permute-start.17) | collective-permute-done | bytes 294944 | tf_op jit(solution)/shard_map/ppermute | solution.py:1275
  556.4 14.9 %collective-permute-done.1 = bf16[2,2,2,24,2304]{4,3,2,1,0:T(8,128)(2,1)S(1)} collective-permute-done((bf16[2,2,2,24,2304]{4,3,2,1,0:T(8,128)(2,1)S(1)}, bf16[2,2,2,24,2304]{4,3,2,1,0:T(8,128)(2,1)S(1)}, u32[]{:S(2)}, u32[]{:S(2)}) %collective-permute-start.1) | collective-permute-done | bytes 884768 | tf_op jit(solution)/shard_map/ppermute | solution.py:1275
  599.1 5.5 collective-permute-done.6
  (280 shorter events, 201.1 us)
Async XLA Ops:
  107.7 45.4 %all-to-all-start = ((bf16[4,192,512]{2,1,0:T(8,128)(2,1)}), bf16[4,192,512]{2,1,0:T(8,128)(2,1)S(1)}, u32[]{:S(2)}, u32[]{:S(2)}) async-start(bf16[4,192,512]{2,1,0:T(8,128)(2,1)} %get-tuple-element.103.att_ref), calls=%async_computation | async-start | bytes 1572864 | tf_op jit(solution)/shard_map/all_to_all | solution.py:1340
  153.1 41.6 %all-to-all-start.1 = ((bf16[4,192,512]{2,1,0:T(8,128)(2,1)}), bf16[4,192,512]{2,1,0:T(8,128)(2,1)S(1)}, u32[]{:S(2)}, u32[]{:S(2)}) async-start(bf16[4,192,512]{2,1,0:T(8,128)(2,1)} %get-tuple-element.57), calls=%async_computation.1 | async-start | bytes 1572864 | tf_op jit(solution)/shard_map/all_to_all | solution.py:1340
  198.4 22.9 %all-to-all-start.2 = ((bf16[2,2,80,1024]{3,2,1,0:T(8,128)(2,1)}), bf16[2,2,80,1024]{3,2,1,0:T(8,128)(2,1)S(1)}, u32[]{:S(2)}, u32[]{:S(2)}) async-start(bf16[2,2,80,1024]{3,2,1,0:T(8,128)(2,1)} %get-tuple-element.61), calls=%async_computation.2 | async-start | bytes 1310720 | tf_op jit(solution)/shard_map/all_to_all | solution.py:1343
  202.0 23.0 %collective-permute-start.37 = (f32[2,2,96,2]{2,3,1,0:T(2,128)S(1)}, f32[2,2,96,2]{2,3,1,0:T(2,128)S(1)}, u32[]{:S(2)}, u32[]{:S(2)}) collective-permute-start(f32[2,2,96,2]{2,3,1,0:T(2,128)S(1)} %fusion.27), channel_id=1, source_target_pairs={{0,4},{4,0},{8,12},{12,8},{16,20},{20,16},{24,28},{28,24},{1,5},{5... | collective-permute-start | bytes 9224 | tf_op jit(solution)/shard_map/ppermute | solution.py:1275
  226.3 56.8 %collective-permute-start.7 = (bf16[2,2,2,2,24,768]{5,4,3,2,1,0:T(8,128)(2,1)S(1)}, bf16[2,2,2,2,24,768]{5,4,3,2,1,0:T(8,128)(2,1)}, u32[]{:S(2)}, u32[]{:S(2)}) collective-permute-start(bf16[2,2,2,2,24,768]{5,4,3,2,1,0:T(8,128)(2,1)S(1)} %dynamic-slice_bitcast_fusion.8), channel_id=1, source_target_pairs={{0,1},{1,0},{2,3},{3,2},{4,5},{5,4},{6,7},{7,6},{8,9},{9,8},{10,11... | collective-permute-start | bytes 1769480 | tf_op jit(solution)/shard_map/ppermute | solution.py:1275
  245.9 182.4 %collective-permute-start.21 = (bf16[2,2,2,2,96,768]{5,4,3,2,1,0:T(8,128)(2,1)}, bf16[2,2,2,2,96,768]{5,4,3,2,1,0:T(8,128)(2,1)}, u32[]{:S(2)}, u32[]{:S(2)}) collective-permute-start(bf16[2,2,2,2,96,768]{5,4,3,2,1,0:T(8,128)(2,1)} %dynamic-slice_bitcast_fusion), channel_id=1, source_target_pairs={{0,1},{1,0},{2,3},{3,2},{4,5},{5,4},{6,7},{7,6},{8,9},{9,8},{10,11... | collective-permute-start | bytes 7077896 | tf_op jit(solution)/shard_map/ppermute | solution.py:1275
  246.4 187.2 %collective-permute-start.14 = (bf16[2,2,2,2,24,3072]{5,4,3,2,1,0:T(8,128)(2,1)}, bf16[2,2,2,2,24,3072]{5,4,3,2,1,0:T(8,128)(2,1)}, u32[]{:S(2)}, u32[]{:S(2)}) collective-permute-start(bf16[2,2,2,2,24,3072]{5,4,3,2,1,0:T(8,128)(2,1)} %dynamic-slice_bitcast_fusion.1), channel_id=1, source_target_pairs={{0,1},{1,0},{2,3},{3,2},{4,5},{5,4},{6,7},{7,6},{8,9},{9,8},{10,11... | collective-permute-start | bytes 7077896 | tf_op jit(solution)/shard_map/ppermute | solution.py:1275
  253.0 128.6 %collective-permute-start.41 = (f32[192,2]{0,1:T(2,128)S(1)}, f32[192,2]{0,1:T(2,128)S(1)}, u32[]{:S(2)}, u32[]{:S(2)}) collective-permute-start(f32[192,2]{0,1:T(2,128)S(1)} %select_n.351), channel_id=1, source_target_pairs={{0,2},{1,3},{2,0},{3,1},{4,6},{5,7},{6,4},{7,5},{8,10},{9,11},{10,... | collective-permute-start | bytes 4616 | tf_op jit(solution)/shard_map/ppermute | solution.py:1275
  263.4 23.0 %all-to-all-start.10 = ((bf16[4,80,512]{2,1,0:T(8,128)(2,1)}), bf16[4,80,512]{2,1,0:T(8,128)(2,1)S(1)}, u32[]{:S(2)}, u32[]{:S(2)}) async-start(bf16[4,80,512]{2,1,0:T(8,128)(2,1)} %get-tuple-element.69), calls=%async_computation.10 | async-start | bytes 655360 | tf_op jit(solution)/shard_map/all_to_all | solution.py:1346
  287.1 23.0 %all-to-all-start.3 = ((bf16[2,2,3,64,1024]{4,3,2,1,0:T(8,128)(2,1)}), bf16[2,2,3,64,1024]{4,3,2,1,0:T(8,128)(2,1)S(1)}, u32[]{:S(2)}, u32[]{:S(2)}) async-start(bf16[2,2,3,64,1024]{4,3,2,1,0:T(8,128)(2,1)} %attn_bwd_1_0.1), calls=%async_computation.3 | async-start | bytes 3145728 | tf_op jit(solution)/shard_map/all_to_all | solution.py:1343
  300.3 29.8 %collective-permute-start.9 = (bf16[2,2,24,768]{3,2,1,0:T(8,128)(2,1)S(1)}, bf16[2,2,24,768]{3,2,1,0:T(8,128)(2,1)S(1)}, u32[]{:S(2)}, u32[]{:S(2)}) collective-permute-start(bf16[2,2,24,768]{3,2,1,0:T(8,128)(2,1)S(1)} %dynamic-slice_bitcast_fusion.16), channel_id=1, source_target_pairs={{0,8},{4,12},{8,0},{12,4},{16,24},{20,28},{24,16},{28,20},{1,9},{5... | collective-permute-start | bytes 442376 | tf_op jit(solution)/shard_map/ppermute | solution.py:1275
  310.1 22.7 %all-to-all-start.5 = ((bf16[4,3,64,512]{3,2,1,0:T(8,128)(2,1)}), bf16[4,3,64,512]{3,2,1,0:T(8,128)(2,1)S(1)}, u32[]{:S(2)}, u32[]{:S(2)}) async-start(bf16[4,3,64,512]{3,2,1,0:T(8,128)(2,1)} %attn_bwd_2_0.1), calls=%async_computation.5 | async-start | bytes 1572864 | tf_op jit(solution)/shard_map/all_to_all | solution.py:1346
  332.8 21.8 %all-to-all-start.9 = ((bf16[2,2,3,64,1024]{4,3,2,1,0:T(8,128)(2,1)}), bf16[2,2,3,64,1024]{4,3,2,1,0:T(8,128)(2,1)S(1)}, u32[]{:S(2)}, u32[]{:S(2)}) async-start(bf16[2,2,3,64,1024]{4,3,2,1,0:T(8,128)(2,1)} %attn_bwd_1_1.1), calls=%async_computation.9 | async-start | bytes 3145728 | tf_op jit(solution)/shard_map/all_to_all | solution.py:1343
  345.7 35.9 %collective-permute-start.11 = (bf16[24,768]{1,0:T(8,128)(2,1)S(1)}, bf16[24,768]{1,0:T(8,128)(2,1)S(1)}, u32[]{:S(2)}, u32[]{:S(2)}) collective-permute-start(bf16[24,768]{1,0:T(8,128)(2,1)S(1)} %dynamic-slice_bitcast_fusion.19), channel_id=1, source_target_pairs={{0,2},{1,3},{2,0},{3,1},{4,6},{5,7},{6,4},{7,5},{8,10},{9,11},{10,... | collective-permute-start | bytes 110600 | tf_op jit(solution)/shard_map/ppermute | solution.py:1275
  354.7 33.6 %all-to-all-start.11 = ((bf16[4,3,64,512]{3,2,1,0:T(8,128)(2,1)}), bf16[4,3,64,512]{3,2,1,0:T(8,128)(2,1)S(1)}, u32[]{:S(2)}, u32[]{:S(2)}) async-start(bf16[4,3,64,512]{3,2,1,0:T(8,128)(2,1)} %attn_bwd_2_1.1), calls=%async_computation.11 | async-start | bytes 1572864 | tf_op jit(solution)/shard_map/all_to_all | solution.py:1346
  382.9 33.4 %collective-permute-start.13 = (bf16[48,768]{1,0:T(8,128)(2,1)S(1)}, bf16[48,768]{1,0:T(8,128)(2,1)S(1)}, u32[]{:S(2)}, u32[]{:S(2)}) collective-permute-start(bf16[48,768]{1,0:T(8,128)(2,1)S(1)} %bitcast.282), channel_id=1, source_target_pairs={{0,2},{1,3},{2,0},{3,1},{4,6},{5,7},{6,4},{7,5},{8,10},{9,11},{10,... | collective-permute-start | bytes 221192 | tf_op jit(solution)/shard_map/ppermute | solution.py:1275
  389.2 32.9 %all-to-all-start.6 = ((bf16[4,3,192,512]{3,2,1,0:T(8,128)(2,1)}), bf16[4,3,192,512]{3,2,1,0:T(8,128)(2,1)S(1)}, u32[]{:S(2)}, u32[]{:S(2)}) async-start(bf16[4,3,192,512]{3,2,1,0:T(8,128)(2,1)} %sum_grad_0.1), calls=%async_computation.6 | async-start | bytes 4718592 | tf_op jit(solution)/shard_map/all_to_all | solution.py:1340
  423.6 33.8 %all-to-all-start.12 = ((bf16[4,3,192,512]{3,2,1,0:T(8,128)(2,1)}), bf16[4,3,192,512]{3,2,1,0:T(8,128)(2,1)}, u32[]{:S(2)}, u32[]{:S(2)}) async-start(bf16[4,3,192,512]{3,2,1,0:T(8,128)(2,1)} %sum_grad_1.1), calls=%async_computation.12 | async-start | bytes 4718592 | tf_op jit(solution)/shard_map/all_to_all | solution.py:1340
  431.5 50.6 %collective-permute-start.22 = (bf16[2,2,2,96,768]{4,3,2,1,0:T(8,128)(2,1)S(1)}, bf16[2,2,2,96,768]{4,3,2,1,0:T(8,128)(2,1)}, u32[]{:S(2)}, u32[]{:S(2)}) collective-permute-start(bf16[2,2,2,96,768]{4,3,2,1,0:T(8,128)(2,1)S(1)} %dynamic-slice_bitcast_fusion.3), channel_id=1, source_target_pairs={{0,2},{1,3},{2,0},{3,1},{4,6},{5,7},{6,4},{7,5},{8,10},{9,11},{10,... | collective-permute-start | bytes 3538952 | tf_op jit(solution)/shard_map/ppermute | solution.py:1275
  438.1 52.1 %collective-permute-start.15 = (bf16[2,2,2,24,3072]{4,3,2,1,0:T(8,128)(2,1)}, bf16[2,2,2,24,3072]{4,3,2,1,0:T(8,128)(2,1)}, u32[]{:S(2)}, u32[]{:S(2)}) collective-permute-start(bf16[2,2,2,24,3072]{4,3,2,1,0:T(8,128)(2,1)} %dynamic-slice_bitcast_fusion.4), channel_id=1, source_target_pairs={{0,4},{4,0},{8,12},{12,8},{16,20},{20,16},{24,28},{28,24},{1,5},{5... | collective-permute-start | bytes 3538952 | tf_op jit(solution)/shard_map/ppermute | solution.py:1275
  485.5 39.2 %collective-permute-start.23 = (bf16[2,2,96,768]{3,2,1,0:T(8,128)(2,1)}, bf16[2,2,96,768]{3,2,1,0:T(8,128)(2,1)}, u32[]{:S(2)}, u32[]{:S(2)}) collective-permute-start(bf16[2,2,96,768]{3,2,1,0:T(8,128)(2,1)} %dynamic-slice_bitcast_fusion.6), channel_id=1, source_target_pairs={{0,4},{4,0},{8,12},{12,8},{16,20},{20,16},{24,28},{28,24},{1,5},{5... | collective-permute-start | bytes 1769480 | tf_op jit(solution)/shard_map/ppermute | solution.py:1275
  503.9 24.3 %collective-permute-start.16 = (bf16[2,2,24,3072]{3,2,1,0:T(8,128)(2,1)}, bf16[2,2,24,3072]{3,2,1,0:T(8,128)(2,1)}, u32[]{:S(2)}, u32[]{:S(2)}) collective-permute-start(bf16[2,2,24,3072]{3,2,1,0:T(8,128)(2,1)} %dynamic-slice_bitcast_fusion.7), channel_id=1, source_target_pairs={{0,8},{4,12},{8,0},{12,4},{16,24},{20,28},{24,16},{28,20},{1,9},{5... | collective-permute-start | bytes 1769480 | tf_op jit(solution)/shard_map/ppermute | solution.py:1275
  519.3 31.8 %collective-permute-start = (bf16[2,2,2,2,24,2304]{5,4,3,2,1,0:T(8,128)(2,1)}, bf16[2,2,2,2,24,2304]{5,4,3,2,1,0:T(8,128)(2,1)}, u32[]{:S(2)}, u32[]{:S(2)}) collective-permute-start(bf16[2,2,2,2,24,2304]{5,4,3,2,1,0:T(8,128)(2,1)} %dynamic-slice_bitcast_fusion.2), channel_id=1, source_target_pairs={{0,1},{1,0},{2,3},{3,2},{4,5},{5,4},{6,7},{7,6},{8,9},{9,8},{10,11... | collective-permute-start | bytes 5308424 | tf_op jit(solution)/shard_map/ppermute | solution.py:1275
  574.0 21.6 %collective-permute-start.27 = (bf16[192,768]{1,0:T(8,128)(2,1)S(1)}, bf16[192,768]{1,0:T(8,128)(2,1)S(1)}, u32[]{:S(2)}, u32[]{:S(2)}) collective-permute-start(bf16[192,768]{1,0:T(8,128)(2,1)S(1)} %bitcast.269), channel_id=1, source_target_pairs={{0,2},{1,3},{2,0},{3,1},{4,6},{5,7},{6,4},{7,5},{8,10},{9,11},{10,... | collective-permute-start | bytes 884744 | tf_op jit(solution)/shard_map/ppermute | solution.py:1275
  (63 other events, 668.2 us)

commit v3 on v2

--- a/solution.py
+++ b/solution.py
@@ -681,60 +681,6 @@
     )(att, xp, output_grad, *weights, *gains)
 
 
-def weight_grad_body(*refs):
-    micros = (len(refs) - 6) // 6
-    groups = [refs[6 * k : 6 * k + 6] for k in range(micros)]
-    down_ref, up_ref, proj_ref, lt, _, _ = refs[6 * micros :]
-
-    @pl.when(pl.program_id(0) == 0)
-    def _():
-        total = None
-        for k, (low, dup, hid, cot, mix, brl) in enumerate(groups):
-            lt[k] = low[...].T
-            part = dot_tn(mix[...], brl[...])
-            total = part if total is None else total + part
-        proj_ref[...] = total.astype(bf16)
-
-    up = down = None
-    for k, (low, dup, hid, cot, mix, brl) in enumerate(groups):
-        u = dot_nn(lt[k], dup[...])
-        d = dot_tn(hid[...], cot[...])
-        up = u if up is None else up + u
-        down = d if down is None else down + d
-    up_ref[...] = up.astype(bf16)
-    down_ref[...] = down.astype(bf16)
-
-
-def weight_grads(groups, tok, width, hidden):
-    full = pl.BlockSpec((tok, width), lambda n: (0, 0))
-    part = pl.BlockSpec((tok, CHUNK), lambda n: (0, n))
-    micros = len(groups)
-    return pl.pallas_call(
-        weight_grad_body,
-        grid=(hidden // CHUNK,),
-        in_specs=[full, part, part, full, full, full] * micros,
-        out_specs=[
-            pl.BlockSpec((CHUNK, width), lambda n: (n, 0)),
-            pl.BlockSpec((width, CHUNK), lambda n: (0, n)),
-            pl.BlockSpec((width, width), lambda n: (0, 0)),
-        ],
-        out_shape=[
-            jax.ShapeDtypeStruct((hidden, width), bf16),
-            jax.ShapeDtypeStruct((width, hidden), bf16),
-            jax.ShapeDtypeStruct((width, width), bf16),
-        ],
-        scratch_shapes=[pltpu.VMEM((micros, width, tok), bf16)]
-        + [pltpu.VMEM((8, 128), f32)] * 2,
-        compiler_params=pltpu.CompilerParams(vmem_limit_bytes=VMEM),
-        cost_estimate=pl.CostEstimate(
-            flops=2 * micros * tok * width * (2 * hidden + width),
-            bytes_accessed=30_000_000,
-            transcendentals=0,
-        ),
-        name="weight_grads",
-    )(*[a for g in groups for a in g])
-
-
 def join_heads(tg_ref, c):
     reps = tg_ref.shape[0]
     return jnp.concatenate([tg_ref[r, c] for r in range(reps)], 0)
@@ -1270,6 +1216,660 @@
     )(layer_in, weight, gain, bias, lengths)
 
 
+def bit_of(axis, bit):
+    return lax.axis_index(axis) // (1 << bit) % 2
+
+
+def bit_peer(axis, bit):
+    return lax.axis_index(axis) + (1 << bit) * (1 - 2 * bit_of(axis, bit))
+
+
+def attend_back(block, gblock, doc, put, scr, pattern, count, lanes):
+    ks, vs, qs, qr, gs, gr, dq = scr
+    bs = min(512, lanes)
+    zeros = jnp.zeros((HD, bs), bf16)
+    r = lax.broadcasted_iota(jnp.int32, (HD, bs), 0)
+    fill = jnp.zeros((HD - 32, bs), bf16)
+    for s in range(0, count, bs):
+        sl = slice(s, s + bs)
+        same = doc[:, sl] == r
+        aux_k = jnp.where(same | ((r >= 16) & (r < 19)), 1.0, 0.0).astype(bf16)
+        aux_q = jnp.where(same | (r >= 4), 0.0, NEG).astype(bf16)
+        aux_v = jnp.where((r >= 19) & (r < 21), 1.0, 0.0).astype(bf16)
+        q = (block(0, s, bs).astype(f32) * 0.125).astype(bf16)
+        tile = gblock(s, bs)
+        g, stats = tile[:HD], tile[HD:]
+        qs[:, sl] = jnp.concatenate([q, aux_q[:16], stats, fill], 0)
+        gs[:, sl] = jnp.concatenate([g, zeros[:16], stats, fill], 0)
+        qr[sl, :] = jnp.concatenate([q, zeros], 0).T
+        gr[sl, :] = jnp.concatenate([g, zeros], 0).T
+        ks[sl, :] = jnp.concatenate([block(1, s, bs), aux_k], 0).T
+        vs[sl, :] = jnp.concatenate([block(2, s, bs), aux_v], 0).T
+
+    keep = rel_pos((bs, bs), 0, 0, pattern) <= rel_pos((bs, bs), 1, 0, pattern)
+    for j in range(count // bs):
+        jl = slice(j * bs, (j + 1) * bs)
+        dva, dka = None, None
+        for i in range(j, count // bs):
+            il = slice(i * bs, (i + 1) * bs)
+            p = jnp.exp2(dot_nn(ks[jl, :], qs[:, il]) * LOG2E)
+            if i == j:
+                p = jnp.where(keep, p, 0.0)
+            dp = dot_nn(vs[jl, :], gs[:, il])
+            ds = (p * dp).astype(bf16)
+            dvi = dot_nn(p.astype(bf16), gr[il, :])
+            dki = dot_nn(ds, qr[il, :])
+            dva = dvi if dva is None else dva + dvi
+            dka = dki if dka is None else dka + dki
+            dqi = dot_nn(block(1, j * bs, bs), ds) * 0.125
+            if j == 0:
+                dq[:, il] = dqi
+            else:
+                dq[:, il] += dqi
+        put(1, j * bs, bs, dka.T[:HD].astype(bf16))
+        put(2, j * bs, bs, dva.T[:HD].astype(bf16))
+        put(0, j * bs, bs, dq[:, jl].astype(bf16))
+
+
+class Halving:
+    def __init__(self, source, steps, buffers, gathered, out, sems):
+        self.source, self.steps, self.buffers = source, steps, buffers
+        self.gathered, self.out, self.sems = gathered, out, sems
+        self.names = ["high", "x", "y"]
+        self.at = 0
+        self.pending = None
+
+    def pick(self, ref, axis, name, index):
+        lead = (slice(None),) * axis
+        if name == "high":
+            half = ref.shape[axis] // 2
+            return lead + (pl.ds(index * half, half),)
+        return lead + (index,)
+
+    def start(self):
+        if self.at < len(self.steps):
+            name, axis_name, bit = self.steps[self.at]
+            axis = self.names.index(name)
+            mine = bit_of(axis_name, bit)
+            target = self.buffers[self.at]
+            copy = remote(
+                self.source.at[self.pick(self.source, axis, name, 1 - mine)],
+                target,
+                self.sems.at[0, self.at],
+                self.sems.at[1, self.at],
+                axis_name,
+                bit_peer(axis_name, bit),
+            )
+            copy.start()
+            self.pending = ("sum", copy, target, self.pick(self.source, axis, name, mine))
+            if name != "high":
+                self.names.pop(axis)
+            return
+        stage = self.at - len(self.steps)
+        y, c = bit_of("rep", 1), bit_of("rep", 0)
+        if stage == 0:
+            self.gathered[y, c] = self.source[0]
+            part, landing, bit = (y, c), (1 - y, c), 1
+        elif stage == 1:
+            part, landing, bit = (slice(None), c), (slice(None), 1 - c), 0
+        else:
+            self.pending = None
+            return
+        copy = lambda place: remote(
+            self.gathered.at[part],
+            self.gathered.at[place],
+            self.sems.at[0, self.at],
+            self.sems.at[1, self.at],
+            "rep",
+            bit_peer("rep", bit),
+        )
+        copy(part).start()
+        self.pending = ("gather", copy(part), copy(landing), None)
+
+    def finish(self):
+        kind, first, second, mine = self.pending
+        if kind == "sum":
+            first.wait()
+            rows = second.shape[0]
+
+            def add(n, carry):
+                at = (n,) if mine[0] == slice(None) else None
+                if at is None:
+                    head = mine[0]
+                    base = head.start if isinstance(head, pl.Slice) else None
+                    value = self.source[(base + n,) + mine[1:]]
+                else:
+                    value = self.source[at + mine[1:]]
+                second[n] = (second[n].astype(f32) + value.astype(f32)).astype(bf16)
+                return carry
+
+            lax.fori_loop(0, rows, add, 0)
+            self.source = second
+        else:
+            first.wait_send()
+            second.wait_recv()
+        self.at += 1
+
+    def pump(self):
+        if self.pending is not None:
+            self.finish()
+            self.start()
+
+    def drain(self):
+        while self.pending is not None:
+            self.pump()
+        for y in range(2):
+            for c in range(2):
+                self.out[y, c] = self.gathered[y, c].astype(f32)
+
+
+def reduce_steps(order, seq_bits):
+    steps = []
+    for name in order:
+        if name == "y":
+            steps.append(("y", "rep", 1))
+        elif name == "x":
+            steps.append(("x", "seq", 0))
+        else:
+            steps += [("high", "seq", b) for b in range(seq_bits - 1, 0, -1)]
+    return steps
+
+
+def reduce_buffers(shape, steps):
+    high, rows, cols = shape[0], shape[3], shape[4]
+    rest = ["x", "y"]
+    out = []
+    for name, _, _ in steps:
+        if name == "high":
+            high //= 2
+        else:
+            rest.remove(name)
+        out.append((high,) + (2,) * len(rest) + (rows, cols))
+    return out
+
+
+REDUCE_ORDERS = ("yxz", "xyz", "yxz")
+
+
+def backward_body(
+    r_hbm,
+    p1_hbm,
+    p2_hbm,
+    da0_ref,
+    da1_ref,
+    att_ref,
+    mix_ref,
+    len_ref,
+    w0_ref,
+    w1_ref,
+    w2_ref,
+    tg_ref,
+    t0_ref,
+    t1_ref,
+    t2_ref,
+    *scratch,
+    seq_bits,
+):
+    (r, p1, p2, g0, g1s, g2s, g1, g2, d1, d2, e1, e2, sums, ks, vs, qs, qr, gs, gr, dq) = scratch[:20]
+    load_sems, g1_sems, g2_sems, d1_sems, d2_sems, tg_sems, tg1_sems, own_sems = scratch[20:28]
+    rest = list(scratch[28:])
+    halvings = []
+    for order, source, out in zip(
+        REDUCE_ORDERS, (w0_ref, w1_ref, w2_ref), (t0_ref, t1_ref, t2_ref)
+    ):
+        steps = reduce_steps(order, seq_bits)
+        buffers = [rest.pop(0) for _ in steps]
+        gathered, sems = rest.pop(0), rest.pop(0)
+        halvings.append(Halving(source, steps, buffers, gathered, out, sems))
+    reps, cols, tok = da0_ref.shape
+    micros = att_ref.shape[0]
+    span = tok * reps
+    wide = span // 2
+    me = lax.axis_index("rep")
+    place = team_place()
+    side = place % 2
+    scr = (ks, vs, qs, qr, gs, gr, dq)
+
+    barrier = pltpu.get_barrier_semaphore()
+    peers = [("rep", rep_peer(k)) for k in range(1, 4)]
+    peers += [("seq", team_member(k)) for k in range(1, 4)]
+    peers += [("seq", bit_peer("seq", b)) for b in range(2, seq_bits)]
+    for axis, peer in peers:
+        pl.semaphore_signal(
+            barrier, inc=1, device_id={axis: peer}, device_id_type=pl.DeviceIdType.MESH
+        )
+    load_r = lambda m: pltpu.make_async_copy(r_hbm.at[m], r, load_sems.at[0])
+    load_1 = lambda m: pltpu.make_async_copy(p1_hbm.at[m], p1, load_sems.at[1])
+    load_2 = lambda m: pltpu.make_async_copy(p2_hbm.at[m], p2, load_sems.at[2])
+    load_r(0).start()
+    load_1(0).start()
+    load_2(0).start()
+    pl.semaphore_wait(barrier, len(peers))
+    for h in halvings:
+        h.start()
+
+    def pump():
+        for h in halvings:
+            h.pump()
+
+    def g1_copy(m, s, source):
+        return remote(
+            g1s.at[m, s],
+            g1.at[m, source, s],
+            g1_sems.at[0, m, s],
+            g1_sems.at[1, m, s],
+            "seq",
+            pair_partner(),
+        )
+
+    def g2_copy(m, k, source):
+        return remote(
+            g2s.at[m, (place + k) % 4],
+            g2.at[m, source],
+            g2_sems.at[0, m, k - 1],
+            g2_sems.at[1, m, k - 1],
+            "seq",
+            team_member(k),
+        )
+
+    def d1_copy(m, s, source):
+        return remote(
+            d1.at[m, s, 1 - side],
+            e1.at[m, source, s],
+            d1_sems.at[0, m, s],
+            d1_sems.at[1, m, s],
+            "seq",
+            pair_partner(),
+        )
+
+    def d2_copy(m, k, source):
+        return remote(
+            d2.at[m, (place + k) % 4],
+            e2.at[m, source],
+            d2_sems.at[0, m, k - 1],
+            d2_sems.at[1, m, k - 1],
+            "seq",
+            team_member(k),
+        )
+
+    def tg0_copy(k, source):
+        return remote(
+            sums.at[0, rep_peer(k)],
+            tg_ref.at[0, source],
+            tg_sems.at[0, k - 1],
+            tg_sems.at[1, k - 1],
+            "rep",
+            rep_peer(k),
+        )
+
+    def tg1_copy(j, k, source):
+        return remote(
+            sums.at[1, rep_peer(k), :, head_rows(j)],
+            tg_ref.at[1, source, :, head_rows(j)],
+            tg1_sems.at[0, j, k - 1],
+            tg1_sems.at[1, j, k - 1],
+            "rep",
+            rep_peer(k),
+        )
+
+    own_copy = lambda m: pltpu.make_async_copy(sums.at[m, me], tg_ref.at[m, me], own_sems.at[m])
+
+    def half(j):
+        return pl.ds(pl.multiple_of(((3 * me + j) % 2) * 256, 256), 256)
+
+    def quarter_at(j):
+        c = (3 * me + j) % 4
+        return c % 2 * 2 + c // 2
+
+    def quarter(j):
+        return pl.ds(pl.multiple_of(quarter_at(j) * 128, 128), 128)
+
+    for m, da_ref in enumerate((da0_ref, da1_ref)):
+        for j in range(3):
+            rows = slice(j * HD, (j + 1) * HD)
+            for b in range(reps):
+                g = da_ref[b, rows, :]
+                inner = jnp.sum(
+                    g.astype(f32) * att_ref[m, b, rows, :].astype(f32), 0, keepdims=True
+                )
+                total = mix_ref[m, j : j + 1, b * tok : (b + 1) * tok]
+                high, mid, low = split3(-total)
+                inner_high, inner_mid, _ = split3(-inner)
+                g0[m, j, b, :HD, :] = g
+                g0[m, j, b, HD:, :] = stat_rows((high, mid, low, inner_high, inner_mid), tok)
+        for b in range(reps):
+            bl = slice(b * 256, (b + 1) * 256)
+            g1s[m, 0, :, bl] = g0[m, 1 - side, b, :, half(1 - side)]
+            g1[m, side, 0, :, bl] = g0[m, side, b, :, half(side)]
+            piece = g0[m, 2, b, :, half(2)]
+            g1s[m, 1, :, bl] = piece
+            g1[m, side, 1, :, bl] = piece
+            for g in range(4):
+                j = min(g, 2)
+                g2s[m, g, :, b * 128 : (b + 1) * 128] = g0[m, j, b, :, quarter(j)]
+        g2[m, place] = g2s[m, place]
+        for s in range(2):
+            g1_copy(m, s, side).start()
+        for k in range(1, 4):
+            g2_copy(m, k, place).start()
+
+    def docs(m, pattern):
+        return doc_rows(len_ref, m, segment_start(pattern, span), 2**pattern, span)
+
+    def own_head(m, j):
+        def block(c, start, size):
+            at = start % tok
+            return r[start // tok, c, head_rows(j), at : at + size]
+
+        def gblock(start, size):
+            at = start % tok
+            return g0[m, j, start // tok, :, at : at + size]
+
+        def put(c, start, size, value):
+            at = start % tok
+            sums[m, start // tok, c, head_rows(j), at : at + size] = value
+
+        attend_back(block, gblock, docs(m, 0), put, scr, 0, span, tok)
+
+    def add_others(m, j):
+        e, s = PLACE1[j]
+        for b in range(reps):
+            bl = slice(b * 256, (b + 1) * 256)
+            t = sums[m, b, :, j * HD : (j + 1) * HD, half(j)].astype(f32)
+            t = t + e1[m, e, s, :, :, bl].astype(f32)
+            sums[m, b, :, j * HD : (j + 1) * HD, half(j)] = t.astype(bf16)
+            t = sums[m, b, :, j * HD : (j + 1) * HD, quarter(j)].astype(f32)
+            t = t + e2[m, j, :, :, b * 128 : (b + 1) * 128].astype(f32)
+            sums[m, b, :, j * HD : (j + 1) * HD, quarter(j)] = t.astype(bf16)
+
+    def wait_others(m):
+        for s in range(2):
+            d1_copy(m, s, 1 - side).wait_recv()
+        for k in range(1, 4):
+            d2_copy(m, k, (place + 4 - k) % 4).wait_recv()
+
+    load_r(0).wait()
+
+    def first_heads(j, carry):
+        own_head(0, j)
+        return carry
+
+    lax.fori_loop(0, 3, first_heads, 0)
+    load_r(1).start()
+
+    def others(m):
+        def paired(s, inner):
+            g1_copy(m, s, 1 - side).wait_recv()
+
+            def block(c, start, size):
+                at = start % wide
+                return p1[start // wide, s, c, :, at : at + size]
+
+            def gblock(start, size):
+                at = start % wide
+                return g1[m, start // wide, s, :, at : at + size]
+
+            def put(c, start, size, value):
+                at = start % wide
+                d1[m, s, start // wide, c, :, at : at + size] = value
+
+            attend_back(block, gblock, docs(m, 1), put, scr, 1, span, wide)
+            e1[m, side, s] = d1[m, s, side]
+            d1_copy(m, s, side).start()
+            return inner
+
+        load_1(m).wait()
+        lax.fori_loop(0, 2, paired, 0)
+        if m + 1 < micros:
+            load_1(m + 1).start()
+        pump()
+        if m == 1:
+            wait_others(0)
+            for j in range(3):
+                add_others(0, j)
+            for k in range(1, 4):
+                tg0_copy(k, me).start()
+            own_copy(0).start()
+        for k in range(1, 4):
+            g2_copy(m, k, (place + 4 - k) % 4).wait_recv()
+        load_2(m).wait()
+
+        def block(c, start, size):
+            at = start % tok
+            return p2[start // tok, c, :, at : at + size]
+
+        def gblock(start, size):
+            at = start % tok
+            return g2[m, start // tok, :, at : at + size]
+
+        def put(c, start, size, value):
+            at = start % tok
+            d2[m, start // tok, c, :, at : at + size] = value
+
+        attend_back(block, gblock, docs(m, 2), put, scr, 2, span, tok)
+        e2[m, place] = d2[m, place]
+        for k in range(1, 4):
+            d2_copy(m, k, place).start()
+        if m + 1 < micros:
+            load_2(m + 1).start()
+
+    others(0)
+    others(1)
+    load_r(1).wait()
+    for j in range(3):
+        own_head(1, j)
+        if j == 0:
+            wait_others(1)
+        add_others(1, j)
+        for k in range(1, 4):
+            tg1_copy(j, k, me).start()
+        pump()
+    own_copy(1).start()
+    for h in halvings:
+        h.drain()
+    for m in range(micros):
+        own_copy(m).wait()
+        for s in range(2):
+            g1_copy(m, s, side).wait_send()
+            d1_copy(m, s, side).wait_send()
+        for k in range(1, 4):
+            g2_copy(m, k, place).wait_send()
+            d2_copy(m, k, place).wait_send()
+    for k in range(1, 4):
+        source = (me + reps - k) % reps
+        tg0_copy(k, source).wait_recv()
+        tg0_copy(k, me).wait_send()
+        for j in range(3):
+            tg1_copy(j, k, source).wait_recv()
+            tg1_copy(j, k, me).wait_send()
+
+
+def backward_call(pieces, da, att, totals, lengths, grads, seq_bits):
+    micros, reps, cols, tok = att.shape
+    span = tok * reps
+    any_spec = pl.BlockSpec(memory_space=pl.ANY)
+
+    def vm(*shape):
+        return pltpu.VMEM(shape, bf16)
+
+    dma = pltpu.SemaphoreType.DMA
+    halving = []
+    for order, g in zip(REDUCE_ORDERS, grads):
+        steps = reduce_steps(order, seq_bits)
+        halving += [vm(*b) for b in reduce_buffers(g.shape, steps)]
+        halving += [vm(2, 2, *g.shape[3:]), dma((2, len(steps) + 2))]
+    tall, flat = vm(span, 128), vm(128, span)
+    outs = [((micros, reps, 3, cols, tok), bf16, any_spec)]
+    outs += [((2, 2) + g.shape[3:], f32, vmem_spec()) for g in grads]
+    return pl.pallas_call(
+        functools.partial(backward_body, seq_bits=seq_bits),
+        in_specs=[any_spec] * 3 + [vmem_spec()] * 4 + [smem_spec()] + [vmem_spec()] * 3,
+        out_specs=[o[2] for o in outs],
+        out_shape=[jax.ShapeDtypeStruct(o[0], o[1]) for o in outs],
+        scratch_shapes=[
+            vm(reps, 3, cols, tok),
+            vm(2, 2, 3, HD, span // 2),
+            vm(4, 3, HD, span // 4),
+            vm(micros, 3, reps, HPAD, tok),
+            vm(micros, 2, HPAD, span // 2),
+            vm(micros, 4, HPAD, span // 4),
+            vm(micros, 2, 2, HPAD, span // 2),
+            vm(micros, 4, HPAD, span // 4),
+            vm(micros, 2, 2, 3, HD, span // 2),
+            vm(micros, 4, 3, HD, span // 4),
+            vm(micros, 2, 2, 3, HD, span // 2),
+            vm(micros, 4, 3, HD, span // 4),
+            vm(micros, reps, 3, cols, tok),
+            tall,
+            tall,
+            flat,
+            tall,
+            flat,
+            tall,
+            pltpu.VMEM((HD, span), f32),
+            dma((3,)),
+            dma((2, micros, 2)),
+            dma((2, micros, 3)),
+            dma((2, micros, 2)),
+            dma((2, micros, 3)),
+            dma((2, 3)),
+            dma((2, 3, 3)),
+            dma((micros,)),
+            *halving,
+        ],
+        compiler_params=pltpu.CompilerParams(
+            vmem_limit_bytes=60 << 20, collective_id=2, has_side_effects=True
+        ),
+        cost_estimate=pl.CostEstimate(
+            flops=100_000_000_000, bytes_accessed=40_000_000, transcendentals=30_000_000
+        ),
+        name="backward",
+    )(*pieces, *da, att, totals, lengths, *grads)
+
+
+def split_rows(value, parts, rows):
+    mine, other = [], []
+    first = bit_of("rep", 0) == 0
+    for n in range(parts):
+        a = value[(2 * n) * rows : (2 * n + 1) * rows]
+        b = value[(2 * n + 1) * rows : (2 * n + 2) * rows]
+        mine.append(jnp.where(first, a, b))
+        other.append(jnp.where(first, b, a))
+    return mine, other
+
+
+def weight_grad_body(*refs, chunks):
+    ins, refs = refs[:12], refs[12:]
+    down_ref, up_ref, proj_ref, lt = refs[:4]
+    keeps, sends, gets, sems = refs[4:7], refs[7:10], refs[10:13], refs[13:16]
+    groups = [ins[:6], ins[6:]]
+    n = pl.program_id(0)
+
+    def copy(t, slot):
+        return remote(
+            sends[t].at[slot],
+            gets[t].at[slot],
+            sems[t].at[0, slot],
+            sems[t].at[1, slot],
+            "rep",
+            bit_peer("rep", 0),
+        )
+
+    def spread(t, slot, value):
+        keep = keeps[t]
+        parts, rows = keep.shape[1], keep.shape[2]
+        mine, other = split_rows(value, parts, rows)
+        for k in range(parts):
+            keep[slot, k] = mine[k].astype(bf16)
+            sends[t][slot, k] = other[k].astype(bf16)
+        copy(t, slot).start()
+
+    @pl.when(n == 0)
+    def _():
+        barrier = pltpu.get_barrier_semaphore()
+        pl.semaphore_signal(
+            barrier,
+            inc=1,
+            device_id={"rep": bit_peer("rep", 0)},
+            device_id_type=pl.DeviceIdType.MESH,
+        )
+        pl.semaphore_wait(barrier, 1)
+        total = None
+        for k, (low, dup, hid, cot, mix, brl) in enumerate(groups):
+            lt[k] = low[...].T
+            part = dot_tn(mix[...], brl[...])
+            total = part if total is None else total + part
+        spread(2, 0, total)
+
+    @pl.when(n < chunks)
+    def _():
+        up = down = None
+        for k, (low, dup, hid, cot, mix, brl) in enumerate(groups):
+            u = dot_nn(lt[k], dup[...])
+            d = dot_tn(hid[...], cot[...])
+            up = u if up is None else up + u
+            down = d if down is None else down + d
+        spread(0, n, down)
+        spread(1, n, up)
+
+    def merged(t, slot, out_ref):
+        copy(t, slot).wait()
+        keep, got = keeps[t], gets[t]
+        for k in range(keep.shape[1]):
+            out_ref[k] = (keep[slot, k].astype(f32) + got[slot, k].astype(f32)).astype(bf16)
+
+    @pl.when(n > 0)
+    def _():
+        merged(0, n - 1, down_ref)
+        merged(1, n - 1, up_ref)
+
+    @pl.when(n == chunks)
+    def _():
+        merged(2, 0, proj_ref)
+
+
+def weight_grads(groups, tok, width, hidden, seqs, reps):
+    chunk = 768
+    chunks = hidden // chunk
+    last = chunks - 1
+    full = pl.BlockSpec((tok, width), lambda n: (0, 0))
+    part = pl.BlockSpec((tok, chunk), lambda n: (0, jnp.minimum(n, last)))
+    down_rows, up_rows = hidden // seqs // reps, width // seqs // reps
+    per = chunk // down_rows // 2
+    blocks = seqs * reps // 2
+    shapes = [(chunks, per, down_rows, width), (chunks, blocks, up_rows, chunk), (1, blocks, up_rows, width)]
+    boxes = [pltpu.VMEM(s, bf16) for s in shapes]
+    return pl.pallas_call(
+        functools.partial(weight_grad_body, chunks=chunks),
+        grid=(chunks + 1,),
+        in_specs=[full, part, part, full, full, full] * 2,
+        out_specs=[
+            pl.BlockSpec((per, down_rows, width), lambda n: (jnp.maximum(n - 1, 0), 0, 0)),
+            pl.BlockSpec((blocks, up_rows, chunk), lambda n: (0, 0, jnp.maximum(n - 1, 0))),
+            pl.BlockSpec((blocks, up_rows, width), lambda n: (0, 0, 0)),
+        ],
+        out_shape=[
+            jax.ShapeDtypeStruct((blocks, down_rows, width), bf16),
+            jax.ShapeDtypeStruct((blocks, up_rows, hidden), bf16),
+            jax.ShapeDtypeStruct((blocks, up_rows, width), bf16),
+        ],
+        scratch_shapes=[pltpu.VMEM((2, width, tok), bf16)]
+        + boxes
+        + boxes
+        + boxes
+        + [pltpu.SemaphoreType.DMA((2, s[0])) for s in shapes],
+        compiler_params=pltpu.CompilerParams(
+            vmem_limit_bytes=VMEM, collective_id=3, has_side_effects=True
+        ),
+        cost_estimate=pl.CostEstimate(
+            flops=4 * tok * width * (2 * hidden + width),
+            bytes_accessed=30_000_000,
+            transcendentals=0,
+        ),
+        name="weight_grads",
+    )(*[a for g in groups for a in g])
+
+
 def swap(block, axis, bit):
     count = lax.axis_size(axis)
     return lax.ppermute(block, axis, [(n, n ^ (1 << bit)) for n in range(count)])
@@ -1354,7 +1954,6 @@
     )
     residual = [xp[m] for m in micros]
     normed = [nt[m] for m in micros]
-    pieces = [(got_qkv[m], got_pair[m], got_four[m]) for m in micros]
     attended = [got_att, to_reps(own_att[1])]
 
     outputs, branch_grads, head_grads, groups, norm_terms, hidden_terms = [], [], [], [], [], []
@@ -1372,21 +1971,19 @@
         groups.append((low, dup, hid, cotp, mixl, brl))
         norm_terms.append(ng)
         hidden_terms.append(nh)
-    grad_down, grad_up, grad_proj = weight_grads(groups, tok, width, up_weight.shape[1])
-
-    down_total = reduce_rows(grad_down, order_yxz)
-    up_total = reduce_rows(grad_up, order_xzy)
-    proj_total = reduce_rows(grad_proj, order_xzy)
-
-    input_grads, input_terms, token_grads = [], [], []
-    for m in micros:
-        g0, g1, g2 = pack_grad(head_grads[m], own_att[m], totals[m], span, reps, m)
-        g1, g2 = to_pair(g1), to_four(g2)
-        x0, x1, x2 = pieces[m]
-        d0 = attn_bwd(x0, g0, seq_lengths, 0, m, span, reps)
-        d1 = to_pair(attn_bwd(x1, g1, seq_lengths, 1, m, span, reps))
-        d2 = to_four(attn_bwd(x2, g2, seq_lengths, 2, m, span, reps))
-        token_grads.append(to_reps(sum_grad(d0, d1, d2, span, reps, m)))
+    seq_bits = bits_of(seqs)
+    grads = [
+        g.reshape((seqs // 2, 2, reps // 2) + g.shape[1:])
+        for g in weight_grads(groups, tok, width, up_weight.shape[1], seqs, reps)
+    ]
+    token_grad, down_total, up_total, proj_total = backward_call(
+        (got_qkv, got_pair, got_four), head_grads, own_att, totals, seq_lengths, grads, seq_bits
+    )
+    down_total, up_total, proj_total = (
+        t.reshape(-1, t.shape[-1]) for t in (down_total, up_total, proj_total)
+    )
+    token_grads = [token_grad[m] for m in micros]
+    input_grads, input_terms = [], []
     grad_qkv = qkv_grad_call(list(zip(normed, token_grads)), tok, width, reps)
     for m in micros:
         grad, terms = input_grad_call(

time: 611 us -> 486 us (0.80)
  waiting for transfers between devices: 123 us -> 31.4 us
  starting transfers between devices: 97.2 us -> 44.4 us
  Pallas kernels: 317 us -> 364 us
  local copies, waits for them, and re-layouts: 41 us -> 27.1 us
  other arithmetic: 26.3 us -> 13 us
    ppermute x42 -> x21, waiting for transfers between devices: 81.5 us -> 31.4 us  [swap(): return lax.ppermute(block, axis, [(n, n ^ 1 << bit) for n in range(count)])]
    pallas_call x11 -> x2, Pallas kernels: 130 us -> 178 us  [the longest x1 156 us: backward_call(): pl.pallas_call(functools.partial(backward_body, seq_bits=seq_bits), in_sp...]
    all_to_all x8 -> x0, starting transfers between devices: 29.8 us -> none  [the longest x4 14.9 us: to_pair(): return lax.all_to_all(x, 'seq', 0, 0, tiled=True, axis_index_groups=pairs)]
    all_to_all x8 -> x0, waiting for transfers between devices: 26.9 us -> none  [the longest x4 26.9 us: to_pair(): return lax.all_to_all(x, 'seq', 0, 0, tiled=True, axis_index_groups=pairs)]
    ppermute x42 -> x21, starting transfers between devices: 47.8 us -> 33.3 us  [swap(): return lax.ppermute(block, axis, [(n, n ^ 1 << bit) for n in range(count)])]
    all_to_all x5 -> x3, waiting for transfers between devices: 14.3 us -> 0.01 us  [to_reps(): return lax.all_to_all(x, 'rep', 0, 0, tiled=True)]
    convert_element_type x20 -> x5, other arithmetic: 16.5 us -> 3.29 us  [reduce_rows(): y = (keep.astype(f32) + got.astype(f32)).astype(x.dtype)]
    squeeze x24 -> x9, local copies, waits for them, and re-layouts: 11.6 us -> 1.77 us  [reduce_rows(): send = lax.dynamic_index_in_dim(y, 1 - mine, at, keepdims=False)]
  transfers between devices with their start and end apart: 55 -> 24, of which waited for: 22 -> 9; matrix products, arithmetic and copies ran while one was open for 9% -> 6% of each run, Pallas kernels for 35% -> 55%
where the time goes in v3:
time: 486 us; the launch traced here: 482 us
  Pallas kernels  364 us (75%)
  starting transfers between devices  44.4 us (9%)
  waiting for transfers between devices  31.4 us (6%)
  local copies, waits for them, and re-layouts  27.1 us (6%)
  other arithmetic  13 us (3%)
    pallas_call x1, Pallas kernels, backward_call(): pl.pallas_call(functools.partial(backward_body, seq_bits=seq_bits), in_sp...  156 us
    pallas_call x1, Pallas kernels, forward_call(): pl.pallas_call(forward_body, in_specs=[vmem_spec()] * 4 + [smem_spec()],...  102 us
    pallas_call x2, Pallas kernels, ffn_call(): pl.pallas_call(ffn_body, grid=(1,), in_specs=[pl.BlockSpec((reps, cols, t...  60.6 us
    ppermute x21, starting transfers between devices, swap(): return lax.ppermute(block, axis, [(n, n ^ 1 << bit) for n in range(count)])  33.3 us
    ppermute x21, waiting for transfers between devices, swap(): return lax.ppermute(block, axis, [(n, n ^ 1 << bit) for n in range(count)])  31.4 us
    pallas_call x1, Pallas kernels, weight_grads(): pl.pallas_call(functools.partial(weight_grad_body, chunks=chunks), grid=(...  21.6 us
    pallas_call x2, Pallas kernels, input_grad_call(): pl.pallas_call(input_grad_body, grid=(3,), in_specs=[pl.BlockSpec((reps,...  16.8 us
    all_to_all x3, starting transfers between devices, to_reps(): return lax.all_to_all(x, 'rep', 0, 0, tiled=True)  11.1 us
  transfers between devices with their start and end apart: 24, of which 9 were waited for; matrix products, arithmetic and copies ran while one was open for 6% of the time, Pallas kernels for 55%

profile of v3, /device:TPU:0, one launch (start us, length us, event | category | flops | bytes accessed | tf_op | source)
XLA Modules:
  0.0 481.8 jit_solution(14672400112117353758)
XLA Ops:
  3.2 101.6 %forward.1 = (bf16[2,512,768]{2,1,0:T(8,128)(2,1)}, bf16[2,768,512]{2,1,0:T(8,128)(2,1)}, bf16[2,4,3,192,512]{4,3,2,1,0:T(8,128)(2,1)}, bf16[2,2,2,3,64,1024]{5,...) custom-call(bf16[2,512,768]{2,1,0:T(8,128)(2,1)} %x_ref.1, ...), custom_call_target="tpu_custom_call" | custom-call | flops 60000002048 | bytes 30000000 | tf_op jit(solution)/shard_map/forward/pallas_call | solution.py:1182
  107.0 3.5 all-to-all-start
  114.1 30.2 %ffn_0.1 = (bf16[512,768]{1,0:T(8,128)(2,1)}, f32[512,768]{1,0:T(8,128)}, bf16[4,192,512]{2,1,0:T(8,128)(2,1)}, bf16[512,768]{1,0:T(8,128)(2,1)}, bf16[512,768]{...) custom-call(bf16[4,192,512]{2,1,0:T(8,128)(2,1)} %get-tuple-element., ...), custom_call_target="tpu_custom_call" | custom-call | flops 10871635968 | bytes 25000000 | tf_op jit(solution)/shard_map/ffn_0/pallas_call | solution.py:658
  144.4 4.0 all-to-all-start.1
  148.4 30.4 %ffn_1.1 = (bf16[512,768]{1,0:T(8,128)(2,1)}, f32[512,768]{1,0:T(8,128)}, bf16[4,192,512]{2,1,0:T(8,128)(2,1)}, bf16[512,768]{1,0:T(8,128)(2,1)}, bf16[512,768]{...) custom-call(bf16[4,192,512]{2,1,0:T(8,128)(2,1)} %copy-done.5, ...), custom_call_target="tpu_custom_call" | custom-call | flops 10871635968 | bytes 25000000 | tf_op jit(solution)/shard_map/ffn_1/pallas_call | solution.py:658
  183.3 3.7 all-to-all-start.2
  187.0 21.6 %weight_grads.1 = (bf16[16,96,768]{2,1,0:T(8,128)(2,1)}, bf16[16,24,3072]{2,1,0:T(8,128)(2,1)}, bf16[16,24,768]{2,1,0:T(8,128)(2,1)}) custom-call(bf16[512,768]{1,0:T(8,128)(2,1)} %get-tuple-element.60.refs_0_, bf16[512,3072]{1,0:T(8,128)(2,1)} %get-tuple-element.61.refs_1_, bf16[512,3072]{1,0:T(8,128)(2,1)} %get-tuple-element.62.refs_2_, ...), custom_call_target="tpu_custom_call" | custom-call | flops 10871635968 | bytes 30000000 | tf_op jit(solution)/shard_map/weight_grads/pallas_call | solution.py:1842
  210.8 156.1 %backward.1 = (bf16[2,4,3,192,512]{4,3,2,1,0:T(8,128)(2,1)}, f32[2,2,96,768]{3,2,1,0:T(8,128)}, f32[2,2,24,3072]{3,2,1,0:T(8,128)}, f32[2,2,24,768]{3,2,1,0:T(8,128)}) custom-call(bf16[2,4,3,192,512]{4,3,2,1,0:T(8,128)(2,1)} %get-tuple-element.54.r_hbm, bf16[2,2,2,3,64,1024]{5,4,3,2,1,0:T(8,128)(2,1)} %get-tuple-element.55.p1_hbm, ...), custom_call_target="tpu_custom_call" | custom-call | flops 99999997952 | bytes 40000000 | tf_op jit(solution)/shard_map/backward/pallas_call | solution.py:1704
  366.9 5.0 %slice_bitcast_fusion.1 = (bf16[4,3,192,512]{3,2,1,0:T(8,128)(2,1)}, bf16[4,3,192,512]{3,2,1,0:T(8,128)(2,1)}) fusion(bf16[2,4,3,192,512]{4,3,2,1,0:T(8,128)(2,1)} %get-tuple-element.75), kind=kLoop, calls=%fused_computation.3 | loop fusion | bytes 9437184 | tf_op jit(solution)/shard_map/squeeze | solution.py:1985
  371.9 7.5 %qkv_grad.1 = bf16[768,2304]{1,0:T(8,128)(2,1)} custom-call(bf16[768,512]{1,0:T(8,128)(2,1)} %get-tuple-element.93.refs_0_, bf16[4,3,192,512]{3,2,1,0:T(8,128)(2,1)} %get-tuple-element.90.tg_ref.refs_1_, bf16[768,512]{1,0:T(8,128)(2,1)} %get-tuple-element.92.refs_2_, bf16[4,3,192,512]{3,2,1,0:T(8,128)(2,1)} %get-tuple-element.91.tg_ref.refs_3_), custom_call_target="tpu_custom_call" | custom-call | flops 3623878656 | bytes 10000000 | tf_op jit(solution)/shard_map/qkv_grad/pallas_call | solution.py:702
  381.1 2.3 collective-permute-start
  383.7 3.3 collective-permute-done.17
  388.2 3.3 collective-permute-done.18
  391.5 8.4 %input_grad_0.1 = (bf16[512,768]{1,0:T(8,128)(2,1)}, f32[2,768]{1,0:T(2,128)}) custom-call(bf16[4,3,192,512]{3,2,1,0:T(8,128)(2,1)} %get-tuple-element.90.tg_ref.refs_1_, bf16[768,2304]{1,0:T(8,128)(2,1)} %w_ref.5, bf16[512,768]{1,0:T(8,128)(2,1)} %get-tuple-element.94.xp_ref, f32[512,768]{1,0:T(8,128)} %get-tuple-element.76.branch_ref, ...), custom_call_target="tpu_custom_call" | custom-call | flops 1811939328 | bytes 10000000 | tf_op jit(solution)/shard_map/input_grad_0/pallas_call | solution.py:746
  399.9 8.4 %input_grad_1.1 = (bf16[512,768]{1,0:T(8,128)(2,1)}, f32[2,768]{1,0:T(2,128)}) custom-call(bf16[4,3,192,512]{3,2,1,0:T(8,128)(2,1)} %get-tuple-element.91.tg_ref.refs_3_, bf16[768,2304]{1,0:T(8,128)(2,1)} %w_ref.5, bf16[512,768]{1,0:T(8,128)(2,1)} %get-tuple-element.95.xp_ref, f32[512,768]{1,0:T(8,128)} %get-tuple-element.78.branch_ref, ...), custom_call_target="tpu_custom_call" | custom-call | flops 1811939328 | bytes 10000000 | tf_op jit(solution)/shard_map/input_grad_1/pallas_call | solution.py:746
  418.6 4.8 collective-permute-start.9
  428.6 9.3 %collective-permute-done.1 = bf16[2,2,2,24,2304]{4,3,2,1,0:T(8,128)(2,1)S(1)} collective-permute-done((bf16[2,2,2,24,2304]{4,3,2,1,0:T(8,128)(2,1)S(1)}, bf16[2,2,2,24,2304]{4,3,2,1,0:T(8,128)(2,1)S(1)}, u32[]{:S(2)}, u32[]{:S(2)}) %collective-permute-start.1) | collective-permute-done | bytes 884768 | tf_op jit(solution)/shard_map/ppermute | solution.py:1875
  438.2 5.1 %collective-permute-start.2 = (bf16[2,2,24,2304]{3,2,1,0:T(8,128)(2,1)S(1)}, bf16[2,2,24,2304]{3,2,1,0:T(8,128)(2,1)}, u32[]{:S(2)}, u32[]{:S(2)}) collective-permute-start(bf16[2,2,24,2304]{3,2,1,0:T(8,128)(2,1)S(1)} %dynamic-slice_bitcast_fusion.2), channel_id=1, source_target_pairs={{0,4},{4,0},{8,12},{12,8},{16,20},{20,16},{24,28},{28,24},{1,5},{5... | collective-permute-start | bytes 1327112 | tf_op jit(solution)/shard_map/ppermute | solution.py:1875
  446.0 2.8 collective-permute-start.11
  448.9 4.0 collective-permute-done.2
  456.0 4.1 collective-permute-done.3
  460.3 3.0 collective-permute-start.4
  466.2 2.6 collective-permute-start.13
  472.1 4.4 collective-permute-done.6
  (149 shorter events, 50.9 us)
Async XLA Ops:
  107.0 37.4 %all-to-all-start = ((bf16[4,192,512]{2,1,0:T(8,128)(2,1)}), bf16[4,192,512]{2,1,0:T(8,128)(2,1)S(1)}, u32[]{:S(2)}, u32[]{:S(2)}) async-start(bf16[4,192,512]{2,1,0:T(8,128)(2,1)} %slice_bitcast_fusion.5), calls=%async_computation | async-start | bytes 1572864 | tf_op jit(solution)/shard_map/all_to_all | solution.py:1940
  144.4 38.9 %all-to-all-start.1 = ((bf16[4,192,512]{2,1,0:T(8,128)(2,1)}), bf16[4,192,512]{2,1,0:T(8,128)(2,1)S(1)}, u32[]{:S(2)}, u32[]{:S(2)}) async-start(bf16[4,192,512]{2,1,0:T(8,128)(2,1)} %get-tuple-element.57), calls=%async_computation.1 | async-start | bytes 1572864 | tf_op jit(solution)/shard_map/all_to_all | solution.py:1940
  179.7 2.7 collective-permute-start.14
  182.5 26.1 %collective-permute-start.15 = (f32[2,2,2,96,2]{3,4,2,1,0:T(2,128)S(1)}, f32[2,2,2,96,2]{3,4,2,1,0:T(2,128)S(1)}, u32[]{:S(2)}, u32[]{:S(2)}) collective-permute-start(f32[2,2,2,96,2]{3,4,2,1,0:T(2,128)S(1)} %dynamic-slice_bitcast_fusion.5), channel_id=1, source_target_pairs={{0,2},{1,3},{2,0},{3,1},{4,6},{5,7},{6,4},{7,5},{8,10},{9,11},{10,... | collective-permute-start | bytes 18440 | tf_op jit(solution)/shard_map/ppermute | solution.py:1875
  183.3 26.6 %all-to-all-start.2 = ((bf16[4,192,512]{2,1,0:T(8,128)(2,1)}), bf16[4,192,512]{2,1,0:T(8,128)(2,1)S(1)}, u32[]{:S(2)}, u32[]{:S(2)}) async-start(bf16[4,192,512]{2,1,0:T(8,128)(2,1)} %get-tuple-element.58), calls=%async_computation.2 | async-start | bytes 1572864 | tf_op jit(solution)/shard_map/all_to_all | solution.py:1940
  208.6 174.7 %collective-permute-start.16 = (f32[2,2,96,2]{2,3,1,0:T(2,128)S(1)}, f32[2,2,96,2]{2,3,1,0:T(2,128)S(1)}, u32[]{:S(2)}, u32[]{:S(2)}) collective-permute-start(f32[2,2,96,2]{2,3,1,0:T(2,128)S(1)} %fusion.9), channel_id=1, source_target_pairs={{0,4},{4,0},{8,12},{12,8},{16,20},{20,16},{24,28},{28,24},{1,5},{5... | collective-permute-start | bytes 9224 | tf_op jit(solution)/shard_map/ppermute | solution.py:1875
  381.1 33.0 %collective-permute-start = (bf16[2,2,2,2,24,2304]{5,4,3,2,1,0:T(8,128)(2,1)S(1)}, bf16[2,2,2,2,24,2304]{5,4,3,2,1,0:T(8,128)(2,1)S(1)}, u32[]{:S(2)}, u32[]{:S(2)}) collective-permute-start(bf16[2,2,2,2,24,2304]{5,4,3,2,1,0:T(8,128)(2,1)S(1)} %dynamic-slice_bitcast_fusion), channel_id=1, source_target_pairs={{0,1},{1,0},{2,3},{3,2},{4,5},{5,4},{6,7},{7,6},{8,9},{9,8},{10,11... | collective-permute-start | bytes 5308424 | tf_op jit(solution)/shard_map/ppermute | solution.py:1875
  383.4 3.7 collective-permute-start.17
  387.0 4.5 collective-permute-start.18
  391.5 21.3 %collective-permute-start.19 = (f32[96,2]{0,1:T(2,128)S(1)}, f32[96,2]{0,1:T(2,128)S(1)}, u32[]{:S(2)}, u32[]{:S(2)}) collective-permute-start(f32[96,2]{0,1:T(2,128)S(1)} %fusion.14), channel_id=1, source_target_pairs={{0,1},{1,0},{2,3},{3,2},{4,5},{5,4},{6,7},{7,6},{8,9},{9,8},{10,11... | collective-permute-start | bytes 2312 | tf_op jit(solution)/shard_map/ppermute | solution.py:1875
  412.3 1.4 collective-permute-start.7
  413.8 4.1 collective-permute-start.8
  416.1 21.8 %collective-permute-start.1 = (bf16[2,2,2,24,2304]{4,3,2,1,0:T(8,128)(2,1)S(1)}, bf16[2,2,2,24,2304]{4,3,2,1,0:T(8,128)(2,1)S(1)}, u32[]{:S(2)}, u32[]{:S(2)}) collective-permute-start(bf16[2,2,2,24,2304]{4,3,2,1,0:T(8,128)(2,1)S(1)} %dynamic-slice_bitcast_fusion.1), channel_id=1, source_target_pairs={{0,2},{1,3},{2,0},{3,1},{4,6},{5,7},{6,4},{7,5},{8,10},{9,11},{10,... | collective-permute-start | bytes 2654216 | tf_op jit(solution)/shard_map/ppermute | solution.py:1875
  418.6 6.8 %collective-permute-start.9 = (f32[2,2,24,6]{2,1,3,0:T(2,128)}, f32[2,2,24,6]{2,1,3,0:T(2,128)}, u32[]{:S(2)}, u32[]{:S(2)}) collective-permute-start(f32[2,2,24,6]{2,1,3,0:T(2,128)} %bitcast.146), channel_id=1, source_target_pairs={{0,4},{4,0},{8,12},{12,8},{16,20},{20,16},{24,28},{28,24},{1,5},{5... | collective-permute-start | bytes 6920 | tf_op jit(solution)/shard_map/ppermute | solution.py:1875
  424.8 19.9 %collective-permute-start.20 = (f32[192,2]{0,1:T(2,128)}, f32[192,2]{0,1:T(2,128)}, u32[]{:S(2)}, u32[]{:S(2)}) collective-permute-start(f32[192,2]{0,1:T(2,128)} %select_n.192), channel_id=1, source_target_pairs={{0,2},{1,3},{2,0},{3,1},{4,6},{5,7},{6,4},{7,5},{8,10},{9,11},{10,... | collective-permute-start | bytes 4616 | tf_op jit(solution)/shard_map/ppermute | solution.py:1875
  426.8 18.6 %collective-permute-start.10 = (f32[2,24,6]{1,0,2:T(2,128)}, f32[2,24,6]{1,0,2:T(2,128)}, u32[]{:S(2)}, u32[]{:S(2)}) collective-permute-start(f32[2,24,6]{1,0,2:T(2,128)} %bitcast.147), channel_id=1, source_target_pairs={{0,8},{4,12},{8,0},{12,4},{16,24},{20,28},{24,16},{28,20},{1,9},{5... | collective-permute-start | bytes 3464 | tf_op jit(solution)/shard_map/ppermute | solution.py:1875
  438.2 14.7 %collective-permute-start.2 = (bf16[2,2,24,2304]{3,2,1,0:T(8,128)(2,1)S(1)}, bf16[2,2,24,2304]{3,2,1,0:T(8,128)(2,1)}, u32[]{:S(2)}, u32[]{:S(2)}) collective-permute-start(bf16[2,2,24,2304]{3,2,1,0:T(8,128)(2,1)S(1)} %dynamic-slice_bitcast_fusion.2), channel_id=1, source_target_pairs={{0,4},{4,0},{8,12},{12,8},{16,20},{20,16},{24,28},{28,24},{1,5},{5... | collective-permute-start | bytes 1327112 | tf_op jit(solution)/shard_map/ppermute | solution.py:1875
  446.0 10.0 %collective-permute-start.11 = (f32[24,6]{0,1:T(8,128)S(1)}, f32[24,6]{0,1:T(8,128)S(1)}, u32[]{:S(2)}, u32[]{:S(2)}) collective-permute-start(f32[24,6]{0,1:T(8,128)S(1)} %bitcast.167), channel_id=1, source_target_pairs={{0,16},{4,20},{8,24},{12,28},{16,0},{20,4},{24,8},{28,12},{1,17},{... | collective-permute-start | bytes 1736 | tf_op jit(solution)/shard_map/ppermute | solution.py:1875
  454.1 6.1 %collective-permute-start.3 = (bf16[2,24,2304]{2,1,0:T(8,128)(2,1)S(1)}, bf16[2,24,2304]{2,1,0:T(8,128)(2,1)S(1)}, u32[]{:S(2)}, u32[]{:S(2)}) collective-permute-start(bf16[2,24,2304]{2,1,0:T(8,128)(2,1)S(1)} %dynamic-slice_bitcast_fusion.3), channel_id=1, source_target_pairs={{0,8},{4,12},{8,0},{12,4},{16,24},{20,28},{24,16},{28,20},{1,9},{5... | collective-permute-start | bytes 663560 | tf_op jit(solution)/shard_map/ppermute | solution.py:1875
  456.0 7.9 %collective-permute-start.12 = (f32[24,6]{0,1:T(8,128)S(1)}, f32[24,6]{0,1:T(8,128)S(1)}, u32[]{:S(2)}, u32[]{:S(2)}) collective-permute-start(f32[24,6]{0,1:T(8,128)S(1)} %bitcast_add_fusion.4), channel_id=1, source_target_pairs={{0,1},{1,0},{2,3},{3,2},{4,5},{5,4},{6,7},{7,6},{8,9},{9,8},{10,11... | collective-permute-start | bytes 1736 | tf_op jit(solution)/shard_map/ppermute | solution.py:1875
  460.3 5.7 %collective-permute-start.4 = (bf16[24,2304]{1,0:T(8,128)(2,1)S(1)}, bf16[24,2304]{1,0:T(8,128)(2,1)S(1)}, u32[]{:S(2)}, u32[]{:S(2)}) collective-permute-start(bf16[24,2304]{1,0:T(8,128)(2,1)S(1)} %dynamic-slice_bitcast_fusion.4), channel_id=1, source_target_pairs={{0,16},{4,20},{8,24},{12,28},{16,0},{20,4},{24,8},{28,12},{1,17},{... | collective-permute-start | bytes 331784 | tf_op jit(solution)/shard_map/ppermute | solution.py:1875
  466.0 2.7 collective-permute-start.5
  466.2 5.2 %collective-permute-start.13 = (f32[48,6]{0,1:T(8,128)S(1)}, f32[48,6]{0,1:T(8,128)S(1)}, u32[]{:S(2)}, u32[]{:S(2)}) collective-permute-start(f32[48,6]{0,1:T(8,128)S(1)} %select_n.185), channel_id=1, source_target_pairs={{0,2},{1,3},{2,0},{3,1},{4,6},{5,7},{6,4},{7,5},{8,10},{9,11},{10,... | collective-permute-start | bytes 3464 | tf_op jit(solution)/shard_map/ppermute | solution.py:1875
  468.8 7.7 %collective-permute-start.6 = (bf16[48,2304]{1,0:T(8,128)(2,1)S(1)}, bf16[48,2304]{1,0:T(8,128)(2,1)}, u32[]{:S(2)}, u32[]{:S(2)}) collective-permute-start(bf16[48,2304]{1,0:T(8,128)(2,1)S(1)} %bitcast.153), channel_id=1, source_target_pairs={{0,2},{1,3},{2,0},{3,1},{4,6},{5,7},{6,4},{7,5},{8,10},{9,11},{10,... | collective-permute-start | bytes 663560 | tf_op jit(solution)/shard_map/ppermute | solution.py:1875
  (21 other events, 246.2 us)

commit v4 on v3

--- a/solution.py
+++ b/solution.py
@@ -75,361 +75,36 @@
     return out.astype(bf16)
 
 
-def attn_fwd_body(x_ref, len_ref, o_ref, ks, qs, *, pattern, micro, span):
-    groups, _, _, lanes = x_ref.shape
-    count = groups * lanes
-    doc = doc_rows(len_ref, micro, segment_start(pattern, span), 2**pattern, count)
-
-    def block(c, start, size):
-        return x_ref[start // lanes, c, :, start % lanes : start % lanes + size]
-
-    kb = min(512, lanes)
-    for s in range(0, count, kb):
-        sl = slice(s, s + kb)
-        r = lax.broadcasted_iota(jnp.int32, (HD, kb), 0)
-        same = doc[:, sl] == r
-        aux_k = jnp.where(same, 1.0, 0.0).astype(bf16)
-        aux_q = jnp.where(same | (r >= 4), 0.0, NEG).astype(bf16)
-        q = (block(0, s, kb).astype(f32) * 0.125).astype(bf16)
-        qs[:, sl] = jnp.concatenate([q, aux_q], 0)
-        ks[sl, :] = jnp.concatenate([block(1, s, kb), aux_k], 0).T
-
-    qb = 256
-    grain = 512 if pattern == 0 else 256
-
-    def tiles(i):
-        low = (i * qb) // grain * grain
-        out = [(s, min(512, low - s), False) for s in range(0, low, 512)]
-        return out + [(low, grain, True)]
-
-    def scores(i):
-        out = []
-        for s, size, diagonal in tiles(i):
-            t = dot_nn(ks[s : s + size, :], qs[:, i * qb : (i + 1) * qb])
-            if diagonal:
-                keep = rel_pos((size, qb), 0, s % 512, pattern) <= rel_pos(
-                    (size, qb), 1, (i * qb) % 512, pattern
-                )
-                t = jnp.where(keep, t, NEG)
-            out.append(t)
-        return out
-
-    following = scores(0)
-    for i in range(count // qb):
-        current = following
-        if (i + 1) * qb < count:
-            following = scores(i + 1)
-        top = functools.reduce(jnp.maximum, [jnp.max(t, 0, keepdims=True) for t in current])
-        top2 = top * LOG2E
-        acc, total = None, None
-        for t, (s, size, _) in zip(current, tiles(i)):
-            p = jnp.exp2(t * LOG2E - top2)
-            part = jnp.sum(p, 0, keepdims=True)
-            out = dot_nn(block(2, s, size), p.astype(bf16))
-            acc = out if acc is None else acc + out
-            total = part if total is None else total + part
-        lse = top + jnp.log(total)
-        g, at = (i * qb) // lanes, (i * qb) % lanes
-        o_ref[g, :HD, at : at + qb] = (acc / total).astype(bf16)
-        o_ref[g, HD:, at : at + qb] = stat_rows(split3(lse), qb)
-
-
-def attn_bwd_body(
-    x_ref, g_ref, len_ref, o_ref, ks, vs, qs, qr, gs, gr, dq, *, pattern, micro, span
-):
-    groups, _, _, lanes = x_ref.shape
-    count = groups * lanes
-    doc = doc_rows(len_ref, micro, segment_start(pattern, span), 2**pattern, count)
-    bs = min(512, lanes)
-
-    def block(c, start, size):
-        return x_ref[start // lanes, c, :, start % lanes : start % lanes + size]
-
-    zeros = jnp.zeros((HD, bs), bf16)
-    r = lax.broadcasted_iota(jnp.int32, (HD, bs), 0)
-    fill = jnp.zeros((HD - 32, bs), bf16)
-    for s in range(0, count, bs):
-        sl = slice(s, s + bs)
-        same = doc[:, sl] == r
-        aux_k = jnp.where(same | ((r >= 16) & (r < 19)), 1.0, 0.0).astype(bf16)
-        aux_q = jnp.where(same | (r >= 4), 0.0, NEG).astype(bf16)
-        aux_v = jnp.where((r >= 19) & (r < 21), 1.0, 0.0).astype(bf16)
-        q = (block(0, s, bs).astype(f32) * 0.125).astype(bf16)
-        k = block(1, s, bs)
-        v = block(2, s, bs)
-        at = s % lanes
-        g = g_ref[s // lanes, :HD, at : at + bs]
-        stats = g_ref[s // lanes, HD:, at : at + bs]
-        qs[:, sl] = jnp.concatenate([q, aux_q[:16], stats, fill], 0)
-        gs[:, sl] = jnp.concatenate([g, zeros[:16], stats, fill], 0)
-        qr[sl, :] = jnp.concatenate([q, zeros], 0).T
-        gr[sl, :] = jnp.concatenate([g, zeros], 0).T
-        ks[sl, :] = jnp.concatenate([k, aux_k], 0).T
-        vs[sl, :] = jnp.concatenate([v, aux_v], 0).T
-
-    keep = rel_pos((bs, bs), 0, 0, pattern) <= rel_pos((bs, bs), 1, 0, pattern)
-    for j in range(count // bs):
-        jl = slice(j * bs, (j + 1) * bs)
-        dva, dka = None, None
-        for i in range(j, count // bs):
-            il = slice(i * bs, (i + 1) * bs)
-            p = jnp.exp2(dot_nn(ks[jl, :], qs[:, il]) * LOG2E)
-            if i == j:
-                p = jnp.where(keep, p, 0.0)
-            dp = dot_nn(vs[jl, :], gs[:, il])
-            ds = (p * dp).astype(bf16)
-            dvi = dot_nn(p.astype(bf16), gr[il, :])
-            dki = dot_nn(ds, qr[il, :])
-            dva = dvi if dva is None else dva + dvi
-            dka = dki if dka is None else dka + dki
-            dqi = dot_nn(block(1, j * bs, bs), ds) * 0.125
-            if j == 0:
-                dq[:, il] = dqi
-            else:
-                dq[:, il] += dqi
-        g, at = (j * bs) // lanes, (j * bs) % lanes
-        o_ref[g, 1, :, at : at + bs] = dka.T[:HD].astype(bf16)
-        o_ref[g, 2, :, at : at + bs] = dva.T[:HD].astype(bf16)
-        o_ref[g, 0, :, at : at + bs] = dq[:, jl].astype(bf16)
-
-
-def specs_of(pattern, span, reps):
-    if pattern == 0:
-        return (
-            3,
-            pl.BlockSpec((reps, 3, HD, span // reps), lambda n: (0, 0, n, 0)),
-            pl.BlockSpec((reps, None, HPAD, span // reps), lambda n: (0, n, 0, 0)),
-            (reps, 3, HPAD, span // reps),
-            (reps, 3, 3 * HD, span // reps),
-        )
-    if pattern == 1:
-        return (
-            2,
-            pl.BlockSpec((2, None, 3, HD, span // 2), lambda n: (0, n, 0, 0, 0)),
-            pl.BlockSpec((2, None, HPAD, span // 2), lambda n: (0, n, 0, 0)),
-            (2, 2, HPAD, span // 2),
-            (2, 2, 3, HD, span // 2),
-        )
-    return (
-        1,
-        pl.BlockSpec((4, 3, HD, span // 4), lambda n: (0, 0, 0, 0)),
-        pl.BlockSpec((4, HPAD, span // 4), lambda n: (0, 0, 0)),
-        (4, HPAD, span // 4),
-        (4, 3, HD, span // 4),
-    )
+def shift():
+    return lax.axis_index("rep") % 2
+
+
+def taker():
+    return shift()
+
+
+def owner_of(j):
+    return (j + shift()) % 4
+
+
+def slot_of(place):
+    return (place + 4 - shift()) % 4
+
+
+def clamp_slot(j):
+    return j - j // 3
+
+
+def place1(j):
+    return (taker(), 1) if j == 2 else (j, 0)
 
 
 def smem_spec():
     return pl.BlockSpec(memory_space=pltpu.SMEM)
 
 
-def attn_fwd(x, lengths, pattern, micro, span, reps):
-    n, x_spec, o_spec, o_shape, _ = specs_of(pattern, span, reps)
-    return pl.pallas_call(
-        functools.partial(attn_fwd_body, pattern=pattern, micro=micro, span=span),
-        grid=(n,),
-        in_specs=[x_spec, smem_spec()],
-        out_specs=o_spec,
-        out_shape=jax.ShapeDtypeStruct(o_shape, bf16),
-        scratch_shapes=[pltpu.VMEM((span, 128), bf16), pltpu.VMEM((128, span), bf16)],
-        compiler_params=pltpu.CompilerParams(vmem_limit_bytes=VMEM),
-        cost_estimate=pl.CostEstimate(
-            flops=n * 5_000_000_000, bytes_accessed=n * 1_200_000, transcendentals=n * 2_600_000
-        ),
-        name=f"attn_fwd_{pattern}_{micro}",
-    )(x, lengths)
-
-
-def attn_bwd(x, g, lengths, pattern, micro, span, reps):
-    n, x_spec, g_spec, _, d_shape = specs_of(pattern, span, reps)
-    wide = pltpu.VMEM((128, span), bf16)
-    tall = pltpu.VMEM((span, 128), bf16)
-    return pl.pallas_call(
-        functools.partial(attn_bwd_body, pattern=pattern, micro=micro, span=span),
-        grid=(n,),
-        in_specs=[x_spec, g_spec, smem_spec()],
-        out_specs=x_spec,
-        out_shape=jax.ShapeDtypeStruct(d_shape, bf16),
-        scratch_shapes=[tall, tall, wide, tall, wide, tall, pltpu.VMEM((HD, span), f32)],
-        compiler_params=pltpu.CompilerParams(vmem_limit_bytes=VMEM),
-        cost_estimate=pl.CostEstimate(
-            flops=n * 8_000_000_000, bytes_accessed=n * 2_000_000, transcendentals=n * 2_600_000
-        ),
-        name=f"attn_bwd_{pattern}_{micro}",
-    )(x, g, lengths)
-
-
-OWNER1 = {(0, 0): 0, (0, 1): 2, (1, 0): 1}
-PLACE1 = {0: (0, 0), 1: (1, 0), 2: (0, 1)}
-
-
-def half_of(j):
-    return (3 * lax.axis_index("rep") + j) % 2
-
-
-def quarter_of(j):
-    return class_slot((3 * lax.axis_index("rep") + j) % 4)
-
-
-def lane_slice(start, size):
-    return pl.ds(pl.multiple_of(start, size), size)
-
-
-def pack_qkv_body(r_ref, p1_ref, p2_ref):
-    reps = r_ref.shape[0]
-    for e in range(2):
-        for s in range(2):
-            j = OWNER1.get((e, s), 1)
-            for b in range(reps):
-                p1_ref[e, s, :, :, b * 256 : (b + 1) * 256] = r_ref[
-                    b, :, j * HD : (j + 1) * HD, lane_slice(half_of(j) * 256, 256)
-                ]
-    for g in range(4):
-        j = min(g, 2)
-        for b in range(reps):
-            p2_ref[g, :, :, b * 128 : (b + 1) * 128] = r_ref[
-                b, :, j * HD : (j + 1) * HD, lane_slice(quarter_of(j) * 128, 128)
-            ]
-
-
 def vmem_spec():
     return pl.BlockSpec(memory_space=pltpu.VMEM)
-
-
-def small_call(body, outs, args, name, nbytes, scratch=(), smem=()):
-    return pl.pallas_call(
-        body,
-        in_specs=[smem_spec() if n in smem else vmem_spec() for n in range(len(args))],
-        out_specs=[vmem_spec() for _ in outs],
-        out_shape=[jax.ShapeDtypeStruct(s, d) for s, d in outs],
-        scratch_shapes=list(scratch),
-        compiler_params=pltpu.CompilerParams(vmem_limit_bytes=VMEM),
-        cost_estimate=pl.CostEstimate(flops=1_000_000, bytes_accessed=nbytes, transcendentals=0),
-        name=name,
-    )(*args)
-
-
-def pack_qkv(r, span, reps, micro):
-    return small_call(
-        pack_qkv_body,
-        [((2, 2, 3, HD, span // 2), bf16), ((4, 3, HD, span // 4), bf16)],
-        (r,),
-        f"pack_qkv_{micro}",
-        5_000_000,
-    )
-
-
-def mix_body(o0_ref, o1_ref, o2_ref, att_ref, mix_ref):
-    reps = o0_ref.shape[0]
-
-    def stat(tile):
-        t = tile[HD:, :].astype(f32)
-        return t[0:1] + t[1:2] + t[2:3]
-
-    mix_ref[...] = jnp.zeros_like(mix_ref)
-    for j in range(3):
-        half, quarter = half_of(j), quarter_of(j)
-        e, s = PLACE1[j]
-        for b in range(reps):
-            for a in range(4):
-                la = slice(a * 128, (a + 1) * 128)
-                t0 = o0_ref[b, j, :, la]
-                lb = b * 256 + (a % 2) * 128
-                t1 = o1_ref[e, s, :, lb : lb + 128]
-                t2 = o2_ref[j, :, b * 128 : (b + 1) * 128]
-                l0 = stat(t0)
-                l1 = jnp.where(half == a // 2, stat(t1), NEG)
-                l2 = jnp.where(quarter == a, stat(t2), NEG)
-                top = jnp.maximum(jnp.maximum(l0, l1), l2)
-                e0, e1, e2 = jnp.exp(l0 - top), jnp.exp(l1 - top), jnp.exp(l2 - top)
-                total = e0 + e1 + e2
-                inv = 1.0 / total
-                mixed = (
-                    t0[:HD].astype(f32) * (e0 * inv)
-                    + t1[:HD].astype(f32) * (e1 * inv)
-                    + t2[:HD].astype(f32) * (e2 * inv)
-                )
-                att_ref[b, j * HD : (j + 1) * HD, la] = mixed.astype(bf16)
-                col = b * 512 + a * 128
-                mix_ref[j : j + 1, col : col + 128] = top + jnp.log(total)
-
-
-def mix(o0, o1, o2, span, reps, micro):
-    return small_call(
-        mix_body,
-        [((reps, 3 * HD, span // reps), bf16), ((8, span), f32)],
-        (o0, o1, o2),
-        f"mix_{micro}",
-        4_000_000,
-    )
-
-
-def pack_grad_body(g_ref, att_ref, mix_ref, g0_ref, p1_ref, p2_ref):
-    reps, _, tok = g_ref.shape
-    for j in range(3):
-        rows = slice(j * HD, (j + 1) * HD)
-        for b in range(reps):
-            g = g_ref[b, rows, :]
-            inner = jnp.sum(g.astype(f32) * att_ref[b, rows, :].astype(f32), 0, keepdims=True)
-            total = mix_ref[j : j + 1, b * tok : (b + 1) * tok]
-            h, m, l = split3(-total)
-            ih, im, _ = split3(-inner)
-            g0_ref[b, j, :HD, :] = g
-            g0_ref[b, j, HD:, :] = stat_rows((h, m, l, ih, im), tok)
-    for e in range(2):
-        for s in range(2):
-            j = OWNER1.get((e, s), 1)
-            for b in range(reps):
-                p1_ref[e, s, :, b * 256 : (b + 1) * 256] = g0_ref[
-                    b, j, :, lane_slice(half_of(j) * 256, 256)
-                ]
-    for g in range(4):
-        j = min(g, 2)
-        for b in range(reps):
-            p2_ref[g, :, b * 128 : (b + 1) * 128] = g0_ref[
-                b, j, :, lane_slice(quarter_of(j) * 128, 128)
-            ]
-
-
-def pack_grad(g, att, mixed, span, reps, micro):
-    return small_call(
-        pack_grad_body,
-        [
-            ((reps, 3, HPAD, span // reps), bf16),
-            ((2, 2, HPAD, span // 2), bf16),
-            ((4, HPAD, span // 4), bf16),
-        ],
-        (g, att, mixed),
-        f"pack_grad_{micro}",
-        5_000_000,
-    )
-
-
-def sum_grad_body(d0_ref, d1_ref, d2_ref, out_ref):
-    reps = d0_ref.shape[0]
-    for j in range(3):
-        rows = slice(j * HD, (j + 1) * HD)
-        half, quarter = half_of(j), quarter_of(j)
-        e, s = PLACE1[j]
-        for b in range(reps):
-            for a in range(4):
-                la = slice(a * 128, (a + 1) * 128)
-                lb = b * 256 + (a % 2) * 128
-                t0 = d0_ref[b, :, rows, la].astype(f32)
-                t1 = d1_ref[e, s, :, :, lb : lb + 128].astype(f32)
-                t2 = d2_ref[j, :, :, b * 128 : (b + 1) * 128].astype(f32)
-                t = t0 + jnp.where(half == a // 2, t1, 0.0) + jnp.where(quarter == a, t2, 0.0)
-                out_ref[b, :, rows, la] = t.astype(bf16)
-
-
-def sum_grad(d0, d1, d2, span, reps, micro):
-    return small_call(
-        sum_grad_body,
-        [((reps, 3, 3 * HD, span // reps), bf16)],
-        (d0, d1, d2),
-        f"sum_grad_{micro}",
-        7_000_000,
-    )[0]
 
 
 def onehot_rows(tok):
@@ -456,55 +131,6 @@
     along = jnp.mean(dn * xhat, axis=-1, keepdims=True)
     dx = rstd * (dn - low - xhat * along)
     return dx, jnp.sum(grad * xhat, 0, keepdims=True), jnp.sum(grad, 0, keepdims=True)
-
-
-def qkv_body(x_ref, w_ref, gain_ref, bias_ref, out_ref, xp_ref, nt_ref, n_scr):
-    tok, width = x_ref.shape
-
-    @pl.when(pl.program_id(0) == 0)
-    def _():
-        xp = dot_nn(onehot_rows(tok), x_ref[...])
-        xp_ref[...] = xp.astype(bf16)
-        xhat, _ = normalize(xp)
-        n = (xhat * gain_ref[...] + bias_ref[...]).astype(bf16)
-        n_scr[...] = n
-        nt_ref[...] = n.T
-
-    t = dot_nn(n_scr[...], w_ref[...]).astype(bf16).T
-    reps, _, cols, _ = out_ref.shape
-    for r in range(reps):
-        out_ref[r, 0] = t[r * cols : (r + 1) * cols]
-
-
-def qkv_call(layer_in, weight, gain, bias, m, reps):
-    _, tok, width = layer_in.shape
-    cols = width // reps
-    return pl.pallas_call(
-        qkv_body,
-        grid=(3,),
-        in_specs=[
-            pl.BlockSpec((None, tok, width), lambda c: (m, 0, 0)),
-            pl.BlockSpec((width, width), lambda c: (0, c)),
-            pl.BlockSpec((1, width), lambda c: (0, 0)),
-            pl.BlockSpec((1, width), lambda c: (0, 0)),
-        ],
-        out_specs=[
-            pl.BlockSpec((reps, 1, cols, tok), lambda c: (0, c, 0, 0)),
-            pl.BlockSpec((tok, width), lambda c: (0, 0)),
-            pl.BlockSpec((width, tok), lambda c: (0, 0)),
-        ],
-        out_shape=[
-            jax.ShapeDtypeStruct((reps, 3, cols, tok), bf16),
-            jax.ShapeDtypeStruct((tok, width), bf16),
-            jax.ShapeDtypeStruct((width, tok), bf16),
-        ],
-        scratch_shapes=[pltpu.VMEM((tok, width), bf16)],
-        compiler_params=pltpu.CompilerParams(vmem_limit_bytes=VMEM),
-        cost_estimate=pl.CostEstimate(
-            flops=6 * tok * width * width, bytes_accessed=9_000_000, transcendentals=0
-        ),
-        name=f"qkv_{m}",
-    )(layer_in, weight, gain, bias)
 
 
 CHUNK = 512
@@ -639,7 +265,7 @@
 
 def ffn_call(att, xp, output_grad, weights, gains, m):
     reps, cols, tok = att.shape
-    width = xp.shape[1]
+    width = xp.shape[2]
     hidden = weights[1].shape[1]
     vec = vmem_spec()
     shapes = [
@@ -660,7 +286,7 @@
         grid=(1,),
         in_specs=[
             pl.BlockSpec((reps, cols, tok), lambda n: (0, 0, 0)),
-            pl.BlockSpec((tok, width), lambda n: (0, 0)),
+            pl.BlockSpec((None, tok, width), lambda n: (m, 0, 0)),
             pl.BlockSpec((None, tok, width), lambda n: (m, 0, 0)),
         ]
         + [pl.BlockSpec(memory_space=pl.ANY)] * 3
@@ -679,95 +305,6 @@
         ),
         name=f"ffn_{m}",
     )(att, xp, output_grad, *weights, *gains)
-
-
-def join_heads(tg_ref, c):
-    reps = tg_ref.shape[0]
-    return jnp.concatenate([tg_ref[r, c] for r in range(reps)], 0)
-
-
-def qkv_grad_body(*refs):
-    micros = (len(refs) - 1) // 2
-    out_ref = refs[-1]
-    total = None
-    for k in range(micros):
-        nt, tg = refs[2 * k], refs[2 * k + 1]
-        part = dot_nt(nt[...], join_heads(tg, 0))
-        total = part if total is None else total + part
-    out_ref[...] = total.astype(bf16)
-
-
-def qkv_grad_call(pairs, tok, width, reps):
-    cols = width // reps
-    return pl.pallas_call(
-        qkv_grad_body,
-        grid=(3,),
-        in_specs=[
-            pl.BlockSpec((width, tok), lambda c: (0, 0)),
-            pl.BlockSpec((reps, 1, cols, tok), lambda c: (0, c, 0, 0)),
-        ]
-        * len(pairs),
-        out_specs=pl.BlockSpec((width, width), lambda c: (0, c)),
-        out_shape=jax.ShapeDtypeStruct((width, 3 * width), bf16),
-        compiler_params=pltpu.CompilerParams(vmem_limit_bytes=VMEM),
-        cost_estimate=pl.CostEstimate(
-            flops=6 * len(pairs) * tok * width * width, bytes_accessed=10_000_000, transcendentals=0
-        ),
-        name="qkv_grad",
-    )(*[a for p in pairs for a in p])
-
-
-def input_grad_body(tg_ref, w_ref, xp_ref, branch_ref, gain_ref, out_ref, ng_ref, acc):
-    tok, width = xp_ref.shape
-    c = pl.program_id(0)
-    part = dot_nn(w_ref[...], join_heads(tg_ref, 0))
-
-    @pl.when(c == 0)
-    def _():
-        acc[...] = part
-
-    @pl.when(c > 0)
-    def _():
-        acc[...] += part
-
-    @pl.when(c == 2)
-    def _():
-        xhat, rstd = normalize(xp_ref[...].astype(f32))
-        dx, gain_i, bias_i = norm_back(acc[...].T, gain_ref[...], xhat, rstd)
-        ng_ref[0:1] = gain_i
-        ng_ref[1:2] = bias_i
-        total = (branch_ref[...] + dx).astype(bf16)
-        out_ref[...] = dot_nn(onehot_cols(tok), total).astype(bf16)
-
-
-def input_grad_call(tg, weight, xp, branch, gain, m):
-    reps, _, cols, tok = tg.shape
-    width = reps * cols
-    return pl.pallas_call(
-        input_grad_body,
-        grid=(3,),
-        in_specs=[
-            pl.BlockSpec((reps, 1, cols, tok), lambda c: (0, c, 0, 0)),
-            pl.BlockSpec((width, width), lambda c: (0, c)),
-            pl.BlockSpec((tok, width), lambda c: (0, 0)),
-            pl.BlockSpec((tok, width), lambda c: (0, 0)),
-            pl.BlockSpec((1, width), lambda c: (0, 0)),
-        ],
-        out_specs=[
-            pl.BlockSpec((tok, width), lambda c: (0, 0)),
-            pl.BlockSpec((2, width), lambda c: (0, 0)),
-        ],
-        out_shape=[
-            jax.ShapeDtypeStruct((tok, width), bf16),
-            jax.ShapeDtypeStruct((2, width), f32),
-        ],
-        scratch_shapes=[pltpu.VMEM((width, tok), f32)],
-        compiler_params=pltpu.CompilerParams(vmem_limit_bytes=VMEM),
-        cost_estimate=pl.CostEstimate(
-            flops=6 * tok * width * width, bytes_accessed=10_000_000, transcendentals=0
-        ),
-        name=f"input_grad_{m}",
-    )(tg, weight, xp, branch, gain)
 
 
 def rep_peer(k):
@@ -1016,20 +553,34 @@
             piece = r[m, b, :, head_rows(2), half(2)]
             stage1[m, 1, :, :, bl] = piece
             p1[m, side, 1, :, :, bl] = piece
-        p1_copy(m, 1, side).start()
+
+        @pl.when(side != taker())
+        def _():
+            p1_copy(m, 1, side).start()
+
         for g in range(4):
-            j = min(g, 2)
+            j = clamp_slot(slot_of(g))
             for b in range(reps):
                 stage2[m, g, :, :, b * 128 : (b + 1) * 128] = r[m, b, :, head_rows(j), quarter(j)]
         p2[m, place] = stage2[m, place]
         for k in range(1, 4):
-            p2_copy(m, k, place).start()
+
+            @pl.when(slot_of(place + k) < 3)
+            def _():
+                p2_copy(m, k, place).start()
 
     def mix_all(m):
-        for s in range(2):
-            b1_copy(m, s, 1 - side).wait_recv()
+        b1_copy(m, 0, 1 - side).wait_recv()
+
+        @pl.when(side != taker())
+        def _():
+            b1_copy(m, 1, 1 - side).wait_recv()
+
         for k in range(1, 4):
-            b2_copy(m, k, (place + 4 - k) % 4).wait_recv()
+
+            @pl.when(slot_of(place + 4 - k) < 3)
+            def _():
+                b2_copy(m, k, (place + 4 - k) % 4).wait_recv()
 
         def stat(tile):
             t = tile[HD:, :].astype(f32)
@@ -1037,14 +588,14 @@
 
         mix_ref[m] = jnp.zeros(mix_ref.shape[1:], f32)
         for j in range(3):
-            e, s = PLACE1[j]
+            e, s = place1(j)
             for b in range(reps):
                 for a in range(4):
                     la = slice(a * 128, (a + 1) * 128)
                     lb = b * 256 + (a % 2) * 128
                     t0 = o0[m, j, b, :, la]
                     t1 = b1[m, e, s, :, lb : lb + 128]
-                    t2 = b2[m, j, :, b * 128 : (b + 1) * 128]
+                    t2 = b2[m, owner_of(j), :, b * 128 : (b + 1) * 128]
                     l0 = stat(t0)
                     l1 = jnp.where((3 * me + j) % 2 == a // 2, stat(t1), NEG)
                     l2 = jnp.where(quarter_at(j) == a, stat(t2), NEG)
@@ -1099,9 +650,10 @@
                 att_copy(k, me).start()
             got_ref[me] = att_ref[0, me]
 
-        def paired(s, inner):
+        wide = span // 2
+
+        def paired(s):
             p1_copy(m, s, 1 - side).wait_recv()
-            wide = span // 2
 
             def block(c, start, size):
                 at = start % wide
@@ -1115,11 +667,15 @@
             attend(block, docs_of(m, 1), put, ks, qs, 1, span, wide)
             b1[m, side, s] = o1[m, s, side]
             b1_copy(m, s, side).start()
+
+        def each_pair(s, inner):
+            @pl.when((s == 0) | (side == taker()))
+            def _():
+                paired(s)
+
             return inner
 
-        lax.fori_loop(0, 2, paired, 0)
-        for k in range(1, 4):
-            p2_copy(m, k, (place + 4 - k) % 4).wait_recv()
+        lax.fori_loop(0, 2, each_pair, 0)
 
         def block(c, start, size):
             at = start % tok
@@ -1130,10 +686,15 @@
             o2[m, start // tok, :HD, at : at + size] = out
             o2[m, start // tok, HD:, at : at + size] = stats
 
-        attend(block, docs_of(m, 2), put, ks, qs, 2, span, tok)
-        b2[m, place] = o2[m, place]
-        for k in range(1, 4):
-            b2_copy(m, k, place).start()
+        @pl.when(slot_of(place) < 3)
+        def _():
+            for k in range(1, 4):
+                p2_copy(m, k, (place + 4 - k) % 4).wait_recv()
+            attend(block, docs_of(m, 2), put, ks, qs, 2, span, tok)
+            b2[m, place] = o2[m, place]
+            for k in range(1, 4):
+                b2_copy(m, k, place).start()
+
         for c in out_copies(m):
             c.start()
         return carry
@@ -1150,11 +711,26 @@
         for k in range(1, 4):
             for j in range(3):
                 qkv_copy(m, j, k, me).wait_send()
-            p2_copy(m, k, place).wait_send()
-            b2_copy(m, k, place).wait_send()
-        for s in range(2):
-            p1_copy(m, s, side).wait_send()
-            b1_copy(m, s, side).wait_send()
+
+            @pl.when(slot_of(place + k) < 3)
+            def _():
+                p2_copy(m, k, place).wait_send()
+
+            @pl.when(slot_of(place) < 3)
+            def _():
+                b2_copy(m, k, place).wait_send()
+
+        p1_copy(m, 0, side).wait_send()
+        b1_copy(m, 0, side).wait_send()
+
+        @pl.when(side != taker())
+        def _():
+            p1_copy(m, 1, side).wait_send()
+
+        @pl.when(side == taker())
+        def _():
+            b1_copy(m, 1, side).wait_send()
+
         return carry
 
     lax.fori_loop(0, micros, finish, 0)
@@ -1275,7 +851,7 @@
     def __init__(self, source, steps, buffers, gathered, out, sems):
         self.source, self.steps, self.buffers = source, steps, buffers
         self.gathered, self.out, self.sems = gathered, out, sems
-        self.names = ["high", "x", "y"]
+        self.names = ["high", "z", "x", "y"]
         self.at = 0
         self.pending = None
 
@@ -1358,9 +934,7 @@
     def drain(self):
         while self.pending is not None:
             self.pump()
-        for y in range(2):
-            for c in range(2):
-                self.out[y, c] = self.gathered[y, c].astype(f32)
+        self.out[...] = self.gathered[...]
 
 
 def reduce_steps(order, seq_bits):
@@ -1370,25 +944,33 @@
             steps.append(("y", "rep", 1))
         elif name == "x":
             steps.append(("x", "seq", 0))
+        elif name == "z":
+            steps.append(("z", "seq", 1))
         else:
-            steps += [("high", "seq", b) for b in range(seq_bits - 1, 0, -1)]
+            steps += [("high", "seq", b) for b in range(seq_bits - 1, 1, -1)]
     return steps
 
 
 def reduce_buffers(shape, steps):
-    high, rows, cols = shape[0], shape[3], shape[4]
-    rest = ["x", "y"]
+    high, rows, cols = shape[0], shape[4], shape[5]
+    left = 3
     out = []
     for name, _, _ in steps:
         if name == "high":
             high //= 2
         else:
-            rest.remove(name)
-        out.append((high,) + (2,) * len(rest) + (rows, cols))
+            left -= 1
+        out.append((high,) + (2,) * left + (rows, cols))
     return out
 
 
-REDUCE_ORDERS = ("yxz", "xyz", "yxz")
+def grad_parts(width, hidden):
+    return (
+        (0, slice(0, width), "yzhx"),
+        (1, slice(0, hidden // 2), "zhyx"),
+        (1, slice(hidden // 2, hidden), "xyzh"),
+        (2, slice(0, width), "xyzh"),
+    )
 
 
 def backward_body(
@@ -1414,12 +996,13 @@
     load_sems, g1_sems, g2_sems, d1_sems, d2_sems, tg_sems, tg1_sems, own_sems = scratch[20:28]
     rest = list(scratch[28:])
     halvings = []
-    for order, source, out in zip(
-        REDUCE_ORDERS, (w0_ref, w1_ref, w2_ref), (t0_ref, t1_ref, t2_ref)
-    ):
+    sources, outs = (w0_ref, w1_ref, w2_ref), (t0_ref, t1_ref, t2_ref)
+    for n, lanes, order in grad_parts(w0_ref.shape[-1], w1_ref.shape[-1]):
         steps = reduce_steps(order, seq_bits)
         buffers = [rest.pop(0) for _ in steps]
         gathered, sems = rest.pop(0), rest.pop(0)
+        source = sources[n].at[:, :, :, :, :, lanes]
+        out = outs[n].at[:, :, :, lanes]
         halvings.append(Halving(source, steps, buffers, gathered, out, sems))
     reps, cols, tok = da0_ref.shape
     micros = att_ref.shape[0]
@@ -1545,13 +1128,20 @@
             g1s[m, 1, :, bl] = piece
             g1[m, side, 1, :, bl] = piece
             for g in range(4):
-                j = min(g, 2)
+                j = clamp_slot(slot_of(g))
                 g2s[m, g, :, b * 128 : (b + 1) * 128] = g0[m, j, b, :, quarter(j)]
         g2[m, place] = g2s[m, place]
-        for s in range(2):
-            g1_copy(m, s, side).start()
+        g1_copy(m, 0, side).start()
+
+        @pl.when(side != taker())
+        def _():
+            g1_copy(m, 1, side).start()
+
         for k in range(1, 4):
-            g2_copy(m, k, place).start()
+
+            @pl.when(slot_of(place + k) < 3)
+            def _():
+                g2_copy(m, k, place).start()
 
     def docs(m, pattern):
         return doc_rows(len_ref, m, segment_start(pattern, span), 2**pattern, span)
@@ -1572,21 +1162,28 @@
         attend_back(block, gblock, docs(m, 0), put, scr, 0, span, tok)
 
     def add_others(m, j):
-        e, s = PLACE1[j]
+        e, s = place1(j)
         for b in range(reps):
             bl = slice(b * 256, (b + 1) * 256)
             t = sums[m, b, :, j * HD : (j + 1) * HD, half(j)].astype(f32)
             t = t + e1[m, e, s, :, :, bl].astype(f32)
             sums[m, b, :, j * HD : (j + 1) * HD, half(j)] = t.astype(bf16)
             t = sums[m, b, :, j * HD : (j + 1) * HD, quarter(j)].astype(f32)
-            t = t + e2[m, j, :, :, b * 128 : (b + 1) * 128].astype(f32)
+            t = t + e2[m, owner_of(j), :, :, b * 128 : (b + 1) * 128].astype(f32)
             sums[m, b, :, j * HD : (j + 1) * HD, quarter(j)] = t.astype(bf16)
 
     def wait_others(m):
-        for s in range(2):
-            d1_copy(m, s, 1 - side).wait_recv()
+        d1_copy(m, 0, 1 - side).wait_recv()
+
+        @pl.when(side != taker())
+        def _():
+            d1_copy(m, 1, 1 - side).wait_recv()
+
         for k in range(1, 4):
-            d2_copy(m, k, (place + 4 - k) % 4).wait_recv()
+
+            @pl.when(slot_of(place + 4 - k) < 3)
+            def _():
+                d2_copy(m, k, (place + 4 - k) % 4).wait_recv()
 
     load_r(0).wait()
 
@@ -1598,7 +1195,7 @@
     load_r(1).start()
 
     def others(m):
-        def paired(s, inner):
+        def paired(s):
             g1_copy(m, s, 1 - side).wait_recv()
 
             def block(c, start, size):
@@ -1616,10 +1213,16 @@
             attend_back(block, gblock, docs(m, 1), put, scr, 1, span, wide)
             e1[m, side, s] = d1[m, s, side]
             d1_copy(m, s, side).start()
+
+        def each_pair(s, inner):
+            @pl.when((s == 0) | (side == taker()))
+            def _():
+                paired(s)
+
             return inner
 
         load_1(m).wait()
-        lax.fori_loop(0, 2, paired, 0)
+        lax.fori_loop(0, 2, each_pair, 0)
         if m + 1 < micros:
             load_1(m + 1).start()
         pump()
@@ -1630,8 +1233,6 @@
             for k in range(1, 4):
                 tg0_copy(k, me).start()
             own_copy(0).start()
-        for k in range(1, 4):
-            g2_copy(m, k, (place + 4 - k) % 4).wait_recv()
         load_2(m).wait()
 
         def block(c, start, size):
@@ -1646,10 +1247,15 @@
             at = start % tok
             d2[m, start // tok, c, :, at : at + size] = value
 
-        attend_back(block, gblock, docs(m, 2), put, scr, 2, span, tok)
-        e2[m, place] = d2[m, place]
-        for k in range(1, 4):
-            d2_copy(m, k, place).start()
+        @pl.when(slot_of(place) < 3)
+        def _():
+            for k in range(1, 4):
+                g2_copy(m, k, (place + 4 - k) % 4).wait_recv()
+            attend_back(block, gblock, docs(m, 2), put, scr, 2, span, tok)
+            e2[m, place] = d2[m, place]
+            for k in range(1, 4):
+                d2_copy(m, k, place).start()
+
         if m + 1 < micros:
             load_2(m + 1).start()
 
@@ -1669,12 +1275,27 @@
         h.drain()
     for m in range(micros):
         own_copy(m).wait()
-        for s in range(2):
-            g1_copy(m, s, side).wait_send()
-            d1_copy(m, s, side).wait_send()
+        g1_copy(m, 0, side).wait_send()
+        d1_copy(m, 0, side).wait_send()
+
+        @pl.when(side != taker())
+        def _():
+            g1_copy(m, 1, side).wait_send()
+
+        @pl.when(side == taker())
+        def _():
+            d1_copy(m, 1, side).wait_send()
+
         for k in range(1, 4):
-            g2_copy(m, k, place).wait_send()
-            d2_copy(m, k, place).wait_send()
+
+            @pl.when(slot_of(place + k) < 3)
+            def _():
+                g2_copy(m, k, place).wait_send()
+
+            @pl.when(slot_of(place) < 3)
+            def _():
+                d2_copy(m, k, place).wait_send()
+
     for k in range(1, 4):
         source = (me + reps - k) % reps
         tg0_copy(k, source).wait_recv()
@@ -1694,13 +1315,14 @@
 
     dma = pltpu.SemaphoreType.DMA
     halving = []
-    for order, g in zip(REDUCE_ORDERS, grads):
+    for n, lanes, order in grad_parts(grads[0].shape[-1], grads[1].shape[-1]):
         steps = reduce_steps(order, seq_bits)
-        halving += [vm(*b) for b in reduce_buffers(g.shape, steps)]
-        halving += [vm(2, 2, *g.shape[3:]), dma((2, len(steps) + 2))]
+        shape = grads[n].shape[:5] + (lanes.stop - lanes.start,)
+        halving += [vm(*b) for b in reduce_buffers(shape, steps)]
+        halving += [vm(2, 2, *shape[4:]), dma((2, len(steps) + 2))]
     tall, flat = vm(span, 128), vm(128, span)
     outs = [((micros, reps, 3, cols, tok), bf16, any_spec)]
-    outs += [((2, 2) + g.shape[3:], f32, vmem_spec()) for g in grads]
+    outs += [((2, 2) + g.shape[4:], bf16, vmem_spec()) for g in grads]
     return pl.pallas_call(
         functools.partial(backward_body, seq_bits=seq_bits),
         in_specs=[any_spec] * 3 + [vmem_spec()] * 4 + [smem_spec()] + [vmem_spec()] * 3,
@@ -1870,44 +1492,250 @@
     )(*[a for g in groups for a in g])
 
 
-def swap(block, axis, bit):
-    count = lax.axis_size(axis)
-    return lax.ppermute(block, axis, [(n, n ^ (1 << bit)) for n in range(count)])
+TAIL_ORDERS = ("yxzh", "xzhy", "zhyx")
+
+
+def tail_body(
+    tg_hbm,
+    w_hbm,
+    branch0_hbm,
+    branch1_hbm,
+    xp_ref,
+    nt_ref,
+    gain_ref,
+    ng0_ref,
+    ng1_ref,
+    nh0_ref,
+    nh1_ref,
+    out_ref,
+    total_ref,
+    norm_ref,
+    hidden_ref,
+    *scratch,
+    seq_bits,
+):
+    tg, w, branch, acc, keep, send, get, vec, vec_get, load_sems, core_sems, vec_sems = scratch[:12]
+    rest = list(scratch[12:])
+    micros, tok, width = xp_ref.shape
+    reps = tg.shape[2]
+    parts, rows = keep.shape[1], keep.shape[2]
+
+    barrier = pltpu.get_barrier_semaphore()
+    bits = [("rep", 0), ("rep", 1)] + [("seq", b) for b in range(seq_bits)]
+    for axis, bit in bits:
+        pl.semaphore_signal(
+            barrier,
+            inc=1,
+            device_id={axis: bit_peer(axis, bit)},
+            device_id_type=pl.DeviceIdType.MESH,
+        )
+    loads = [
+        pltpu.make_async_copy(tg_hbm.at[m, :, c], tg.at[m, c], load_sems.at[m * 3 + c])
+        for c in range(3)
+        for m in range(micros)
+    ]
+    loads += [pltpu.make_async_copy(w_hbm, w, load_sems.at[6])]
+    loads += [
+        pltpu.make_async_copy(b, branch.at[m], load_sems.at[7 + m])
+        for m, b in enumerate((branch0_hbm, branch1_hbm))
+    ]
+    for c in loads:
+        c.start()
+    pl.semaphore_wait(barrier, len(bits))
+
+    def core_copy(c):
+        return remote(
+            send.at[c],
+            get.at[c],
+            core_sems.at[0, c],
+            core_sems.at[1, c],
+            "rep",
+            bit_peer("rep", 0),
+        )
+
+    def piece(m, c):
+        return jnp.concatenate([tg[m, c, r] for r in range(reps)], 0)
+
+    for c in range(3):
+        total = None
+        for m in range(micros):
+            loads[c * micros + m].wait()
+            part = dot_nt(nt_ref[m], piece(m, c))
+            total = part if total is None else total + part
+        mine, other = split_rows(total, parts, rows)
+        for k in range(parts):
+            keep[c, k] = mine[k].astype(bf16)
+            send[c, k] = other[k].astype(bf16)
+        core_copy(c).start()
+
+    halvings = []
+    for c, order in enumerate(TAIL_ORDERS):
+        steps = reduce_steps(order, seq_bits)
+        summed = rest.pop(0)
+        buffers = [rest.pop(0) for _ in steps]
+        gathered, sems = rest.pop(0), rest.pop(0)
+        out = total_ref.at[:, :, :, c * width : (c + 1) * width]
+        halvings.append(Halving(summed, steps, buffers, gathered, out, sems))
+
+    def core_sum(c):
+        core_copy(c).wait()
+        summed = halvings[c].source
+
+        def add(z, carry):
+            for n in range(8):
+                k = z * 8 + n
+                total = keep[c, k].astype(f32) + get[c, k].astype(f32)
+                summed[z, n // 4, n // 2 % 2, n % 2] = total.astype(bf16)
+            return carry
+
+        lax.fori_loop(0, parts // 8, add, 0)
+        halvings[c].start()
+
+    loads[6].wait()
+
+    def grad_part(m, c):
+        part = dot_nn(w[:, c * width : (c + 1) * width], piece(m, c))
+        if c == 0:
+            acc[...] = part
+        else:
+            acc[...] += part
+
+    def grad_end(m):
+        xhat, rstd = normalize(xp_ref[m].astype(f32))
+        dx, gain_i, bias_i = norm_back(acc[...].T, gain_ref[...], xhat, rstd)
+        loads[7 + m].wait()
+        total = (branch[m] + dx).astype(bf16)
+        out_ref[m] = dot_nn(onehot_cols(tok), total).astype(bf16)
+        return gain_i, bias_i
+
+    core_sum(0)
+    grad_part(0, 0)
+    core_sum(1)
+    grad_part(0, 1)
+    core_sum(2)
+    grad_part(0, 2)
+    gain0, bias0 = grad_end(0)
+
+    def pump():
+        for h in halvings:
+            h.pump()
+
+    pump()
+    grad_part(1, 0)
+    grad_part(1, 1)
+    pump()
+    grad_part(1, 2)
+    gain1, bias1 = grad_end(1)
+    vec[0] = jnp.zeros(vec.shape[1:], f32)
+    vec[0, 0:1] = gain0 + gain1
+    vec[0, 1:2] = bias0 + bias1
+    vec[0, 2:6] = ng0_ref[...] + ng1_ref[...]
+    fold = nh0_ref.shape[1] // width
+    for n in range(2):
+        for k in range(fold):
+            cl = slice(k * width, (k + 1) * width)
+            row = 8 + n * fold + k
+            vec[0, row : row + 1] = nh0_ref[n : n + 1, cl] + nh1_ref[n : n + 1, cl]
+    for n, (axis, bit) in enumerate(bits):
+        copy = remote(
+            vec.at[n],
+            vec_get.at[n],
+            vec_sems.at[0, n],
+            vec_sems.at[1, n],
+            axis,
+            bit_peer(axis, bit),
+        )
+        copy.start()
+        pump()
+        copy.wait()
+        vec[n + 1] = vec[n] + vec_get[n]
+    s = lax.axis_index("seq")
+    last = len(bits)
+    seqs = 1 << seq_bits
+    cols = vec[last].T
+    acc[:, : cols.shape[1]] = cols
+
+
+    def rows_at(block, size):
+        if size % 8 == 0:
+            return acc[pl.ds(pl.multiple_of(block * size, 8), size), :16]
+        out = cols[:size]
+        for n in range(1, width // size):
+            out = jnp.where(block == n, cols[n * size : (n + 1) * size], out)
+        return out
+
+    norm_ref[...] = rows_at(s, norm_ref.shape[0])[:, :6]
+    own = hidden_ref.shape[0]
+    per = width // own
+    picked = rows_at(s % per, own)
+    out = jnp.zeros((own, 2), f32)
+    for k in range(fold):
+        pair = jnp.concatenate(
+            [picked[:, 8 + k : 9 + k], picked[:, 8 + fold + k : 9 + fold + k]], 1
+        )
+        out = jnp.where(s // per == k, pair, out)
+    hidden_ref[...] = out
+    for h in halvings:
+        h.drain()
+
+
+def tail_call(tg, weight, branch, xp, nt, gain, ng, nh, seq_bits):
+    micros, tok, width = xp.shape
+    reps, _, cols = tg.shape[1:4]
+    hidden = nh[0].shape[1]
+    seqs = 1 << seq_bits
+    rows = width // seqs // reps
+    parts = seqs * reps // 2
+    any_spec = pl.BlockSpec(memory_space=pl.ANY)
+
+    def vm(*shape):
+        return pltpu.VMEM(shape, bf16)
+
+    dma = pltpu.SemaphoreType.DMA
+    shape = (seqs // 4, 2, 2, reps // 2, rows, width)
+    halving = []
+    for order in TAIL_ORDERS:
+        steps = reduce_steps(order, seq_bits)
+        halving += [vm(*shape)] + [vm(*b) for b in reduce_buffers(shape, steps)]
+        halving += [vm(2, 2, rows, width), dma((2, len(steps) + 2))]
+    outs = [
+        ((micros, tok, width), bf16),
+        ((2, 2, rows, 3 * width), bf16),
+        ((width // seqs, 6), f32),
+        ((hidden // seqs, 2), f32),
+    ]
+    return pl.pallas_call(
+        functools.partial(tail_body, seq_bits=seq_bits),
+        in_specs=[any_spec] * 4 + [vmem_spec()] * 7,
+        out_specs=[vmem_spec()] * 4,
+        out_shape=[jax.ShapeDtypeStruct(s, d) for s, d in outs],
+        scratch_shapes=[
+            vm(micros, 3, reps, cols, tok),
+            vm(width, 3 * width),
+            pltpu.VMEM((micros, tok, width), f32),
+            pltpu.VMEM((width, tok), f32),
+            vm(3, parts, rows, width),
+            vm(3, parts, rows, width),
+            vm(3, parts, rows, width),
+            pltpu.VMEM((seq_bits + 3, 16, width), f32),
+            pltpu.VMEM((seq_bits + 2, 16, width), f32),
+            dma((9,)),
+            dma((2, 3)),
+            dma((2, seq_bits + 2)),
+            *halving,
+        ],
+        compiler_params=pltpu.CompilerParams(
+            vmem_limit_bytes=VMEM, collective_id=4, has_side_effects=True
+        ),
+        cost_estimate=pl.CostEstimate(
+            flops=24 * tok * width * width, bytes_accessed=20_000_000, transcendentals=0
+        ),
+        name="tail",
+    )(tg, weight, *branch, xp, nt, gain, *ng, *nh)
 
 
 def bits_of(count):
     return count.bit_length() - 1
-
-
-def reduce_rows(x, order):
-    seqs, reps = lax.axis_size("seq"), lax.axis_size("rep")
-    rows, cols = x.shape
-    sb, rb = bits_of(seqs), bits_of(reps)
-    y = x.reshape((2,) * (sb + rb) + (rows // (seqs * reps), cols))
-    names = [("seq", b) for b in reversed(range(sb))] + [("rep", b) for b in reversed(range(rb))]
-    for step in order(sb, rb):
-        at = names.index(step)
-        axis, bit = step
-        mine = (lax.axis_index(axis) >> bit) & 1
-        send = lax.dynamic_index_in_dim(y, 1 - mine, at, keepdims=False)
-        keep = lax.dynamic_index_in_dim(y, mine, at, keepdims=False)
-        got = swap(send.astype(x.dtype), axis, bit)
-        y = (keep.astype(f32) + got.astype(f32)).astype(x.dtype)
-        names.pop(at)
-    for bit in range(rb):
-        other = swap(y, "rep", bit)
-        mine = (lax.axis_index("rep") >> bit) & 1
-        y = jnp.where(mine == 0, jnp.stack([y, other]), jnp.stack([other, y]))
-        y = y.reshape((-1,) + y.shape[2:])
-    return y.astype(f32)
-
-
-def order_yxz(sb, rb):
-    return [("rep", b) for b in range(rb)] + [("seq", b) for b in range(sb)]
-
-
-def order_xzy(sb, rb):
-    return [("rep", 0)] + [("seq", b) for b in range(sb)] + [("rep", b) for b in range(1, rb)]
 
 
 def on_device(
@@ -1952,8 +1780,6 @@
     xp, nt, got_qkv, got_pair, got_four, own_att, got_att, totals = forward_call(
         layer_in, qkv_weight, row(input_gain), row(input_bias), seq_lengths, reps
     )
-    residual = [xp[m] for m in micros]
-    normed = [nt[m] for m in micros]
     attended = [got_att, to_reps(own_att[1])]
 
     outputs, branch_grads, head_grads, groups, norm_terms, hidden_terms = [], [], [], [], [], []
@@ -1963,7 +1789,7 @@
     )
     for m in micros:
         out, branch, da, mixl, low, hid, dup, brl, cotp, ng, nh = ffn_call(
-            attended[m], residual[m], output_grad, weights, gains, m
+            attended[m], xp, output_grad, weights, gains, m
         )
         outputs.append(out)
         branch_grads.append(branch)
@@ -1973,32 +1799,30 @@
         hidden_terms.append(nh)
     seq_bits = bits_of(seqs)
     grads = [
-        g.reshape((seqs // 2, 2, reps // 2) + g.shape[1:])
+        g.reshape((seqs // 4, 2, 2, reps // 2) + g.shape[1:])
         for g in weight_grads(groups, tok, width, up_weight.shape[1], seqs, reps)
     ]
     token_grad, down_total, up_total, proj_total = backward_call(
         (got_qkv, got_pair, got_four), head_grads, own_att, totals, seq_lengths, grads, seq_bits
     )
     down_total, up_total, proj_total = (
-        t.reshape(-1, t.shape[-1]) for t in (down_total, up_total, proj_total)
+        t.reshape(-1, t.shape[-1]).astype(f32) for t in (down_total, up_total, proj_total)
     )
-    token_grads = [token_grad[m] for m in micros]
-    input_grads, input_terms = [], []
-    grad_qkv = qkv_grad_call(list(zip(normed, token_grads)), tok, width, reps)
-    for m in micros:
-        grad, terms = input_grad_call(
-            token_grads[m], qkv_weight, residual[m], branch_grads[m], row(input_gain), m
-        )
-        input_grads.append(grad)
-        input_terms.append(terms)
-
-    qkv_total = reduce_rows(grad_qkv, order_yxz)
-    model = jnp.concatenate([sum(input_terms), sum(norm_terms)], 0)
-    norm_total = reduce_rows(model.T, order_yxz)
-    hidden_total = reduce_rows(sum(hidden_terms).T, order_yxz)
+    input_grad, qkv_total, norm_total, hidden_total = tail_call(
+        token_grad,
+        qkv_weight,
+        branch_grads,
+        xp,
+        nt,
+        row(input_gain),
+        norm_terms,
+        hidden_terms,
+        seq_bits,
+    )
+    qkv_total = qkv_total.reshape(-1, qkv_total.shape[-1]).astype(f32)
     return (
         jnp.stack(outputs),
-        jnp.stack(input_grads),
+        input_grad,
         qkv_total,
         proj_total,
         up_total,

time: 486 us -> 394 us (0.81)
  starting transfers between devices: 44.4 us -> 12.2 us
  waiting for transfers between devices: 31.4 us -> 0.01 us
  local copies, waits for them, and re-layouts: 27.1 us -> 12.1 us
  Pallas kernels: 364 us -> 358 us
  other arithmetic: 13 us -> 7.49 us
    ppermute x21 -> x0, starting transfers between devices: 33.3 us -> none  [swap(): return lax.ppermute(block, axis, [(n, n ^ 1 << bit) for n in range(count)])]
    ppermute x21 -> x0, waiting for transfers between devices: 31.4 us -> none  [swap(): return lax.ppermute(block, axis, [(n, n ^ 1 << bit) for n in range(count)])]
    pallas_call x3 -> x1, Pallas kernels: 24.3 us -> 51.7 us  [tail_call(): pl.pallas_call(functools.partial(tail_body, seq_bits=seq_bits), in_specs=...]
    pallas_call x1, Pallas kernels: 156 us -> 133 us  [backward_call(): pl.pallas_call(functools.partial(backward_body, seq_bits=seq_bits), in_sp...]
    pallas_call x1, Pallas kernels: 102 us -> 89.7 us  [forward_call(): pl.pallas_call(forward_body, in_specs=[vmem_spec()] * 4 + [smem_spec()],...]
    squeeze x12 -> x0, local copies, waits for them, and re-layouts: 9.31 us -> none  [the longest x1 5.04 us: on_device(): token_grads = [token_grad[m] for m in micros]]
  transfers between devices with their start and end apart: 24 -> 3, of which waited for: 9 -> 0; matrix products, arithmetic and copies ran while one was open for 6% -> 1% of each run, Pallas kernels for 55% -> 21%
where the time goes in v4:
time: 394 us; the launch traced here: 391 us
  Pallas kernels  358 us (91%)
  starting transfers between devices  12.2 us (3%)
  local copies, waits for them, and re-layouts  12.1 us (3%)
  other arithmetic  7.49 us (2%)
    pallas_call x1, Pallas kernels, backward_call(): pl.pallas_call(functools.partial(backward_body, seq_bits=seq_bits), in_sp...  133 us
    pallas_call x1, Pallas kernels, forward_call(): pl.pallas_call(forward_body, in_specs=[vmem_spec()] * 4 + [smem_spec()],...  89.7 us
    pallas_call x2, Pallas kernels, ffn_call(): pl.pallas_call(ffn_body, grid=(1,), in_specs=[pl.BlockSpec((reps, cols, t...  60.5 us
    pallas_call x1, Pallas kernels, tail_call(): pl.pallas_call(functools.partial(tail_body, seq_bits=seq_bits), in_specs=...  51.7 us
    pallas_call x1, Pallas kernels, weight_grads(): pl.pallas_call(functools.partial(weight_grad_body, chunks=chunks), grid=(...  23.3 us
    all_to_all x3, starting transfers between devices, to_reps(): return lax.all_to_all(x, 'rep', 0, 0, tiled=True)  12.2 us
  transfers between devices with their start and end apart: 3, of which 0 were waited for; matrix products, arithmetic and copies ran while one was open for 1% of the time, Pallas kernels for 21%

profile of v4, /device:TPU:0, one launch (start us, length us, event | category | flops | bytes accessed | tf_op | source)
XLA Modules:
  0.0 390.7 jit_solution(17545329101590343329)
XLA Ops:
  0.6 1.3 reshape.62.gain_ref
  1.9 1.3 reshape.63.bias_ref
  3.2 89.7 %forward.1 = (bf16[2,512,768]{2,1,0:T(8,128)(2,1)}, bf16[2,768,512]{2,1,0:T(8,128)(2,1)}, bf16[2,4,3,192,512]{4,3,2,1,0:T(8,128)(2,1)}, bf16[2,2,2,3,64,1024]{5,...) custom-call(bf16[2,512,768]{2,1,0:T(8,128)(2,1)} %x_ref.1, ...), custom_call_target="tpu_custom_call" | custom-call | flops 60000002048 | bytes 30000000 | tf_op jit(solution)/shard_map/forward/pallas_call | solution.py:758
  92.9 2.1 slice_bitcast_fusion
  95.0 4.6 %all-to-all-start = ((bf16[4,192,512]{2,1,0:T(8,128)(2,1)}), bf16[4,192,512]{2,1,0:T(8,128)(2,1)S(1)}, u32[]{:S(2)}, u32[]{:S(2)}) async-start(bf16[4,192,512]{2,1,0:T(8,128)(2,1)} %slice_bitcast_fusion), calls=%async_computation | async-start | bytes 1572864 | tf_op jit(solution)/shard_map/all_to_all | solution.py:1768
  99.6 0.6 reshape.64.mg_ref
  100.8 0.6 reshape.66.bg_ref
  101.4 0.6 reshape.67.bb_ref
  101.9 30.2 %ffn_0.1 = (bf16[512,768]{1,0:T(8,128)(2,1)}, f32[512,768]{1,0:T(8,128)}, bf16[4,192,512]{2,1,0:T(8,128)(2,1)}, bf16[512,768]{1,0:T(8,128)(2,1)}, bf16[512,768]{...) custom-call(bf16[4,192,512]{2,1,0:T(8,128)(2,1)} %get-tuple-element., ...), custom_call_target="tpu_custom_call" | custom-call | flops 10871635968 | bytes 25000000 | tf_op jit(solution)/shard_map/ffn_0/pallas_call | solution.py:284
  132.2 3.9 %all-to-all-start.1 = ((bf16[4,192,512]{2,1,0:T(8,128)(2,1)}), bf16[4,192,512]{2,1,0:T(8,128)(2,1)S(1)}, u32[]{:S(2)}, u32[]{:S(2)}) async-start(bf16[4,192,512]{2,1,0:T(8,128)(2,1)} %get-tuple-element.57), calls=%async_computation.1 | async-start | bytes 1572864 | tf_op jit(solution)/shard_map/all_to_all | solution.py:1768
  136.1 30.3 %ffn_1.1 = (bf16[512,768]{1,0:T(8,128)(2,1)}, f32[512,768]{1,0:T(8,128)}, bf16[4,192,512]{2,1,0:T(8,128)(2,1)}, bf16[512,768]{1,0:T(8,128)(2,1)}, bf16[512,768]{...) custom-call(bf16[4,192,512]{2,1,0:T(8,128)(2,1)} %copy-done.2, ...), custom_call_target="tpu_custom_call" | custom-call | flops 10871635968 | bytes 25000000 | tf_op jit(solution)/shard_map/ffn_1/pallas_call | solution.py:284
  166.4 2.4 pad_maximum_fusion
  168.9 3.7 all-to-all-start.2
  172.6 23.3 %weight_grads.1 = (bf16[16,96,768]{2,1,0:T(8,128)(2,1)}, bf16[16,24,3072]{2,1,0:T(8,128)(2,1)}, bf16[16,24,768]{2,1,0:T(8,128)(2,1)}) custom-call(bf16[512,768]{1,0:T(8,128)(2,1)} %get-tuple-element.60.refs_0_, bf16[512,3072]{1,0:T(8,128)(2,1)} %get-tuple-element.61.refs_1_, bf16[512,3072]{1,0:T(8,128)(2,1)} %get-tuple-element.62.refs_2_, ...), custom_call_target="tpu_custom_call" | custom-call | flops 10871635968 | bytes 30000000 | tf_op jit(solution)/shard_map/weight_grads/pallas_call | solution.py:1464
  195.9 0.9 copy-done.3
  196.8 132.6 %backward.1 = (bf16[2,4,3,192,512]{4,3,2,1,0:T(8,128)(2,1)}, bf16[2,2,96,768]{3,2,1,0:T(8,128)(2,1)}, bf16[2,2,24,3072]{3,2,1,0:T(8,128)(2,1)}, bf16[2,2,24,768]{3,2,1,0:T(8,128)(2,1)}) custom-call(bf16[2,4,3,192,512]{4,3,2,1,0:T(8,128)(2,1)} %get-tuple-element.54.r_hbm, bf16[2,2,2,3,64,1024]{5,4,3,2,1,0:T(8,128)(2,1)} %get-tuple-element.55.p1_hbm, ...), custom_call_target="tpu_custom_call" | custom-call | flops 99999997952 | bytes 40000000 | tf_op jit(solution)/shard_map/backward/pallas_call | solution.py:1326
  329.4 51.7 %tail.1 = (bf16[2,512,768]{2,1,0:T(8,128)(2,1)}, bf16[2,2,24,2304]{3,2,1,0:T(8,128)(2,1)}, f32[96,6]{1,0:T(8,128)}, f32[384,2]{1,0:T(8,128)}) custom-call(bf16[2,4,3,192,512]{4,3,2,1,0:T(8,128)(2,1)} %get-tuple-element.75.tg_hbm, bf16[768,2304]{1,0:T(8,128)(2,1)} %w_hbm.1, f32[512,768]{1,0:T(8,128)} %get-tuple-element.76.branch0_hbm, ...), custom_call_target="tpu_custom_call" | custom-call | flops 7247757312 | bytes 20000000 | tf_op jit(solution)/shard_map/tail/pallas_call | solution.py:1707
  381.1 1.7 copy.24
  382.8 1.5 copy.23
  384.3 0.7 bitcast_convert_fusion.3
  385.0 2.0 bitcast_convert_fusion.2
  387.1 1.2 bitcast_convert_fusion.1
  388.2 1.1 bitcast_convert_fusion
  389.3 1.1 copy.26
  (27 shorter events, 0.6 us)
Async XLA Ops:
  92.9 6.8 %copy-start.8 = (f32[768]{0:T(1024)S(1)}, f32[768]{0:T(1024)}, u32[]{:S(2)}) copy-start(f32[768]{0:T(1024)} %param.22) | copy-start | bytes 9220
  92.9 7.3 %copy-start.9 = (f32[768]{0:T(1024)S(1)}, f32[768]{0:T(1024)}, u32[]{:S(2)}) copy-start(f32[768]{0:T(1024)} %param.23) | copy-start | bytes 9220
  92.9 7.9 %copy-start.10 = (f32[768]{0:T(1024)S(1)}, f32[768]{0:T(1024)}, u32[]{:S(2)}) copy-start(f32[768]{0:T(1024)} %param.24) | copy-start | bytes 9220
  92.9 8.5 %copy-start.11 = (f32[768]{0:T(1024)S(1)}, f32[768]{0:T(1024)}, u32[]{:S(2)}) copy-start(f32[768]{0:T(1024)} %param.25) | copy-start | bytes 9220
  95.0 37.2 %all-to-all-start = ((bf16[4,192,512]{2,1,0:T(8,128)(2,1)}), bf16[4,192,512]{2,1,0:T(8,128)(2,1)S(1)}, u32[]{:S(2)}, u32[]{:S(2)}) async-start(bf16[4,192,512]{2,1,0:T(8,128)(2,1)} %slice_bitcast_fusion), calls=%async_computation | async-start | bytes 1572864 | tf_op jit(solution)/shard_map/all_to_all | solution.py:1768
  132.2 4.0 %copy-start.2 = (bf16[4,192,512]{2,1,0:T(8,128)(2,1)}, bf16[4,192,512]{2,1,0:T(8,128)(2,1)S(1)}, u32[]{:S(2)}) copy-start(bf16[4,192,512]{2,1,0:T(8,128)(2,1)S(1)} %all-to-all-done.att_ref) | copy-start | bytes 2359300
  132.2 36.7 %all-to-all-start.1 = ((bf16[4,192,512]{2,1,0:T(8,128)(2,1)}), bf16[4,192,512]{2,1,0:T(8,128)(2,1)S(1)}, u32[]{:S(2)}, u32[]{:S(2)}) async-start(bf16[4,192,512]{2,1,0:T(8,128)(2,1)} %get-tuple-element.57), calls=%async_computation.1 | async-start | bytes 1572864 | tf_op jit(solution)/shard_map/all_to_all | solution.py:1768
  136.1 30.3 %copy-start.4 = (bf16[512,768]{1,0:T(8,128)(2,1)S(1)}, bf16[512,768]{1,0:T(8,128)(2,1)}, u32[]{:S(2)}) copy-start(bf16[512,768]{1,0:T(8,128)(2,1)} %get-tuple-element.51) | copy-start | bytes 2359300
  168.9 27.0 %copy-start.1 = (bf16[4,192,512]{2,1,0:T(8,128)(2,1)}, bf16[4,192,512]{2,1,0:T(8,128)(2,1)S(1)}, u32[]{:S(2)}) copy-start(bf16[4,192,512]{2,1,0:T(8,128)(2,1)S(1)} %all-to-all-done.1.da0_ref) | copy-start | bytes 2359300
  168.9 27.0 %all-to-all-start.2 = ((bf16[4,192,512]{2,1,0:T(8,128)(2,1)}), bf16[4,192,512]{2,1,0:T(8,128)(2,1)S(1)}, u32[]{:S(2)}, u32[]{:S(2)}) async-start(bf16[4,192,512]{2,1,0:T(8,128)(2,1)} %get-tuple-element.58), calls=%async_computation.2 | async-start | bytes 1572864 | tf_op jit(solution)/shard_map/all_to_all | solution.py:1768
  195.9 0.9 copy-start.3
  329.4 54.9 %copy-start.7 = (bf16[2,2,24,768]{3,2,1,0:T(8,128)(2,1)S(1)}, bf16[2,2,24,768]{3,2,1,0:T(8,128)(2,1)}, u32[]{:S(2)}) copy-start(bf16[2,2,24,768]{3,2,1,0:T(8,128)(2,1)} %get-tuple-element.85) | copy-start | bytes 442372
  381.1 5.9 %copy-start.6 = (bf16[2,2,24,3072]{3,2,1,0:T(8,128)(2,1)S(1)}, bf16[2,2,24,3072]{3,2,1,0:T(8,128)(2,1)}, u32[]{:S(2)}) copy-start(bf16[2,2,24,3072]{3,2,1,0:T(8,128)(2,1)} %get-tuple-element.86) | copy-start | bytes 1769476
  385.0 3.2 copy-start.5
  387.1 2.3 copy-start
